TPU v7x, 32 devices: a whole 2x2x4 slice. The times are simulated.
32 devices in a mesh: dp: 16 (over z, x, core), mp: 2 (over y).
Axes of the slice: x: 2, y: 2, z: 4, core: 2. Of those that a mesh axis runs over, the one named last changes fastest.
Arguments:
- tokens: bfloat16 [16384, 768], P('dp', 'mp'), may hold values from -6 to 6
- norm_gain: bfloat16 [768], P('mp'), may hold values from 0.5 to 1.5
- proj_gate: bfloat16 [768, 1536], P(None, 'mp'), may hold values from -0.21875 to 0.21875
- proj_inner: bfloat16 [768, 1536], P(None, 'mp'), may hold values from -0.21875 to 0.21875
- proj_state: bfloat16 [768, 256], replicated, may hold values from -0.21875 to 0.21875
- proj_step: bfloat16 [768, 2, 24], P(None, None, 'mp'), may hold values from -0.21875 to 0.21875
- conv_inner: float32 [4, 1536], P(None, 'mp'), may hold values from -3 to 3
- conv_inner_bias: float32 [1536], P('mp'), may hold values from -3 to 3
- conv_state: float32 [4, 256], replicated, may hold values from -3 to 3
- conv_state_bias: float32 [256], replicated, may hold values from -3 to 3
- step_bias: float32 [2, 24], P(None, 'mp'), may hold values from -5 to -2
- decay_log: float32 [2, 24], P(None, 'mp'), may hold values from 0 to 2.5
- skip_gain: float32 [24], P('mp'), may hold values from 0.5 to 1.5
- gate_gain: float32 [1536], P('mp'), may hold values from 0.5 to 1.5
- proj_out: bfloat16 [1536, 768], P('mp'), may hold values from -0.15625 to 0.15625
- lengths: int32 [16], P('dp'), may hold values from 257 to 1024, as said below
- cotangent: bfloat16 [16384, 768], P('dp', 'mp'), may hold values from -6 to 6
Outputs:
- block_out: bfloat16 [16384, 768], P('dp', 'mp')
- grad_tokens: float32 [16384, 768], P('dp', 'mp')
- grad_norm_gain: float32 [768], P('mp')
- grad_proj_gate: float32 [768, 1536], P(None, 'mp')
- grad_proj_inner: float32 [768, 1536], P(None, 'mp')
- grad_proj_state: float32 [768, 256], replicated
- grad_proj_step: float32 [768, 2, 24], P(None, None, 'mp')
- grad_conv_inner: float32 [4, 1536], P(None, 'mp')
- grad_conv_inner_bias: float32 [1536], P('mp')
- grad_conv_state: float32 [4, 256], replicated
- grad_conv_state_bias: float32 [256], replicated
- grad_step_bias: float32 [2, 24], P(None, 'mp')
- grad_decay_log: float32 [2, 24], P(None, 'mp')
- grad_skip_gain: float32 [24], P('mp')
- grad_gate_gain: float32 [1536], P('mp')
- grad_proj_out: float32 [1536, 768], P('mp')
Inputs may be any that keep to these rules, and one draw needn't show every extreme that they name: `lengths`: valid positions of each slot; the first slot is full, each other lies in the upper half of 1024 or of 512.
All inputs are finite; a program needn't handle non-finite values.
Results may differ from a plain program's by a relative error of at most 0.012.
Values may be sent and summed in bfloat16 or wider, within the bound.
No kernel may reach another device: no remote copies, remote signals or barrier semaphores. Data moves between devices by JAX's collectives and lax.ppermute only.
A program may use at most 192 MiB of HBM per device.

v0:
```python
from functools import partial

import jax
import jax.numpy as jnp
from jax import lax
from jax.experimental import pallas as pl
from jax.experimental.pallas import tpu as pltpu
from jax.sharding import PartitionSpec as P

EPSILON = 1e-05
CHUNK = 128
PROJECT_BLOCK, MIX_BLOCK, GATE_BLOCK, BACK_BLOCK = 256, 256, 256, 128
LANES = 128
F32 = jnp.float32
BF16 = jnp.bfloat16
HIGHEST = lax.Precision.HIGHEST
VMEM_LIMIT = 12 * 1024 * 1024
SHARDS = 16
LOG2_E = 1.4426950408889634
LATE_ROWS = 72


def mm(a, b):
    return jnp.dot(a, b, preferred_element_type=F32)


def mm_nt(a, b):
    return lax.dot_general(a, b, (((1,), (1,)), ((), ())), preferred_element_type=F32)


def mm_tn(a, b):
    return lax.dot_general(a, b, (((0,), (0,)), ((), ())), preferred_element_type=F32)


def split_two(v):
    hi = v.astype(BF16)
    return hi, (v - hi.astype(F32)).astype(BF16)


def expand(v, spread):
    hi, lo = split_two(v)
    return mm(jnp.concatenate([hi, lo], axis=1), spread)


def row_mask(block, rows, length):
    pos = block * rows + lax.broadcasted_iota(jnp.int32, (rows, 1), 0)
    return (pos < length).astype(F32)


def to_row(col_a, col_b):
    rows = col_a.shape[0]
    lane = lax.broadcasted_iota(jnp.int32, (rows, LANES), 1)
    tile = jnp.where(lane == 0, col_a, jnp.where(lane == 1, col_b, 0.0))
    return jnp.transpose(tile)[0:8, :]


def sigmoid(v):
    return 0.5 * jnp.tanh(0.5 * v) + 0.5


def natural(rank, own, oth):
    return jnp.where(
        rank == 0, jnp.concatenate([own, oth], axis=1), jnp.concatenate([oth, own], axis=1)
    )


def eight(row):
    return jnp.broadcast_to(row, (8, row.shape[1]))


def stage_kernel(w_state, w_step, *refs, count, head_dim):
    sources, outs, sems = refs[:count], refs[count:-1], refs[-1]
    spread, gather, w_state_t = outs[count:]
    copies = [
        pltpu.make_async_copy(src, dst, sems.at[k]) for k, (src, dst) in enumerate(zip(sources, outs))
    ]
    for copy in copies:
        copy.start()
    state_width = w_state.shape[1]
    w_state_t[:state_width, :] = jnp.transpose(w_state[...].astype(F32)).astype(BF16)
    w_state_t[state_width:, :] = jnp.transpose(w_step[...].astype(F32)).astype(BF16)
    head = lax.broadcasted_iota(jnp.int32, spread.shape, 1) // head_dim
    row = lax.broadcasted_iota(jnp.int32, spread.shape, 0) % LANES
    spread[...] = jnp.where(head == row, 1.0, 0.0).astype(BF16)
    head = lax.broadcasted_iota(jnp.int32, gather.shape, 0) // head_dim
    lane = lax.broadcasted_iota(jnp.int32, gather.shape, 1)
    gather[...] = jnp.where(head == lane, 1.0, 0.0).astype(BF16)
    for copy in copies:
        copy.wait()


def project_kernel(
    i, scalars, own, oth, gain, w_gate, w_inner, w_state, w_step, conv, head_par, spread,
    normed_ref, gate_ref, pre_ref, slope_ref, hs_ref, act_ref, sact_ref, xd_ref, hf_ref, sb_ref,
    ext, carry, *, heads, width, state_width, block,
):
    @pl.when(i == 0)
    def _():
        ext[0:8, :] = jnp.zeros((8, ext.shape[1]), F32)
        carry[...] = jnp.zeros_like(carry)

    x = natural(scalars[1], own[...], oth[...]).astype(F32)
    inv = lax.rsqrt(jnp.mean(x * x, axis=-1, keepdims=True) + EPSILON)
    normed = (x * inv * gain[...]).astype(BF16)
    normed_ref[...] = normed
    step_pre = mm(normed, w_step[...])
    z = step_pre + head_par[0:1, :]
    dt = jnp.maximum(z, 0.0) + jnp.log1p(jnp.exp(-jnp.abs(z)))
    rate = head_par[1:2, :] * dt
    dtm = dt * row_mask(i, block, scalars[0])
    hs_ref[:, 0:LANES] = z
    hs_ref[:, LANES : 2 * LANES] = dt
    tri_r = lax.broadcasted_iota(jnp.int32, (CHUNK, CHUNK), 0)
    tri_c = lax.broadcasted_iota(jnp.int32, (CHUNK, CHUNK), 1)
    tri = (tri_c <= tri_r).astype(F32)
    is_fwd = lax.broadcasted_iota(jnp.int32, (CHUNK, LANES), 1) < heads
    per = block // CHUNK
    to_spread = [dtm]
    keeps = []
    for c_idx in range(per):
        rows = slice(c_idx * CHUNK, (c_idx + 1) * CHUNK)
        rate_c = rate[rows]
        cum = jnp.dot(tri, rate_c, precision=HIGHEST, preferred_element_type=F32)
        tot = cum[CHUNK - 1 : CHUNK, :]
        cumx = jnp.where(is_fwd, cum, cum - rate_c)
        hs_ref[rows, 2 * LANES : 3 * LANES] = cumx
        hs_ref[rows, 3 * LANES :] = jnp.broadcast_to(tot, (CHUNK, LANES))
        to_spread.append(dtm[rows] * jnp.exp(jnp.where(is_fwd, tot - cumx, cumx)))
        keeps.append(eight(jnp.exp(tot)))
    wide = expand(jnp.concatenate(to_spread + keeps, axis=0), spread[...])

    ext[8 : 8 + block, 0:width] = mm(normed, w_inner[...])
    ext[8 : 8 + block, width:] = mm(normed, w_state[...])
    gate_ref[...] = mm(normed, w_gate[...])
    whole_ext = ext[...]
    pre = whole_ext[8:]
    pre_ref[...] = pre.astype(BF16)
    c = conv[4:5, :] + conv[3:4, :] * pre
    for j in range(3):
        c = c + conv[j : j + 1, :] * pltpu.roll(whole_ext, 3 - j, 0)[8:]
    sg = sigmoid(c)
    both = c * sg
    slope_ref[...] = (sg * (1.0 + c * (1.0 - sg))).astype(BF16)
    ext[0:8, :] = ext[block : block + 8, :]
    act = both[:, :width]
    act_ref[...] = act
    sact = both[:, width:].astype(BF16)
    sact_ref[...] = sact
    xd_ref[:, 0:width] = (act * wide[0:block, :width]).astype(BF16)
    xd_ref[:, width:] = (act * wide[0:block, width:]).astype(BF16)
    n = state_width // 4
    for c_idx in range(per):
        rows = slice(c_idx * CHUNK, (c_idx + 1) * CHUNK)
        coef = wide[block + c_idx * CHUNK : block + (c_idx + 1) * CHUNK]
        keep = wide[2 * block + 8 * c_idx : 2 * block + 8 * c_idx + 1, :width]
        hf_ref[c_idx] = carry[...].astype(BF16)
        carry[...] = carry[...] * keep + mm_tn(
            sact[rows, 0:n], (act[rows] * coef[:, :width]).astype(BF16)
        )
        sb_ref[c_idx] = mm_tn(
            sact[rows, 2 * n : 3 * n], (act[rows] * coef[:, width:]).astype(BF16)
        )


def pair_tiles(pair):
    lane = lax.broadcasted_iota(jnp.int32, (1, pair.shape[1]), 1)
    first = (lane < pair.shape[1] // 2).astype(F32)
    keep_a, keep_b = first.astype(BF16), (1.0 - first).astype(BF16)
    return jnp.concatenate([pair * keep_a, pair * keep_b], axis=0)


def mix_kernel(
    i, scalars, act, sact, hs, xd, hf, sb, head_par, spread, y_ref, hb_ref, carry,
    *, heads, width, state_width, block,
):
    @pl.when(i == 0)
    def _():
        carry[...] = jnp.zeros_like(carry)

    n = state_width // 4
    per = block // CHUNK
    r = lax.broadcasted_iota(jnp.int32, (CHUNK, CHUNK), 0)
    c = lax.broadcasted_iota(jnp.int32, (CHUNK, CHUNK), 1)
    lower = c < r
    upper = c > r
    is_fwd = lax.broadcasted_iota(jnp.int32, (block, LANES), 1) < heads
    cum_all = hs[:, 2 * LANES : 3 * LANES]
    tot_all = hs[:, 3 * LANES :]
    wide = expand(
        jnp.concatenate(
            [jnp.exp(jnp.where(is_fwd, cum_all, tot_all - cum_all))]
            + [jnp.exp(tot_all[k * CHUNK : k * CHUNK + 8]) for k in range(per)]
            + [eight(head_par[2:3, :])],
            axis=0,
        ),
        spread[...],
    )
    skip = wide[block + 8 * per : block + 8 * per + 1]
    for c_idx in reversed(range(per)):
        rows = slice(c_idx * CHUNK, (c_idx + 1) * CHUNK)
        cumx = cum_all[rows] * LOG2_E
        cum_t = jnp.transpose(cumx)
        sact_c = sact[rows, :]
        b_f, c_f = sact_c[:, 0:n], sact_c[:, n : 2 * n]
        b_b, c_b = sact_c[:, 2 * n : 3 * n], sact_c[:, 3 * n :]
        s_f = jnp.where(lower, mm_nt(c_f, b_f), 0.0)
        s_b = jnp.where(upper, mm_nt(c_b, b_b), 0.0)
        hb = carry[...].astype(BF16)
        hb_ref[c_idx] = hb
        in_f = mm(c_f, hf[c_idx])
        in_b = mm(c_b, hb)
        keep = wide[block + 8 * c_idx : block + 8 * c_idx + 1, width:]
        carry[...] = carry[...] * keep + sb[c_idx]
        for p in range(heads // 2):
            lanes = slice(p * LANES, (p + 1) * LANES)
            lanes_b = slice(width + p * LANES, width + (p + 1) * LANES)
            w_f, w_b = [], []
            for h in (2 * p, 2 * p + 1):
                damp = jnp.exp2(
                    jnp.minimum(
                        cumx[:, h : h + 1] - cum_t[h : h + 1, :],
                        cum_t[heads + h : heads + h + 1, :] - cumx[:, heads + h : heads + h + 1],
                    )
                )
                w_f.append((s_f * damp).astype(BF16))
                w_b.append((s_b * damp).astype(BF16))
            out = mm(
                jnp.concatenate(w_f + w_b, axis=1),
                jnp.concatenate([pair_tiles(xd[rows, lanes]), pair_tiles(xd[rows, lanes_b])], axis=0),
            )
            y_ref[rows, lanes] = (
                out
                + wide[rows, lanes] * in_f[:, lanes]
                + wide[rows, lanes_b] * in_b[:, lanes]
                + skip[:, lanes] * act[rows, lanes]
            )


def gate_kernel(i, scalars, y, gate, cown, coth, po, gg, dgn_ref, gz_ref, sums_ref, *, block):
    gp = gate[...]
    gated = y[...] * (gp * sigmoid(gp))
    mask = row_mask(i, block, scalars[0])
    cot = natural(scalars[1], cown[...], coth[...])
    dgn = mm_nt((cot.astype(F32) * mask).astype(BF16), po[...])
    dgn_ref[...] = dgn
    scaled = gated * gg[...]
    gz_ref[...] = scaled.astype(BF16)
    sums_ref[...] = to_row(
        jnp.sum(gated * gated, axis=1, keepdims=True), jnp.sum(dgn * scaled, axis=1, keepdims=True)
    )


def gate_back_kernel(
    i, scalars, sums, gate, y, act, dgn, cown, coth, hs, sact, hf, hb, gg, spread, gather,
    g_ref, dgp_ref, dbr_ref, dc_ref, gb_ref, gf_ref, rd_ref, rows_ref, small_ref, carry, prod,
    *, heads, width, state_width, block, inner_width,
):
    @pl.when(i == 0)
    def _():
        carry[...] = jnp.zeros_like(carry)
        small_ref[...] = jnp.zeros_like(small_ref)

    per = block // CHUNK
    is_fwd = lax.broadcasted_iota(jnp.int32, (block, LANES), 1) < heads
    cum_all = hs[:, 2 * LANES : 3 * LANES]
    tot_all = hs[:, 3 * LANES :]
    wide = expand(
        jnp.concatenate(
            [jnp.exp(jnp.where(is_fwd, cum_all, tot_all - cum_all))]
            + [jnp.exp(tot_all[k * CHUNK : k * CHUNK + 8]) for k in range(per)],
            axis=0,
        ),
        spread[...],
    )
    cols = jnp.transpose(sums[...])
    gate_inv = lax.rsqrt(cols[:, 0:1] / inner_width + EPSILON)
    gate_dot = cols[:, 1:2] / inner_width
    gp = gate[...]
    sg = sigmoid(gp)
    act_gate = gp * sg
    yv = y[...]
    gated = yv * act_gate
    dg = dgn[...]
    small_ref[0:1, :] += jnp.sum(dg * gated * gate_inv, axis=0, keepdims=True)
    d_gated = gate_inv * (dg * gg[...]) - gated * (gate_inv * gate_inv * gate_inv * gate_dot)
    d_gp = d_gated * yv * (sg * (1.0 + gp * (1.0 - sg)))
    dgp_ref[...] = d_gp.astype(BF16)
    rd = jnp.sum(d_gp * gp, axis=1, keepdims=True)
    rd_ref[...] = to_row(rd, jnp.zeros_like(rd))
    d_y = d_gated * act_gate
    g_ref[...] = d_y.astype(BF16)
    small_ref[1:2, :] += jnp.sum(d_y * act[...], axis=0, keepdims=True)
    mask = row_mask(i, block, scalars[0])
    cot = natural(scalars[1], cown[...], coth[...])
    dbr_ref[...] = (cot.astype(F32) * (mask * gate_inv)).astype(BF16)
    n = state_width // 4
    for c_idx in range(per):
        rows = slice(c_idx * CHUNK, (c_idx + 1) * CHUNK)
        dy_c = d_y[rows]
        dyf = dy_c * wide[rows, :width]
        dyb = dy_c * wide[rows, width:]
        prod[rows, 0:width] = (dyf * mm(sact[rows, n : 2 * n], hf[c_idx])).astype(BF16)
        prod[rows, width:] = (dyb * mm(sact[rows, 3 * n :], hb[c_idx])).astype(BF16)
        dyf = dyf.astype(BF16)
        dyb = dyb.astype(BF16)
        dc_ref[rows, 0:n] = mm_nt(dyf, hf[c_idx])
        dc_ref[rows, n : 2 * n] = mm_nt(dyb, hb[c_idx])
        gb_ref[c_idx] = carry[...].astype(BF16)
        keep = wide[block + 8 * c_idx : block + 8 * c_idx + 1, width:]
        carry[...] = carry[...] * keep + mm_tn(sact[rows, 3 * n :], dyb)
        gf_ref[c_idx] = mm_tn(sact[rows, n : 2 * n], dyf)
    rows_ref[...] = mm(prod[...], gather[...])


def back_kernel(
    i, scalars, g, act, sact, hs, xd, row_in, hf, hb, gb, gf, dc, pre, slope, conv, head_par, spread, gather,
    ext_in, carry_in, gconv_in, ghead_in, _rest, _rd, rest_ref, rd_ref, gconv_ref, ghead_ref, ext_out,
    carry, ext, stack, xs, rsum,
    *, heads, width, state_width, block, top,
):
    blk = top - i
    per = block // CHUNK

    @pl.when(i == 0)
    def _():
        ext[block:, :] = ext_in[...]
        carry[...] = carry_in[...]
        gconv_ref[...] = gconv_in[...]
        ghead_ref[...] = ghead_in[...]
        stack[3 * CHUNK : 4 * CHUNK, width:] = jnp.zeros((CHUNK, width), BF16)
        rsum[...] = jnp.zeros_like(rsum)

    n = state_width // 4
    conv_width = width + state_width
    r = lax.broadcasted_iota(jnp.int32, (CHUNK, CHUNK), 0)
    c = lax.broadcasted_iota(jnp.int32, (CHUNK, CHUNK), 1)
    later = c > r
    earlier = c < r
    rev = (c >= r).astype(F32)
    tri = (c <= r).astype(F32)
    is_fwd_all = lax.broadcasted_iota(jnp.int32, (block, LANES), 1) < heads
    is_fwd = lax.broadcasted_iota(jnp.int32, (CHUNK, LANES), 1) < heads
    mask = row_mask(blk, block, scalars[0])
    dt_all = hs[:, LANES : 2 * LANES]
    cum_all = hs[:, 2 * LANES : 3 * LANES]
    tot_all = hs[:, 3 * LANES :]
    wide = expand(
        jnp.concatenate(
            [jnp.exp(jnp.where(is_fwd_all, tot_all - cum_all, cum_all)), dt_all * mask]
            + [jnp.exp(tot_all[k * CHUNK : k * CHUNK + 8]) for k in range(per)]
            + [eight(head_par[2:3, :])],
            axis=0,
        ),
        spread[...],
    )
    skip = wide[2 * block + 8 * per : 2 * block + 8 * per + 1]
    rd_parts = []
    for c_idx in reversed(range(per)):
        rows = slice(c_idx * CHUNK, (c_idx + 1) * CHUNK)
        rows_dt = slice(block + c_idx * CHUNK, block + (c_idx + 1) * CHUNK)
        z = hs[rows, 0:LANES]
        dt = dt_all[rows]
        cumx = cum_all[rows] * LOG2_E
        cum_t = jnp.transpose(cumx)
        sact_c = sact[rows, :]
        b_f, c_f = sact_c[:, 0:n], sact_c[:, n : 2 * n]
        b_b, c_b = sact_c[:, 2 * n : 3 * n], sact_c[:, 3 * n :]
        s_f = jnp.where(later, mm_nt(b_f, c_f), 0.0)
        s_b = jnp.where(earlier, mm_nt(b_b, c_b), 0.0)
        grad_f = carry[...]
        grad_f_low = grad_f.astype(BF16)
        grad_b_low = gb[c_idx]
        keep = wide[2 * block + 8 * c_idx : 2 * block + 8 * c_idx + 1]
        keep_f = keep[:, :width]
        edge_f = keep_f * jnp.sum(grad_f * hf[c_idx].astype(F32), axis=0, keepdims=True)
        edge_b = keep[:, width:] * jnp.sum(
            hb[c_idx].astype(F32) * grad_b_low.astype(F32), axis=0, keepdims=True
        )
        e_hi, e_lo = split_two(eight(jnp.concatenate([edge_f, edge_b], axis=1)))
        stack[4 * CHUNK :, :] = jnp.concatenate([e_hi, e_lo], axis=0)
        carry[...] = grad_f * keep_f + gf[c_idx]
        in_f = mm(b_f, grad_f_low)
        in_b = mm(b_b, grad_b_low)
        d_scores = jnp.zeros((CHUNK, CHUNK), F32)
        for p in range(heads // 2):
            lanes = slice(p * LANES, (p + 1) * LANES)
            lanes_b = slice(width + p * LANES, width + (p + 1) * LANES)
            g_pair = g[rows, lanes]
            xf_pair = xd[rows, lanes]
            xb_pair = xd[rows, lanes_b]
            dw = mm_nt(
                jnp.concatenate([pair_tiles(xf_pair), pair_tiles(xb_pair)], axis=0), g_pair
            )
            w_f, w_b = [], []
            for q, h in enumerate((2 * p, 2 * p + 1)):
                damp = jnp.exp2(
                    jnp.minimum(
                        cum_t[h : h + 1, :] - cumx[:, h : h + 1],
                        cumx[:, heads + h : heads + h + 1] - cum_t[heads + h : heads + h + 1, :],
                    )
                )
                low_f = (s_f * damp).astype(BF16)
                low_b = (s_b * damp).astype(BF16)
                w_f.append(low_f)
                w_b.append(low_b)
                dw_f = dw[q * CHUNK : (q + 1) * CHUNK]
                dw_b = dw[(2 + q) * CHUNK : (3 + q) * CHUNK]
                d_scores = d_scores + jnp.where(later, dw_f, dw_b) * damp
                rsum[h : h + 1, :] = jnp.sum(dw_f * low_f.astype(F32), axis=0, keepdims=True)
                rsum[heads + h : heads + h + 1, :] = -jnp.sum(
                    dw_b * low_b.astype(F32), axis=0, keepdims=True
                )
            dx = mm(
                jnp.concatenate(
                    [jnp.concatenate(w_f, axis=1), jnp.concatenate(w_b, axis=1)], axis=0
                ),
                pair_tiles(g_pair),
            )
            edge_pf = wide[rows, lanes]
            edge_pb = wide[rows, lanes_b]
            intra_f = dx[:CHUNK]
            inter_f = edge_pf * in_f[:, lanes]
            dx_f = intra_f + inter_f
            dx_b = dx[CHUNK:] + edge_pb * in_b[:, lanes]
            xf = xf_pair.astype(F32)
            xb = xb_pair.astype(F32)
            xs[:, lanes] = (xf * edge_pf).astype(BF16)
            xs[:, lanes_b] = (xb * edge_pb).astype(BF16)
            act_p = act[rows, lanes]
            hi, lo = split_two(-(xf * intra_f))
            stack[0:CHUNK, lanes] = hi
            stack[CHUNK : 2 * CHUNK, lanes] = lo
            hi, lo = split_two(xb * dx_b)
            stack[0:CHUNK, lanes_b] = hi
            stack[CHUNK : 2 * CHUNK, lanes_b] = lo
            stack[2 * CHUNK : 3 * CHUNK, lanes] = (act_p * dx_f).astype(BF16)
            stack[2 * CHUNK : 3 * CHUNK, lanes_b] = (act_p * dx_b).astype(BF16)
            stack[3 * CHUNK : 4 * CHUNK, lanes] = (xf * inter_f).astype(BF16)
            d_inner = (
                skip[:, lanes] * g_pair.astype(F32)
                + wide[rows_dt, lanes] * dx_f
                + wide[rows_dt, lanes_b] * dx_b
            )
            ext[rows, lanes] = d_inner * slope[rows, lanes].astype(F32)
        low_f = jnp.where(later, d_scores, 0.0).astype(BF16)
        low_b = jnp.where(earlier, d_scores, 0.0).astype(BF16)
        d_bf = mm(low_f, c_f) + mm_nt(xs[:, :width], grad_f_low)
        d_cf = mm_tn(low_f, b_f) + dc[rows, 0:n]
        d_bb = mm(low_b, c_b) + mm_nt(xs[:, width:], grad_b_low)
        d_cb = mm_tn(low_b, b_b) + dc[rows, n : 2 * n]
        d_state = jnp.concatenate([d_bf, d_cf, d_bb, d_cb], axis=1)
        ext[rows, width:] = d_state * slope[rows, width:].astype(F32)
        head_sums = mm(stack[...], gather[...])
        rin = row_in[rows, :]
        d_cum = (
            head_sums[0:CHUNK]
            + head_sums[CHUNK : 2 * CHUNK]
            + jnp.transpose(rsum[...])
            + jnp.where(is_fwd, rin, 0.0)
        )
        d_run = head_sums[3 * CHUNK : 4 * CHUNK] + jnp.where(is_fwd, 0.0, rin)
        edge = head_sums[4 * CHUNK : 4 * CHUNK + 1] + head_sums[4 * CHUNK + 8 : 4 * CHUNK + 9]
        back_run = jnp.dot(rev, d_cum, precision=HIGHEST, preferred_element_type=F32)
        run = jnp.dot(tri, d_run, precision=HIGHEST, preferred_element_type=F32)
        d_rate = jnp.where(is_fwd, back_run + run - d_run, back_run - d_cum + run) + edge
        neg = head_par[1:2, :]
        d_step = neg * d_rate + mask[rows] * head_sums[2 * CHUNK : 3 * CHUNK]
        d_z = d_step / (1.0 + jnp.exp(-z))
        ghead_ref[0:1, :] += jnp.sum(d_rate * (neg * dt), axis=0, keepdims=True)
        ghead_ref[1:2, :] += jnp.sum(d_z, axis=0, keepdims=True)
        rest_ref[rows, conv_width:] = d_z.astype(BF16)
        rd_parts.append(jnp.sum(d_z * (z - head_par[0:1, :]), axis=1, keepdims=True))

    prev = pre[...].astype(F32)
    whole_ext = ext[...]
    moved = whole_ext[:block]
    acc = conv[3:4, :] * moved
    gconv_ref[4:5, :] += jnp.sum(moved, axis=0, keepdims=True)
    gconv_ref[3:4, :] += jnp.sum(moved * prev, axis=0, keepdims=True)
    for j in range(3):
        moved = pltpu.roll(whole_ext, block + 8 - (3 - j), 0)[:block]
        acc = acc + conv[j : j + 1, :] * moved
        gconv_ref[j : j + 1, :] += jnp.sum(moved * prev, axis=0, keepdims=True)
    rest_ref[:, 0:conv_width] = acc.astype(BF16)
    rd = jnp.sum(acc * prev, axis=1, keepdims=True) + jnp.concatenate(rd_parts[::-1], axis=0)
    rd_ref[...] = to_row(rd, jnp.zeros_like(rd))
    ext[block:, :] = ext[0:8, :]
    ext_out[...] = ext[0:8, :]


def columns_of(scalars, other, size):
    rank = scalars[1]
    return pl.ds(pl.multiple_of((1 - rank if other else rank) * size, LANES), size)


def branch_kernel(scalars, gz, po, out_ref, *, other):
    cols = columns_of(scalars, other, out_ref.shape[1])
    out_ref[...] = mm(gz[...], po[:, cols]).astype(out_ref.dtype)


def back_project_kernel(
    scalars, dgp, rest, w_gate, w_inner, w_state, w_step, out_ref, *, other
):
    at = columns_of(scalars, other, out_ref.shape[1])
    a = w_inner.shape[1]
    b = a + w_state.shape[1]
    out_ref[...] = (
        mm_nt(dgp[...], w_gate[at, :])
        + mm_nt(rest[:, 0:a], w_inner[at, :])
        + mm_nt(rest[:, a:b], w_state[at, :])
        + mm_nt(rest[:, b:], w_step[at, :])
    ).astype(out_ref.dtype)


def home_of(r, me, order):
    j = me % SHARDS
    levels = len(order)
    for p, bit in enumerate(order):
        if (r >> (levels - 1 - p)) & 1:
            j = jnp.bitwise_xor(j, 1 << bit)
    return j


def pack_early_kernel(
    scalars, grad_out, grad_gate, w_gate, keep_ref, send_ref, gain_ref, *, order
):
    hi, lo = split_two(grad_gate[...].astype(F32) * w_gate[...].astype(F32))
    ones = jnp.ones((8, hi.shape[1]), BF16)
    gain_ref[...] = mm_nt(ones, hi) + mm_nt(ones, lo)
    part = grad_out.shape[0] // SHARDS
    for r in range(SHARDS):
        j = home_of(r, scalars[2], order)
        out = keep_ref if r < SHARDS // 2 else send_ref
        at = (r % (SHARDS // 2)) * 2 * part
        src = pl.ds(pl.multiple_of(j * part, part), part)
        out[at : at + part, :] = grad_out[src, :]
        out[at + part : at + 2 * part, :] = grad_gate[src, :]


def unpack_early_kernel(scalars, first, second, out_ref, gate_ref, *, order):
    part = out_ref.shape[0] // SHARDS
    for r in range(SHARDS):
        j = home_of(r, scalars[2], order)
        src = first if r < SHARDS // 2 else second
        at = (r % (SHARDS // 2)) * 2 * part
        dst = pl.ds(pl.multiple_of(j * part, part), part)
        out_ref[dst, :] = src[at : at + part, :].astype(F32)
        gate_ref[dst, :] = src[at + part : at + 2 * part, :].astype(F32)


def pack_late_kernel(
    scalars, inner, state, w_inner, w_state_t, gain, gain_part, gconv, ghead, small,
    keep_ref, send_ref, misc, *, order, heads, state_width,
):
    model, width = w_inner.shape
    hi, lo = split_two(inner[...].astype(F32) * w_inner[...].astype(F32))
    ones = jnp.ones((8, hi.shape[1]), BF16)
    gain_row = (mm_nt(ones, hi) + mm_nt(ones, lo) + gain_part[...])[0:1]
    gain_row += jnp.sum(state[...].astype(F32) * w_state_t[...].astype(F32), axis=0, keepdims=True)
    gain_row = gain_row / gain[...]
    step = state[state_width:, :].astype(F32)
    misc[...] = jnp.zeros_like(misc)

    def put_single(k, row):
        at = (k // 2) * 8 + k % 2
        misc[at : at + 1, :] = row

    for k in range(2 * heads):
        put_single(k, step[k : k + 1, :])
    at = 2 * heads
    for k in range(5):
        put_single(at + k, gconv[k : k + 1, 0:width])
    put_single(at + 5, small[0:1, :])
    put_single(at + 6, small[1:2, :])
    at = ((at + 7) // 2) * 8 + (at + 7) % 2
    misc[at : at + 1, 0:LANES] = ghead[0:1, :]
    misc[at : at + 1, LANES : 2 * LANES] = ghead[1:2, :]
    fit = model // state_width
    for k in range(5):
        at = (k // fit) * 8 + 4
        lanes = slice((k % fit) * state_width, (k % fit + 1) * state_width)
        misc[at : at + 1, lanes] = gconv[k : k + 1, width:]
    at = (-(-5 // fit)) * 8 + 4
    misc[at : at + 1, :] = gain_row
    part = model // SHARDS
    part_s = state_width // SHARDS
    rows = part + part_s + 8
    for r in range(SHARDS):
        j = home_of(r, scalars[2], order)
        out = keep_ref if r < SHARDS // 2 else send_ref
        at = (r % (SHARDS // 2)) * rows
        out[at : at + part, :] = inner[pl.ds(pl.multiple_of(j * part, part), part), :]
        out[at + part : at + part + part_s, :] = state[
            pl.ds(pl.multiple_of(j * part_s, part_s), part_s), :
        ]
        out[at + part + part_s : at + rows, :] = misc[
            pl.ds(pl.multiple_of(j * 8, 8), 8), :
        ].astype(BF16)


def unpack_late_kernel(
    scalars, first, second, inner_ref, state_ref, step_ref, convi_ref, singles_ref, convs_ref,
    state, misc, *, order, heads,
):
    model = inner_ref.shape[0]
    state_width = state_ref.shape[1]
    part = model // SHARDS
    part_s = state_width // SHARDS
    rows = part + part_s + 8
    for r in range(SHARDS):
        j = home_of(r, scalars[2], order)
        src = first if r < SHARDS // 2 else second
        at = (r % (SHARDS // 2)) * rows
        inner_ref[pl.ds(pl.multiple_of(j * part, part), part), :] = src[at : at + part, :].astype(F32)
        state[pl.ds(pl.multiple_of(j * part_s, part_s), part_s), :] = src[
            at + part : at + part + part_s, :
        ].astype(F32)
        misc[pl.ds(pl.multiple_of(j * 8, 8), 8), :] = src[at + part + part_s : at + rows, :].astype(F32)
    state_ref[...] = jnp.transpose(state[...])

    def single(k):
        at = (k // 2) * 8 + k % 2
        return misc[at : at + 1, :]

    for h in range(heads):
        for d in range(2):
            step_ref[h, d : d + 1, :] = single(d * heads + h)
    at = 2 * heads
    for k in range(4):
        convi_ref[k : k + 1, :] = single(at + k)
    singles_ref[0:1, :] = single(at + 4)
    singles_ref[1:2, :] = single(at + 5)
    singles_ref[2:3, :] = single(at + 6)
    singles_ref[3:4, :] = single(at + 7)
    fit = model // state_width
    at = (-(-5 // fit)) * 8 + 4
    singles_ref[4:5, :] = misc[at : at + 1, :]
    singles_ref[5:8, :] = jnp.zeros((3, model), F32)
    for k in range(5):
        at = (k // fit) * 8 + 4
        lanes = slice((k % fit) * state_width, (k % fit + 1) * state_width)
        if k < 4:
            convs_ref[k : k + 1, :] = misc[at : at + 1, lanes]
        else:
            singles_ref[5:6, 0:state_width] = misc[at : at + 1, lanes]


def place(i, top):
    return i if top is None else top - i


def rows_of(block, top=None):
    return lambda ref, i: ref.at[pl.ds(pl.multiple_of(place(i, top) * block, block), block)]


def lanes_of(block, top=None):
    return lambda ref, i: ref.at[:, pl.ds(pl.multiple_of(place(i, top) * block, block), block)]


def states_of(block, top=None):
    per = block // CHUNK
    return lambda ref, i: ref.at[pl.ds(place(i, top) * per, per)]


def fixed(ref, i):
    return ref


def call(kernel, blocks, ins, out_views, out_shape, scratch, name, us, aliases=None):
    views = [view for _, view in ins[1:]] + out_views
    arrays = [ins[0]] + [
        pltpu.with_memory_space_constraint(x, pltpu.VMEM) if view is not fixed else x
        for x, view in ins[1:]
    ]

    def looped(scalars, *refs):
        def step(i, _):
            blocks_of = [view(ref, i) for view, ref in zip(views, refs)]
            kernel(i, scalars, *blocks_of, *refs[len(views) :])
            return 0

        lax.fori_loop(0, blocks, step, 0)

    vmem = pl.BlockSpec(memory_space=pltpu.VMEM)
    return pl.pallas_call(
        looped,
        out_shape=[pltpu.VMEM(o.shape, o.dtype) for o in out_shape],
        in_specs=[pl.BlockSpec(memory_space=pltpu.SMEM)] + [vmem] * (len(arrays) - 1),
        out_specs=[vmem] * len(out_shape),
        scratch_shapes=scratch,
        compiler_params=pltpu.CompilerParams(vmem_limit_bytes=VMEM_LIMIT),
        cost_estimate=pl.CostEstimate(
            flops=int(us * 5e8), transcendentals=0, bytes_accessed=int(us * 3e6)
        ),
        name=name,
        input_output_aliases=aliases or {},
    )(*arrays)


def whole(kernel, args, out_shape, scratch, name, us, in_vmem=True):
    vmem = pl.BlockSpec(memory_space=pltpu.VMEM)
    return pl.pallas_call(
        kernel,
        out_shape=[pltpu.VMEM(o.shape, o.dtype) if in_vmem else o for o in out_shape],
        in_specs=[pl.BlockSpec(memory_space=pltpu.SMEM)] + [vmem] * (len(args) - 1),
        out_specs=[vmem] * len(out_shape),
        scratch_shapes=scratch,
        compiler_params=pltpu.CompilerParams(vmem_limit_bytes=VMEM_LIMIT),
        cost_estimate=pl.CostEstimate(
            flops=int(us * 5e8), transcendentals=0, bytes_accessed=int(us * 3e6)
        ),
        name=name,
    )(*args)


def swap_mp(x):
    return lax.ppermute(x, "mp", [(0, 1), (1, 0)])


def swap_dp(x, bit):
    size = lax.axis_size("dp")
    return lax.ppermute(x, "dp", [(i, i ^ (1 << bit)) for i in range(size)])


def add_low(a, b):
    return (a.astype(F32) + b.astype(F32)).astype(BF16)


def after(x, *others):
    return lax.optimization_barrier((x, *others))[0]


def body(
    tokens,
    norm_gain,
    proj_gate,
    proj_inner,
    proj_state,
    proj_step,
    conv_inner,
    conv_inner_bias,
    conv_state,
    conv_state_bias,
    step_bias,
    decay_log,
    skip_gain,
    gate_gain,
    proj_out,
    lengths,
    cotangent,
):
    rows, width_own = tokens.shape
    model = 2 * width_own
    heads = skip_gain.shape[0]
    width = proj_inner.shape[1]
    head_dim = width // heads
    state_width = proj_state.shape[1]
    n = state_width // 4
    conv_width = width + state_width
    inner_width = width * lax.axis_size("mp")
    chunks = rows // CHUNK
    rank = lax.axis_index("mp")
    shape = jax.ShapeDtypeStruct

    oth_tokens = swap_mp(tokens)
    oth_gain = swap_mp(norm_gain.reshape(1, width_own))
    oth_cot = swap_mp(after(cotangent, oth_tokens))

    scalars = jnp.stack([lengths[0], rank, lax.axis_index("dp")]).astype(jnp.int32)
    step_weight = proj_step.reshape(model, 2 * heads)
    step_weight = jnp.pad(step_weight, ((0, 0), (0, LANES - 2 * heads)))
    own_gain = norm_gain.reshape(1, width_own)
    gain = natural(rank, own_gain, oth_gain).astype(F32)
    conv = jnp.concatenate(
        [
            jnp.concatenate([conv_inner, conv_state], axis=1),
            jnp.concatenate([conv_inner_bias, conv_state_bias])[None],
            jnp.zeros((3, conv_width), F32),
        ]
    )
    head_par = jnp.stack(
        [
            step_bias.reshape(-1),
            -jnp.exp(decay_log.reshape(-1)),
            jnp.pad(skip_gain, (0, heads)),
        ]
    )
    head_par = jnp.pad(head_par, ((0, 5), (0, LANES - 2 * heads)))
    staged = (tokens, cotangent, proj_gate, proj_inner, proj_state, proj_out)
    hbm = pl.BlockSpec(memory_space=pl.ANY)
    vmem = pl.BlockSpec(memory_space=pltpu.VMEM)
    tokens_v, cot_v, gate_v, inner_v, state_v, out_v, spread, gather, w_state_t = pl.pallas_call(
        partial(stage_kernel, count=len(staged), head_dim=head_dim),
        out_shape=[pltpu.VMEM(x.shape, x.dtype) for x in staged]
        + [
            pltpu.VMEM((2 * LANES, 2 * width), BF16),
            pltpu.VMEM((2 * width, LANES), BF16),
            pltpu.VMEM((state_width + LANES, model), BF16),
        ],
        in_specs=[vmem, vmem] + [hbm] * len(staged),
        out_specs=[vmem] * (len(staged) + 3),
        scratch_shapes=[pltpu.SemaphoreType.DMA((len(staged),))],
        compiler_params=pltpu.CompilerParams(vmem_limit_bytes=VMEM_LIMIT),
        name="stage",
    )(proj_state, step_weight, *staged)
    gg = gate_gain[None]

    sizes = dict(heads=heads, width=width, state_width=state_width)
    low = lambda *dims: shape(dims, BF16)
    full = lambda *dims: shape(dims, F32)
    block = PROJECT_BLOCK
    up, states = rows_of(block), states_of(block)
    normed, gate_pre, pre, slope, hs, act, sact, xd, hf, sb = call(
        partial(project_kernel, block=block, **sizes),
        rows // block,
        [
            scalars,
            (tokens_v, up),
            (oth_tokens, up),
            (gain, fixed),
            (gate_v, fixed),
            (inner_v, fixed),
            (state_v, fixed),
            (step_weight, fixed),
            (conv, fixed),
            (head_par, fixed),
            (spread, fixed),
        ],
        [up, up, up, up, up, up, up, up, states, states],
        [
            low(rows, model),
            full(rows, width),
            low(rows, conv_width),
            low(rows, conv_width),
            full(rows, 4 * LANES),
            full(rows, width),
            low(rows, state_width),
            low(rows, 2 * width),
            low(chunks, n, width),
            full(chunks, n, width),
        ],
        [pltpu.VMEM((block + 8, conv_width), F32), pltpu.VMEM((n, width), F32)],
        "project",
        12,
    )

    block = MIX_BLOCK
    top = rows // block - 1
    down, states_down = rows_of(block, top), states_of(block, top)
    y, hb = call(
        partial(mix_kernel, block=block, **sizes),
        rows // block,
        [
            scalars,
            (act, down),
            (sact, down),
            (hs, down),
            (xd, down),
            (hf, states_down),
            (sb, states_down),
            (head_par, fixed),
            (spread, fixed),
        ],
        [down, states_down],
        [full(rows, width), low(chunks, n, width)],
        [pltpu.VMEM((n, width), F32)],
        "mix",
        7,
    )

    block = GATE_BLOCK
    up, states, up_lanes = rows_of(block), states_of(block), lanes_of(block)
    dgn, gz, sums = call(
        partial(gate_kernel, block=block),
        rows // block,
        [
            scalars,
            (y, up),
            (gate_pre, up),
            (cot_v, up),
            (oth_cot, up),
            (out_v, fixed),
            (gg, fixed),
        ],
        [up, up, up_lanes],
        [full(rows, width), low(rows, width), full(8, rows)],
        [],
        "gate",
        3,
    )

    oth_sums = swap_mp(sums)
    branch_oth = whole(
        partial(branch_kernel, other=True), (scalars, gz, out_v), [low(rows, width_own)], [], "branch_oth", 3
    )[0]
    sums = sums + oth_sums
    branch_got = swap_mp(after(branch_oth, sums))
    sums_in = after(sums, branch_oth)

    g, dgp, dbr, dc, gb, gf, rd_gate, row_sums, small = call(
        partial(gate_back_kernel, block=block, inner_width=inner_width, **sizes),
        rows // block,
        [
            scalars,
            (sums_in, up_lanes),
            (gate_pre, up),
            (y, up),
            (act, up),
            (dgn, up),
            (cot_v, up),
            (oth_cot, up),
            (hs, up),
            (sact, up),
            (hf, states),
            (hb, states),
            (gg, fixed),
            (spread, fixed),
            (gather, fixed),
        ],
        [up, up, up, up, states, states, up_lanes, up, fixed],
        [
            low(rows, width),
            low(rows, width),
            low(rows, model),
            full(rows, 2 * n),
            low(chunks, n, width),
            full(chunks, n, width),
            full(8, rows),
            full(rows, LANES),
            full(8, width),
        ],
        [pltpu.VMEM((n, width), F32), pltpu.VMEM((block, 2 * width), BF16)],
        "gate_back",
        8,
    )

    def back_part(first, count, g, state):
        block = BACK_BLOCK
        here, states_here, here_lanes = rows_of(block, first), states_of(block, first), lanes_of(block, first)
        ins = [
            scalars,
            (g, here),
            (act, here),
            (sact, here),
            (hs, here),
            (xd, here),
            (row_sums, here),
            (hf, states_here),
            (hb, states_here),
            (gb, states_here),
            (gf, states_here),
            (dc, here),
            (pre, here),
            (slope, here),
            (conv, fixed),
            (head_par, fixed),
            (spread, fixed),
            (gather, fixed),
            *[(x, fixed) for x in state[:4]],
            (state[4], here),
            (state[5], here_lanes),
        ]
        return call(
            partial(back_kernel, block=block, top=first, **sizes),
            count,
            ins,
            [here, here_lanes, fixed, fixed, fixed, fixed],
            [
                low(rows, conv_width + LANES),
                full(8, rows),
                full(8, conv_width),
                full(8, LANES),
                full(8, conv_width),
                full(n, width),
            ],
            [
                pltpu.VMEM((block + 8, conv_width), F32),
                pltpu.VMEM((4 * CHUNK + 16, 2 * width), BF16),
                pltpu.VMEM((CHUNK, 2 * width), BF16),
                pltpu.VMEM((LANES, CHUNK), F32),
            ],
            "mix_back",
            3 * count,
            aliases={len(ins) - 2: 0, len(ins) - 1: 1},
        )

    order_a, order_b = (0, 2, 1, 3), (0, 1, 2, 3)
    grad_out = mm_tn(gz, dbr).astype(BF16)
    grad_gate = mm_tn(normed, dgp).astype(BF16)
    keep, send, gain_part = whole(
        partial(pack_early_kernel, order=order_a),
        (scalars, grad_out, grad_gate, proj_gate),
        [low(width, model), low(width, model), full(8, model)],
        [],
        "pack_early",
        3,
    )

    def halve(keep, send, bit):
        got = swap_dp(send, bit)
        h = keep.shape[0] // 2
        return add_low(keep[:h], got[:h]), add_low(keep[h:], got[h:])

    def finish(keep, send, bit):
        return rest_of_dp(add_low(keep, swap_dp(send, bit)))

    def rest_of_dp(x):
        extra = SHARDS
        while extra < lax.axis_size("dp"):
            x = add_low(x, swap_dp(x, extra.bit_length() - 1))
            extra *= 2
        return x

    zeros = (
        jnp.zeros((8, conv_width), F32),
        jnp.zeros((n, width), F32),
        jnp.zeros((8, conv_width), F32),
        jnp.zeros((8, LANES), F32),
    )
    keep, send = halve(keep, send, order_a[0])
    state = (
        *zeros,
        jnp.zeros((rows, conv_width + LANES), BF16),
        jnp.zeros((8, rows), F32),
    )
    parts = 4
    count = rows // BACK_BLOCK // parts
    g = after(g, send)
    sent, x = swap_dp(send, order_a[1]), None
    for k in range(parts):
        outs = back_part((parts - k) * count - 1, count, g, state)
        rest, rd_rest, gconv, ghead, ext_carry, carry = outs
        if k > 0:
            sent, carry = lax.optimization_barrier((sent, carry))
            h = keep.shape[0] // 2
            if k < 3:
                keep, send = add_low(keep[:h], sent[:h]), add_low(keep[h:], sent[h:])
                carry = after(carry, send)
                sent = swap_dp(send, order_a[k + 1])
            else:
                x = rest_of_dp(add_low(keep, sent))
        state = (ext_carry, carry, gconv, ghead, rest, rd_rest)

    grad_inner = mm_tn(normed, rest[:, :width]).astype(BF16)
    grad_state = mm_tn(rest[:, width:], normed).astype(BF16)
    keep, send = whole(
        partial(pack_late_kernel, order=order_b, heads=heads, state_width=state_width),
        (
            scalars, grad_inner, grad_state, proj_inner, w_state_t, gain, gain_part, gconv, ghead, small
        ),
        [low(LATE_ROWS * SHARDS // 2, model), low(LATE_ROWS * SHARDS // 2, model)],
        [pltpu.VMEM((8 * SHARDS, model), F32)],
        "pack_late",
        3,
    )

    keep, send = halve(keep, send, order_b[0])
    rest, gz_late, tokens_late, oth_late = lax.optimization_barrier((rest, gz, tokens, oth_tokens, send))[:4]
    back_args = (scalars, dgp, rest, gate_v, inner_v, state_v, step_weight)

    def halve_with(keep, send, bit, *work):
        got = after(swap_dp(send, bit), *work)
        h = keep.shape[0] // 2
        return add_low(keep[:h], got[:h]), add_low(keep[h:], got[h:])

    dn_oth = whole(
        partial(back_project_kernel, other=True), back_args, [low(rows, width_own)], [], "back_oth", 4
    )[0]
    rd_part = rd_gate[0] + rd_rest[0]
    sent = swap_dp(x, order_a[3])
    x = jnp.concatenate([x, sent])
    keep, send = halve_with(keep, send, order_b[1], dn_oth, rd_part, x)
    dn_got = swap_mp(dn_oth)
    oth_rd = swap_mp(rd_part.reshape(8, rows // 8)).reshape(rows)
    dn_own = whole(
        partial(back_project_kernel, other=False), back_args, [full(rows, width_own)], [], "back_own", 4
    )[0]
    x = after(x, send)
    sent = swap_dp(x, order_a[2])
    keep, send = halve_with(keep, send, order_b[2], dn_own)

    seq_mask = (jnp.arange(rows) < lengths[0]).astype(F32)[:, None]
    gate_inv = lax.rsqrt(sums[0] / inner_width + EPSILON)[:, None]
    tokens_f = tokens_late.astype(F32)
    branch_own = whole(
        partial(branch_kernel, other=False), (scalars, gz_late, out_v), [full(rows, width_own)], [], "branch_own", 3
    )[0]
    block_out = (tokens_f + seq_mask * gate_inv * (branch_own + branch_got.astype(F32))).astype(BF16)
    x = jnp.concatenate([x, sent])
    z = rest_of_dp(add_low(keep, after(swap_dp(send, order_b[3]), block_out, x)))
    part = model // SHARDS
    tail = z[part:]
    tail_row = lax.broadcasted_iota(jnp.int32, (LATE_ROWS - part, 1), 0)
    alone = (tail_row >= LATE_ROWS - part - 8) & (tail_row < LATE_ROWS - part - 4)
    tail_f = tail.astype(F32)
    tail = jnp.where(alone, tail_f, tail_f + swap_mp(tail).astype(F32)).astype(BF16)
    z = jnp.concatenate([z[:part], tail])
    z = after(z, dn_got)

    oth_f = oth_late.astype(F32)
    square = jnp.sum(tokens_f * tokens_f, axis=1, keepdims=True) + jnp.sum(
        oth_f * oth_f, axis=1, keepdims=True
    )
    inv = lax.rsqrt(square / model + EPSILON)
    grad_full = dn_own + dn_got.astype(F32)
    grad_tokens = (
        cotangent.astype(F32)
        + inv * (grad_full * norm_gain.astype(F32)[None])
        - tokens_f * (inv * inv * ((rd_part + oth_rd)[:, None] / model))
    )

    z = jnp.concatenate([z, swap_dp(z, order_b[3])])
    z = jnp.concatenate([z, after(swap_dp(z, order_b[2]), grad_tokens)])
    x = after(x, z)
    x = jnp.concatenate([x, swap_dp(x, order_a[1])])
    grad_proj_out, grad_proj_gate = whole(
        partial(unpack_early_kernel, order=order_a),
        (scalars, x, swap_dp(x, order_a[0])),
        [full(width, model), full(model, width)],
        [],
        "unpack_early",
        4,
        in_vmem=False,
    )
    z = jnp.concatenate([z, swap_dp(z, order_b[1])])
    grad_proj_inner, grad_proj_state, step, grad_conv_inner, singles, grad_conv_state = whole(
        partial(unpack_late_kernel, order=order_b, heads=heads),
        (scalars, z, swap_dp(z, order_b[0])),
        [
            full(model, width),
            full(model, state_width),
            full(heads, 2, model),
            full(4, width),
            full(8, model),
            full(4, state_width),
        ],
        [pltpu.VMEM((state_width, model), F32), pltpu.VMEM((8 * SHARDS, model), F32)],
        "unpack_late",
        4,
        in_vmem=False,
    )
    grad_norm_gain = lax.dynamic_slice_in_dim(singles[4], rank * width_own, width_own, 0)
    grad_skip = jnp.sum(singles[2].reshape(heads, head_dim), axis=1)
    grad_decay_log = singles[3, : 2 * heads].reshape(2, heads)
    grad_step_bias = singles[3, LANES : LANES + 2 * heads].reshape(2, heads)

    return (
        block_out,
        grad_tokens,
        grad_norm_gain,
        grad_proj_gate,
        grad_proj_inner,
        grad_proj_state,
        step.transpose(2, 1, 0),
        grad_conv_inner,
        singles[0],
        grad_conv_state,
        singles[5, :state_width],
        grad_step_bias,
        grad_decay_log,
        grad_skip,
        singles[1],
        grad_proj_out,
    )


def solution(mesh):
    in_specs = (
        P("dp", "mp"),
        P("mp"),
        P(None, "mp"),
        P(None, "mp"),
        P(),
        P(None, None, "mp"),
        P(None, "mp"),
        P("mp"),
        P(),
        P(),
        P(None, "mp"),
        P(None, "mp"),
        P("mp"),
        P("mp"),
        P("mp", None),
        P("dp"),
        P("dp", "mp"),
    )
    out_specs = (
        P("dp", "mp"),
        P("dp", "mp"),
        P("mp"),
        P(None, "mp"),
        P(None, "mp"),
        P(),
        P(None, None, "mp"),
        P(None, "mp"),
        P("mp"),
        P(),
        P(),
        P(None, "mp"),
        P(None, "mp"),
        P("mp"),
        P("mp"),
        P("mp", None),
    )
    return jax.shard_map(body, mesh=mesh, in_specs=in_specs, out_specs=out_specs, check_vma=False)
```

profile of v0, /device:TPU:0, one launch (start us, length us, event | category | flops | bytes accessed | tf_op | source)
XLA Modules:
  0.0 187.9 jit_solution(12618619645020632299)
XLA Ops:
  1.3 3.0 %collective-permute-start.1 = (bf16[1,384]{1,0:T(2,128)(2,1)S(1)}, bf16[1,384]{1,0:T(2,128)(2,1)S(1)}, u32[]{:S(2)}, u32[]{:S(2)}) collective-permute-start(bf16[1,384]{1,0:T(2,128)(2,1)S(1)} %concatenate.56), channel_id=1, source_target_pairs={{0,1},{1,0},{2,3},{3,2},{4,5},{5,4},{6,7},{7,6},{8,9},{9,8},{10,11... | collective-permute-start | bytes 2312 | tf_op jit(solution)/shard_map/ppermute | solution.py:717
  19.2 4.3 %collective-permute-done.refs_1_ = bf16[1024,384]{1,0:T(8,128)(2,1)S(1)} collective-permute-done((bf16[1024,384]{1,0:T(8,128)(2,1)}, bf16[1024,384]{1,0:T(8,128)(2,1)S(1)}, u32[]{:S(2)}, u32[]{:S(2)}) %collective-permute-start) | collective-permute-done | bytes 786464 | tf_op jit(solution)/shard_map/ppermute | solution.py:717
  23.8 11.1 %project.1 = (bf16[1024,768]{1,0:T(8,128)(2,1)S(1)}, f32[1024,768]{1,0:T(8,128)S(1)}, bf16[1024,1024]{1,0:T(8,128)(2,1)S(1)}, bf16[1024,1024]{1,0:T(8,128)(2,1)S...) custom-call(s32[3]{0:T(128)S(1)} %pad_add_fusion.scalars, ...), custom_call_target="tpu_custom_call" | custom-call | flops 6000000000 | bytes 36000000 | tf_op jit(solution)/shard_map/project/pallas_call | solution.py:685
  35.0 7.0 %mix.1 = (f32[1024,768]{1,0:T(8,128)S(1)}, bf16[8,64,768]{2,1,0:T(8,128)(2,1)S(1)}) custom-call(s32[3]{0:T(128)S(1)} %pad_add_fusion.scalars, f32[1024,768]{1,0:T(8,128)S(1)} %get-tuple-element.110.refs_0_.refs_3_.refs_1_, bf16[1024,256]{1,0:T(8,128)(2,1)S(1)} %get-tuple-element.111.refs_1_.refs_8_.refs_2_, ...), custom_call_target="tpu_custom_call" | custom-call | flops 3500000000 | bytes 21000000 | tf_op jit(solution)/shard_map/mix/pallas_call | solution.py:685
  42.0 3.3 %gate.1 = (f32[1024,768]{1,0:T(8,128)S(1)}, bf16[1024,768]{1,0:T(8,128)(2,1)S(1)}, f32[8,1024]{1,0:T(8,128)S(1)}) custom-call(s32[3]{0:T(128)S(1)} %pad_add_fusion.scalars, f32[1024,768]{1,0:T(8,128)S(1)} %get-tuple-element.116.refs_0_.refs_2_, f32[1024,768]{1,0:T(8,128)S(1)} %get-tuple-element.117.refs_1_, ...), custom_call_target="tpu_custom_call" | custom-call | flops 1500000000 | bytes 9000000 | tf_op jit(solution)/shard_map/gate/pallas_call | solution.py:685
  45.3 1.7 collective-permute-start.3
  49.3 7.6 %gate_back.1 = (bf16[1024,768]{1,0:T(8,128)(2,1)S(1)}, bf16[1024,768]{1,0:T(8,128)(2,1)S(1)}, bf16[1024,768]{1,0:T(8,128)(2,1)S(1)}, f32[1024,128]{1,0:T(8,128)S...) custom-call(s32[3]{0:T(128)S(1)} %pad_add_fusion.scalars, ...), custom_call_target="tpu_custom_call" | custom-call | flops 4000000000 | bytes 24000000 | tf_op jit(solution)/shard_map/gate_back/pallas_call | solution.py:685
  61.3 2.8 %collective-permute-done.4 = bf16[768,768]{1,0:T(8,128)(2,1)S(1)} collective-permute-done((bf16[768,768]{1,0:T(8,128)(2,1)S(1)}, bf16[768,768]{1,0:T(8,128)(2,1)S(1)}, u32[]{:S(2)}, u32[]{:S(2)}) %collective-permute-start.4) | collective-permute-done | bytes 1179680 | tf_op jit(solution)/shard_map/ppermute | solution.py:722
  64.5 1.8 collective-permute-start.5
  66.5 6.8 %mix_back.4 = (bf16[1024,1152]{1,0:T(8,128)(2,1)S(1)}, f32[8,1024]{1,0:T(8,128)S(1)}, f32[8,1024]{1,0:T(8,128)S(1)}, f32[8,128]{1,0:T(8,128)S(1)}, f32[8,1024]{1,0:T(8,128)S(1)}, /*index=5*/f32[64,768]{1,0:T(8,128)S(1)}) custom-call(s32[3]{0:T(128)S(1)} %pad_add_fusion.scalars, ...), custom_call_target="tpu_custom_call", output_to_operand_aliasing={{0}: (22, {}), {1}: (23, {})} | custom-call | flops 3000000000 | bytes 18000000 | tf_op jit(solution)/shard_map/mix_back/pallas_call | solution.py:685
  73.4 6.6 %mix_back.5 = (bf16[1024,1152]{1,0:T(8,128)(2,1)S(1)}, f32[8,1024]{1,0:T(8,128)S(1)}, f32[8,1024]{1,0:T(8,128)S(1)}, f32[8,128]{1,0:T(8,128)S(1)}, f32[8,1024]{1,0:T(8,128)S(1)}, /*index=5*/f32[64,768]{1,0:T(8,128)S(1)}) custom-call(s32[3]{0:T(128)S(1)} %pad_add_fusion.scalars, ...), custom_call_target="tpu_custom_call", output_to_operand_aliasing={{0}: (22, {}), {1}: (23, {})} | custom-call | flops 3000000000 | bytes 18000000 | tf_op jit(solution)/shard_map/mix_back/pallas_call | solution.py:685
  80.1 1.6 collective-permute-start.6
  81.8 6.6 %mix_back.6 = (bf16[1024,1152]{1,0:T(8,128)(2,1)S(1)}, f32[8,1024]{1,0:T(8,128)S(1)}, f32[8,1024]{1,0:T(8,128)S(1)}, f32[8,128]{1,0:T(8,128)S(1)}, f32[8,1024]{1,0:T(8,128)S(1)}, /*index=5*/f32[64,768]{1,0:T(8,128)S(1)}) custom-call(s32[3]{0:T(128)S(1)} %pad_add_fusion.scalars, ...), custom_call_target="tpu_custom_call", output_to_operand_aliasing={{0}: (22, {}), {1}: (23, {})} | custom-call | flops 3000000000 | bytes 18000000 | tf_op jit(solution)/shard_map/mix_back/pallas_call | solution.py:685
  89.0 7.2 %mix_back.7 = (bf16[1024,1152]{1,0:T(8,128)(2,1)S(1)}, f32[8,1024]{1,0:T(8,128)S(1)}, f32[8,1024]{1,0:T(8,128)S(1)}, f32[8,128]{1,0:T(8,128)S(1)}, f32[8,1024]{1,0:T(8,128)}, /*index=5*/f32[64,768]{1,0:T(8,128)}) custom-call(s32[3]{0:T(128)S(1)} %pad_add_fusion.scalars, ...), custom_call_target="tpu_custom_call", output_to_operand_aliasing={{0}: (22, {}), {1}: (23, {})} | custom-call | flops 3000000000 | bytes 18000000 | tf_op jit(solution)/shard_map/mix_back/pallas_call | solution.py:685
  100.1 1.6 collective-permute-start.8
  101.7 2.5 %collective-permute-start.12 = (bf16[96,768]{1,0:T(8,128)(2,1)S(1)}, bf16[96,768]{1,0:T(8,128)(2,1)S(1)}, u32[]{:S(2)}, u32[]{:S(2)}) collective-permute-start(bf16[96,768]{1,0:T(8,128)(2,1)S(1)} %add_convert_fusion.10), channel_id=1, source_target_pairs={{0,16},{2,18},{4,20},{6,22},{8,24},{10,26},{12,28},{14,30},{16,0},... | collective-permute-start | bytes 442376 | tf_op jit(solution)/shard_map/ppermute | solution.py:722
  104.2 7.5 %collective-permute-done.12 = bf16[96,768]{1,0:T(8,128)(2,1)S(1)} collective-permute-done((bf16[96,768]{1,0:T(8,128)(2,1)S(1)}, bf16[96,768]{1,0:T(8,128)(2,1)S(1)}, u32[]{:S(2)}, u32[]{:S(2)}) %collective-permute-start.12) | collective-permute-done | bytes 147488 | tf_op jit(solution)/shard_map/ppermute | solution.py:722
  112.5 8.7 %collective-permute-done.13 = bf16[96,768]{1,0:T(8,128)(2,1)S(1)} collective-permute-done((bf16[96,768]{1,0:T(8,128)(2,1)S(1)}, bf16[96,768]{1,0:T(8,128)(2,1)S(1)}, u32[]{:S(2)}, u32[]{:S(2)}) %collective-permute-start.13) | collective-permute-done | bytes 147488 | tf_op jit(solution)/shard_map/ppermute | solution.py:722
  122.9 2.8 %back_oth.1 = bf16[1024,384]{1,0:T(8,128)(2,1)S(1)} custom-call(s32[3]{0:T(128)S(1)} %pad_add_fusion.scalars, bf16[1024,768]{1,0:T(8,128)(2,1)S(1)} %get-tuple-element.130.dgp, bf16[1024,1152]{1,0:T(8,128)(2,1)S(1)} %get-tuple-element.176.rest, bf16[768,768]{1,0:T(8,128)(2,1)S(1)} %get-tuple-element.106.refs_3_.w_gate, ...), custom_call_target="tpu_custom_call" | custom-call | flops 2000000000 | bytes 12000000 | tf_op jit(solution)/shard_map/back_oth/pallas_call | solution.py:702
  125.7 2.8 %back_own.1 = f32[1024,384]{1,0:T(8,128)S(1)} custom-call(s32[3]{0:T(128)S(1)} %pad_add_fusion.scalars, bf16[1024,768]{1,0:T(8,128)(2,1)S(1)} %get-tuple-element.130.dgp, bf16[1024,1152]{1,0:T(8,128)(2,1)S(1)} %get-tuple-element.176.rest, bf16[768,768]{1,0:T(8,128)(2,1)S(1)} %get-tuple-element.106.refs_3_.w_gate, ...), custom_call_target="tpu_custom_call" | custom-call | flops 2000000000 | bytes 12000000 | tf_op jit(solution)/shard_map/back_own/pallas_call | solution.py:702
  129.6 3.2 %collective-permute-done.11 = bf16[288,768]{1,0:T(8,128)(2,1)S(1)} collective-permute-done((bf16[288,768]{1,0:T(8,128)(2,1)S(1)}, bf16[288,768]{1,0:T(8,128)(2,1)S(1)}, u32[]{:S(2)}, u32[]{:S(2)}) %collective-permute-start.11) | collective-permute-done | bytes 442400 | tf_op jit(solution)/shard_map/ppermute | solution.py:722
  135.9 3.0 %collective-permute-done.14 = bf16[144,768]{1,0:T(8,128)(2,1)S(1)} collective-permute-done((bf16[144,768]{1,0:T(8,128)(2,1)S(1)}, bf16[144,768]{1,0:T(8,128)(2,1)S(1)}, u32[]{:S(2)}, u32[]{:S(2)}) %collective-permute-start.14) | collective-permute-done | bytes 221216 | tf_op jit(solution)/shard_map/ppermute | solution.py:722
  140.0 1.8 collective-permute-done.16
  141.8 5.1 %collective-permute-done.9 = bf16[1024,384]{1,0:T(8,128)(2,1)S(1)} collective-permute-done((bf16[1024,384]{1,0:T(8,128)(2,1)S(1)}, bf16[1024,384]{1,0:T(8,128)(2,1)S(1)}, u32[]{:S(2)}, u32[]{:S(2)}) %collective-permute-start.9) | collective-permute-done | bytes 786464 | tf_op jit(solution)/shard_map/ppermute | solution.py:717
  146.9 2.0 %fusion.2 = (f32[1024,384]{1,0:T(8,128)}, bf16[1024,384]{1,0:T(8,128)(2,1)}) fusion(bf16[1024,384]{1,0:T(8,128)(2,1)S(1)} %copy-done.1, f32[1024,384]{1,0:T(8,128)S(1)} %back_own.1, bf16[1024,384]{1,0:T(8,128)(2,1)S(1)} %collective-permute-done.9, bf16[1024,384]{1,0:T(8,128)(2,1)S(1)} %copy-done.3, f32[1024]{0:T(1024)S(1)} %get-tuple-element.199, ...), kind=kLoop, calls=%fused_computation.5 | loop fusion | flops 5505024 | bytes 8664576 | tf_op jit(solution)/shard_map/sub | solution.py:1107
  149.6 3.4 %collective-permute-done.17 = bf16[24,768]{1,0:T(8,128)(2,1)S(1)} collective-permute-done((bf16[24,768]{1,0:T(8,128)(2,1)S(1)}, bf16[24,768]{1,0:T(8,128)(2,1)S(1)}, u32[]{:S(2)}, u32[]{:S(2)}) %collective-permute-start.17) | collective-permute-done | bytes 36896 | tf_op jit(solution)/shard_map/ppermute | solution.py:717
  153.2 5.8 %collective-permute-done.18 = bf16[72,768]{1,0:T(8,128)(2,1)S(1)} collective-permute-done((bf16[72,768]{1,0:T(8,128)(2,1)S(1)}, bf16[72,768]{1,0:T(8,128)(2,1)S(1)}, u32[]{:S(2)}, u32[]{:S(2)}) %collective-permute-start.18) | collective-permute-done | bytes 110624 | tf_op jit(solution)/shard_map/ppermute | solution.py:722
  159.1 6.6 %collective-permute-done.19 = bf16[144,768]{1,0:T(8,128)(2,1)S(1)} collective-permute-done((bf16[144,768]{1,0:T(8,128)(2,1)S(1)}, bf16[144,768]{1,0:T(8,128)(2,1)S(1)}, u32[]{:S(2)}, u32[]{:S(2)}) %collective-permute-start.19) | collective-permute-done | bytes 221216 | tf_op jit(solution)/shard_map/ppermute | solution.py:722
  165.9 8.2 %collective-permute-done.20 = bf16[288,768]{1,0:T(8,128)(2,1)S(1)} collective-permute-done((bf16[288,768]{1,0:T(8,128)(2,1)S(1)}, bf16[288,768]{1,0:T(8,128)(2,1)S(1)}, u32[]{:S(2)}, u32[]{:S(2)}) %collective-permute-start.20) | collective-permute-done | bytes 442400 | tf_op jit(solution)/shard_map/ppermute | solution.py:722
  174.3 3.4 %collective-permute-done.22 = bf16[384,768]{1,0:T(8,128)(2,1)S(1)} collective-permute-done((bf16[384,768]{1,0:T(8,128)(2,1)S(1)}, bf16[384,768]{1,0:T(8,128)(2,1)S(1)}, u32[]{:S(2)}, u32[]{:S(2)}) %collective-permute-start.22) | collective-permute-done | bytes 589856 | tf_op jit(solution)/shard_map/ppermute | solution.py:722
  177.8 3.3 %unpack_late.1 = (f32[768,768]{1,0:T(8,128)}, f32[768,256]{1,0:T(8,128)}, f32[12,2,768]{2,1,0:T(2,128)}, f32[4,768]{1,0:T(4,128)}, f32[8,768]{1,0:T(8,128)S(1)}, /*index=5*/f32[4,256]{1,0:T(4,128)}) custom-call(s32[3]{0:T(128)S(1)} %pad_add_fusion.scalars, bf16[576,768]{1,0:T(8,128)(2,1)S(1)} %constant_dynamic-update-slice_fusion.5.first, ...), custom_call_target="tpu_custom_call" | custom-call | flops 2000000000 | bytes 12000000 | tf_op jit(solution)/shard_map/unpack_late/pallas_call | solution.py:702
  184.8 3.0 %unpack_early.1 = (f32[768,768]{1,0:T(8,128)}, f32[768,768]{1,0:T(8,128)}) custom-call(s32[3]{0:T(128)S(1)} %pad_add_fusion.scalars, bf16[768,768]{1,0:T(8,128)(2,1)S(1)} %constant_dynamic-update-slice_fusion.9.first, bf16[768,768]{1,0:T(8,128)(2,1)S(1)} %collective-permute-done.23.second), custom_call_target="tpu_custom_call" | custom-call | flops 2000000000 | bytes 12000000 | tf_op jit(solution)/shard_map/unpack_early/pallas_call | solution.py:702
  (120 shorter events, 39.9 us)
Async XLA Ops:
  1.3 17.8 %collective-permute-start.1 = (bf16[1,384]{1,0:T(2,128)(2,1)S(1)}, bf16[1,384]{1,0:T(2,128)(2,1)S(1)}, u32[]{:S(2)}, u32[]{:S(2)}) collective-permute-start(bf16[1,384]{1,0:T(2,128)(2,1)S(1)} %concatenate.56), channel_id=1, source_target_pairs={{0,1},{1,0},{2,3},{3,2},{4,5},{5,4},{6,7},{7,6},{8,9},{9,8},{10,11... | collective-permute-start | bytes 2312 | tf_op jit(solution)/shard_map/ppermute | solution.py:717
  4.3 19.2 %collective-permute-start = (bf16[1024,384]{1,0:T(8,128)(2,1)}, bf16[1024,384]{1,0:T(8,128)(2,1)S(1)}, u32[]{:S(2)}, u32[]{:S(2)}) collective-permute-start(bf16[1024,384]{1,0:T(8,128)(2,1)} %refs_0_.1), channel_id=1, source_target_pairs={{0,1},{1,0},{2,3},{3,2},{4,5},{5,4},{6,7},{7,6},{8,9},{9,8},{10,11... | collective-permute-start | bytes 2359304 | tf_op jit(solution)/shard_map/ppermute | solution.py:717
  13.8 1.3 copy-start.5
  15.1 1.3 copy-start.6
  16.4 1.3 copy-start.8
  23.5 18.5 %collective-permute-start.2 = (bf16[1024,384]{1,0:T(8,128)(2,1)S(1)}, bf16[1024,384]{1,0:T(8,128)(2,1)S(1)}, u32[]{:S(2)}, u32[]{:S(2)}) collective-permute-start(bf16[1024,384]{1,0:T(8,128)(2,1)S(1)} %copy-done.2), channel_id=1, source_target_pairs={{0,1},{1,0},{2,3},{3,2},{4,5},{5,4},{6,7},{7,6},{8,9},{9,8},{10,11... | collective-permute-start | bytes 2359304 | tf_op jit(solution)/shard_map/ppermute | solution.py:717
  45.3 4.0 %collective-permute-start.3 = (f32[8,1024]{1,0:T(8,128)S(1)}, f32[8,1024]{1,0:T(8,128)S(1)}, u32[]{:S(2)}, u32[]{:S(2)}) collective-permute-start(f32[8,1024]{1,0:T(8,128)S(1)} %get-tuple-element.121), channel_id=1, source_target_pairs={{0,1},{1,0},{2,3},{3,2},{4,5},{5,4},{6,7},{7,6},{8,9},{9,8},{10,11... | collective-permute-start | bytes 98312 | tf_op jit(solution)/shard_map/ppermute | solution.py:717
  58.4 1.5 copy-start.7
  61.3 2.9 %collective-permute-start.4 = (bf16[768,768]{1,0:T(8,128)(2,1)S(1)}, bf16[768,768]{1,0:T(8,128)(2,1)S(1)}, u32[]{:S(2)}, u32[]{:S(2)}) collective-permute-start(bf16[768,768]{1,0:T(8,128)(2,1)S(1)} %get-tuple-element.132), channel_id=1, source_target_pairs={{0,2},{2,0},{4,6},{6,4},{8,10},{10,8},{12,14},{14,12},{16,18},{18,... | collective-permute-start | bytes 3538952 | tf_op jit(solution)/shard_map/ppermute | solution.py:722
  64.5 15.5 %collective-permute-start.5 = (bf16[384,768]{1,0:T(8,128)(2,1)S(1)}, bf16[384,768]{1,0:T(8,128)(2,1)S(1)}, u32[]{:S(2)}, u32[]{:S(2)}) collective-permute-start(bf16[384,768]{1,0:T(8,128)(2,1)S(1)} %get-tuple-element.202), channel_id=1, source_target_pairs={{0,8},{2,10},{4,12},{6,14},{8,0},{10,2},{12,4},{14,6},{16,24},{18,... | collective-permute-start | bytes 1769480 | tf_op jit(solution)/shard_map/ppermute | solution.py:722
  80.0 1.8 copy-start.10
  80.1 8.8 %collective-permute-start.6 = (bf16[192,768]{1,0:T(8,128)(2,1)S(1)}, bf16[192,768]{1,0:T(8,128)(2,1)S(1)}, u32[]{:S(2)}, u32[]{:S(2)}) collective-permute-start(bf16[192,768]{1,0:T(8,128)(2,1)S(1)} %get-tuple-element.206), channel_id=1, source_target_pairs={{0,4},{2,6},{4,0},{6,2},{8,12},{10,14},{12,8},{14,10},{16,20},{18,... | collective-permute-start | bytes 884744 | tf_op jit(solution)/shard_map/ppermute | solution.py:722
  97.0 1.5 copy-start.9
  100.0 21.2 %collective-permute-start.7 = (bf16[576,768]{1,0:T(8,128)(2,1)S(1)}, bf16[576,768]{1,0:T(8,128)(2,1)S(1)}, u32[]{:S(2)}, u32[]{:S(2)}) collective-permute-start(bf16[576,768]{1,0:T(8,128)(2,1)S(1)} %get-tuple-element.171), channel_id=1, source_target_pairs={{0,2},{2,0},{4,6},{6,4},{8,10},{10,8},{12,14},{14,12},{16,18},{18,... | collective-permute-start | bytes 2654216 | tf_op jit(solution)/shard_map/ppermute | solution.py:722
  100.1 41.7 %collective-permute-start.8 = (bf16[1024,384]{1,0:T(8,128)(2,1)S(1)}, bf16[1024,384]{1,0:T(8,128)(2,1)S(1)}, u32[]{:S(2)}, u32[]{:S(2)}) collective-permute-start(bf16[1024,384]{1,0:T(8,128)(2,1)S(1)} %branch_oth.1), channel_id=1, source_target_pairs={{0,1},{1,0},{2,3},{3,2},{4,5},{5,4},{6,7},{7,6},{8,9},{9,8},{10,11... | collective-permute-start | bytes 2359304 | tf_op jit(solution)/shard_map/ppermute | solution.py:717
  101.7 10.0 %collective-permute-start.12 = (bf16[96,768]{1,0:T(8,128)(2,1)S(1)}, bf16[96,768]{1,0:T(8,128)(2,1)S(1)}, u32[]{:S(2)}, u32[]{:S(2)}) collective-permute-start(bf16[96,768]{1,0:T(8,128)(2,1)S(1)} %add_convert_fusion.10), channel_id=1, source_target_pairs={{0,16},{2,18},{4,20},{6,22},{8,24},{10,26},{12,28},{14,30},{16,0},... | collective-permute-start | bytes 442376 | tf_op jit(solution)/shard_map/ppermute | solution.py:722
  111.8 9.4 %collective-permute-start.13 = (bf16[96,768]{1,0:T(8,128)(2,1)S(1)}, bf16[96,768]{1,0:T(8,128)(2,1)S(1)}, u32[]{:S(2)}, u32[]{:S(2)}) collective-permute-start(bf16[96,768]{1,0:T(8,128)(2,1)S(1)} %add_convert_fusion.8), channel_id=1, source_target_pairs={{0,16},{2,18},{4,20},{6,22},{8,24},{10,26},{12,28},{14,30},{16,0},... | collective-permute-start | bytes 442376 | tf_op jit(solution)/shard_map/ppermute | solution.py:722
  111.9 17.7 %collective-permute-start.10 = (f32[8,128]{1,0:T(8,128)S(1)}, f32[8,128]{1,0:T(8,128)S(1)}, u32[]{:S(2)}, u32[]{:S(2)}) collective-permute-start(f32[8,128]{1,0:T(8,128)S(1)} %bitcast.26), channel_id=1, source_target_pairs={{0,1},{1,0},{2,3},{3,2},{4,5},{5,4},{6,7},{7,6},{8,9},{9,8},{10,11... | collective-permute-start | bytes 12296 | tf_op jit(solution)/shard_map/ppermute | solution.py:717
  121.4 11.4 %collective-permute-start.11 = (bf16[288,768]{1,0:T(8,128)(2,1)S(1)}, bf16[288,768]{1,0:T(8,128)(2,1)S(1)}, u32[]{:S(2)}, u32[]{:S(2)}) collective-permute-start(bf16[288,768]{1,0:T(8,128)(2,1)S(1)} %get-tuple-element.204), channel_id=1, source_target_pairs={{0,4},{2,6},{4,0},{6,2},{8,12},{10,14},{12,8},{14,10},{16,20},{18,... | collective-permute-start | bytes 1327112 | tf_op jit(solution)/shard_map/ppermute | solution.py:722
  125.7 3.4 %copy-start.1 = (bf16[1024,384]{1,0:T(8,128)(2,1)S(1)}, bf16[1024,384]{1,0:T(8,128)(2,1)}, u32[]{:S(2)}) copy-start(bf16[1024,384]{1,0:T(8,128)(2,1)} %refs_0_.1) | copy-start | bytes 2359300
  128.6 18.4 %collective-permute-start.9 = (bf16[1024,384]{1,0:T(8,128)(2,1)S(1)}, bf16[1024,384]{1,0:T(8,128)(2,1)S(1)}, u32[]{:S(2)}, u32[]{:S(2)}) collective-permute-start(bf16[1024,384]{1,0:T(8,128)(2,1)S(1)} %back_oth.1), channel_id=1, source_target_pairs={{0,1},{1,0},{2,3},{3,2},{4,5},{5,4},{6,7},{7,6},{8,9},{9,8},{10,11... | collective-permute-start | bytes 2359304 | tf_op jit(solution)/shard_map/ppermute | solution.py:717
  132.9 6.0 %collective-permute-start.14 = (bf16[144,768]{1,0:T(8,128)(2,1)S(1)}, bf16[144,768]{1,0:T(8,128)(2,1)S(1)}, u32[]{:S(2)}, u32[]{:S(2)}) collective-permute-start(bf16[144,768]{1,0:T(8,128)(2,1)S(1)} %get-tuple-element.207), channel_id=1, source_target_pairs={{0,8},{2,10},{4,12},{6,14},{8,0},{10,2},{12,4},{14,6},{16,24},{18,... | collective-permute-start | bytes 663560 | tf_op jit(solution)/shard_map/ppermute | solution.py:722
  134.5 12.4 %copy-start.3 = (bf16[1024,384]{1,0:T(8,128)(2,1)S(1)}, bf16[1024,384]{1,0:T(8,128)(2,1)}, u32[]{:S(2)}) copy-start(bf16[1024,384]{1,0:T(8,128)(2,1)} %refs_1_.1) | copy-start | bytes 2359300
  134.5 7.3 %collective-permute-start.16 = (bf16[192,768]{1,0:T(8,128)(2,1)S(1)}, bf16[192,768]{1,0:T(8,128)(2,1)S(1)}, u32[]{:S(2)}, u32[]{:S(2)}) collective-permute-start(bf16[192,768]{1,0:T(8,128)(2,1)S(1)} %pad_maximum_fusion), channel_id=1, source_target_pairs={{0,4},{2,6},{4,0},{6,2},{8,12},{10,14},{12,8},{14,10},{16,20},{18,... | collective-permute-start | bytes 884744 | tf_op jit(solution)/shard_map/ppermute | solution.py:722
  138.9 10.0 %collective-permute-start.15 = (bf16[72,768]{1,0:T(8,128)(2,1)S(1)}, bf16[72,768]{1,0:T(8,128)(2,1)S(1)}, u32[]{:S(2)}, u32[]{:S(2)}) collective-permute-start(bf16[72,768]{1,0:T(8,128)(2,1)S(1)} %add_convert_fusion.12), channel_id=1, source_target_pairs={{0,16},{2,18},{4,20},{6,22},{8,24},{10,26},{12,28},{14,30},{16,0},... | collective-permute-start | bytes 331784 | tf_op jit(solution)/shard_map/ppermute | solution.py:722
  149.0 4.0 %collective-permute-start.17 = (bf16[24,768]{1,0:T(8,128)(2,1)S(1)}, bf16[24,768]{1,0:T(8,128)(2,1)S(1)}, u32[]{:S(2)}, u32[]{:S(2)}) collective-permute-start(bf16[24,768]{1,0:T(8,128)(2,1)S(1)} %slice.166), channel_id=1, source_target_pairs={{0,1},{1,0},{2,3},{3,2},{4,5},{5,4},{6,7},{7,6},{8,9},{9,8},{10,11... | collective-permute-start | bytes 110600 | tf_op jit(solution)/shard_map/ppermute | solution.py:717
  153.1 5.8 %collective-permute-start.18 = (bf16[72,768]{1,0:T(8,128)(2,1)S(1)}, bf16[72,768]{1,0:T(8,128)(2,1)S(1)}, u32[]{:S(2)}, u32[]{:S(2)}) collective-permute-start(bf16[72,768]{1,0:T(8,128)(2,1)S(1)} %pad_maximum_fusion.2), channel_id=1, source_target_pairs={{0,16},{2,18},{4,20},{6,22},{8,24},{10,26},{12,28},{14,30},{16,0},... | collective-permute-start | bytes 331784 | tf_op jit(solution)/shard_map/ppermute | solution.py:722
  159.0 6.7 %collective-permute-start.19 = (bf16[144,768]{1,0:T(8,128)(2,1)S(1)}, bf16[144,768]{1,0:T(8,128)(2,1)S(1)}, u32[]{:S(2)}, u32[]{:S(2)}) collective-permute-start(bf16[144,768]{1,0:T(8,128)(2,1)S(1)} %pad_maximum_fusion.1), channel_id=1, source_target_pairs={{0,8},{2,10},{4,12},{6,14},{8,0},{10,2},{12,4},{14,6},{16,24},{18,... | collective-permute-start | bytes 663560 | tf_op jit(solution)/shard_map/ppermute | solution.py:722
  165.7 8.4 %collective-permute-start.20 = (bf16[288,768]{1,0:T(8,128)(2,1)S(1)}, bf16[288,768]{1,0:T(8,128)(2,1)S(1)}, u32[]{:S(2)}, u32[]{:S(2)}) collective-permute-start(bf16[288,768]{1,0:T(8,128)(2,1)S(1)} %get-tuple-element.211), channel_id=1, source_target_pairs={{0,4},{2,6},{4,0},{6,2},{8,12},{10,14},{12,8},{14,10},{16,20},{18,... | collective-permute-start | bytes 1327112 | tf_op jit(solution)/shard_map/ppermute | solution.py:722
  165.9 11.7 %collective-permute-start.22 = (bf16[384,768]{1,0:T(8,128)(2,1)S(1)}, bf16[384,768]{1,0:T(8,128)(2,1)S(1)}, u32[]{:S(2)}, u32[]{:S(2)}) collective-permute-start(bf16[384,768]{1,0:T(8,128)(2,1)S(1)} %constant_dynamic-update-slice_fusion), channel_id=1, source_target_pairs={{0,8},{2,10},{4,12},{6,14},{8,0},{10,2},{12,4},{14,6},{16,24},{18,... | collective-permute-start | bytes 1769480 | tf_op jit(solution)/shard_map/ppermute | solution.py:722
  174.1 3.6 %collective-permute-start.21 = (bf16[576,768]{1,0:T(8,128)(2,1)S(1)}, bf16[576,768]{1,0:T(8,128)(2,1)}, u32[]{:S(2)}, u32[]{:S(2)}) collective-permute-start(bf16[576,768]{1,0:T(8,128)(2,1)S(1)} %constant_dynamic-update-slice_fusion.5.first), channel_id=1, source_target_pairs={{0,2},{2,0},{4,6},{6,4},{8,10},{10,8},{12,14},{14,12},{16,18},{18,... | collective-permute-start | bytes 2654216 | tf_op jit(solution)/shard_map/ppermute | solution.py:722
  177.7 7.2 %collective-permute-start.23 = (bf16[768,768]{1,0:T(8,128)(2,1)S(1)}, bf16[768,768]{1,0:T(8,128)(2,1)S(1)}, u32[]{:S(2)}, u32[]{:S(2)}) collective-permute-start(bf16[768,768]{1,0:T(8,128)(2,1)S(1)} %constant_dynamic-update-slice_fusion.9.first), channel_id=1, source_target_pairs={{0,2},{2,0},{4,6},{6,4},{8,10},{10,8},{12,14},{14,12},{16,18},{18,... | collective-permute-start | bytes 3538952 | tf_op jit(solution)/shard_map/ppermute | solution.py:722
  (3 other events, 3.3 us)
where the time goes:
time: 189 us; the launch traced here: 188 us
  Pallas kernels  75.7 us (40%)
  waiting for transfers between devices  65 us (34%)
  starting transfers between devices  19.1 us (10%)
  local copies, waits for them, and re-layouts  14.6 us (8%)
  other arithmetic  6.43 us (3%)
  matrix products  5.21 us (3%)
    pallas_call x8, Pallas kernels, call(): pl.pallas_call(looped, out_shape=[pltpu.VMEM(o.shape, o.dtype) for o in o...  56.3 us
    ppermute x16, waiting for transfers between devices, swap_dp(): return lax.ppermute(x, 'dp', [(i, i ^ 1 << bit) for i in range(size)])  51.4 us
    pallas_call x8, Pallas kernels, whole(): pl.pallas_call(kernel, out_shape=[pltpu.VMEM(o.shape, o.dtype) if in_vmem...  17.9 us
    ppermute x8, waiting for transfers between devices, swap_mp(): return lax.ppermute(x, 'mp', [(0, 1), (1, 0)])  13.6 us
    ppermute x16, starting transfers between devices, swap_dp(): return lax.ppermute(x, 'dp', [(i, i ^ 1 << bit) for i in range(size)])  10.7 us
    ppermute x8, starting transfers between devices, swap_mp(): return lax.ppermute(x, 'mp', [(0, 1), (1, 0)])  8.38 us
    unnamed x27, local copies, waits for them, and re-layouts  7.96 us
    dot_general x4, matrix products, mm_tn(): lax.dot_general(a, b, (((0,), (0,)), ((), ())), preferred_element_type=F32)  5.21 us
  transfers between devices with their start and end apart: 24, of which 15 were waited for; matrix products, arithmetic and copies ran while one was open for 7% of the time, Pallas kernels for 28%

commit v1 on v0

--- a/solution.py
+++ b/solution.py
@@ -549,7 +549,7 @@
 
 
 def pack_late_kernel(
-    scalars, inner, state, w_inner, w_state_t, gain, gain_part, gconv, ghead, small,
+    scalars, inner, state, w_inner, w_state_t, gain, gain_part, gconv, ghead, small, gather,
     keep_ref, send_ref, misc, *, order, heads, state_width,
 ):
     model, width = w_inner.shape
@@ -571,8 +571,10 @@
     for k in range(5):
         put_single(at + k, gconv[k : k + 1, 0:width])
     put_single(at + 5, small[0:1, :])
-    put_single(at + 6, small[1:2, :])
-    at = ((at + 7) // 2) * 8 + (at + 7) % 2
+    hi, lo = split_two(eight(small[1:2, :]))
+    skip = mm(hi, gather[0:width, :]) + mm(lo, gather[0:width, :])
+    at = ((at + 6) // 2) * 8 + (at + 6) % 2
+    misc[at : at + 1, 2 * LANES : 3 * LANES] = skip[0:1]
     misc[at : at + 1, 0:LANES] = ghead[0:1, :]
     misc[at : at + 1, LANES : 2 * LANES] = ghead[1:2, :]
     fit = model // state_width
@@ -599,8 +601,8 @@
 
 
 def unpack_late_kernel(
-    scalars, first, second, inner_ref, state_ref, step_ref, convi_ref, singles_ref, convs_ref,
-    state, misc, *, order, heads,
+    scalars, first, second, inner_ref, state_ref, step_ref, convi_ref, convi_b_ref, convs_ref, convs_b_ref,
+    gg_ref, bias_ref, decay_ref, skip_ref, gain_ref, state, misc, *, order, heads,
 ):
     model = inner_ref.shape[0]
     state_width = state_ref.shape[1]
@@ -628,21 +630,24 @@
     at = 2 * heads
     for k in range(4):
         convi_ref[k : k + 1, :] = single(at + k)
-    singles_ref[0:1, :] = single(at + 4)
-    singles_ref[1:2, :] = single(at + 5)
-    singles_ref[2:3, :] = single(at + 6)
-    singles_ref[3:4, :] = single(at + 7)
+    convi_b_ref[...] = single(at + 4)
+    gg_ref[...] = single(at + 5)
+    head_row = single(at + 6)
+    for d in range(2):
+        decay_ref[d : d + 1, :] = head_row[:, d * heads : (d + 1) * heads]
+        bias_ref[d : d + 1, :] = head_row[:, LANES + d * heads : LANES + (d + 1) * heads]
+    skip_ref[...] = head_row[:, 2 * LANES : 2 * LANES + heads]
     fit = model // state_width
-    at = (-(-5 // fit)) * 8 + 4
-    singles_ref[4:5, :] = misc[at : at + 1, :]
-    singles_ref[5:8, :] = jnp.zeros((3, model), F32)
     for k in range(5):
         at = (k // fit) * 8 + 4
         lanes = slice((k % fit) * state_width, (k % fit + 1) * state_width)
-        if k < 4:
-            convs_ref[k : k + 1, :] = misc[at : at + 1, lanes]
-        else:
-            singles_ref[5:6, 0:state_width] = misc[at : at + 1, lanes]
+        out, row = (convs_ref, k) if k < 4 else (convs_b_ref, 0)
+        out[row : row + 1, :] = misc[at : at + 1, lanes]
+    at = (-(-5 // fit)) * 8 + 4
+    half = model // 2
+    gain_ref[...] = jnp.where(
+        scalars[1] == 0, misc[at : at + 1, :half], misc[at : at + 1, half:]
+    )
 
 
 def place(i, top):
@@ -984,7 +989,7 @@
             aliases={len(ins) - 2: 0, len(ins) - 1: 1},
         )
 
-    order_a, order_b = (0, 2, 1, 3), (0, 1, 2, 3)
+    order_a, order_b = (0, 1, 2, 3), (0, 1, 2, 3)
     grad_out = mm_tn(gz, dbr).astype(BF16)
     grad_gate = mm_tn(normed, dgp).astype(BF16)
     keep, send, gain_part = whole(
@@ -1030,8 +1035,13 @@
     for k in range(parts):
         outs = back_part((parts - k) * count - 1, count, g, state)
         rest, rd_rest, gconv, ghead, ext_carry, carry = outs
+        if k == 1:
+            sent, carry, branch_got = lax.optimization_barrier((sent, carry, branch_got))
+        elif k == 2:
+            sent, carry = lax.optimization_barrier((sent, carry))
+        elif k == 3:
+            sent, rest = lax.optimization_barrier((sent, rest))
         if k > 0:
-            sent, carry = lax.optimization_barrier((sent, carry))
             h = keep.shape[0] // 2
             if k < 3:
                 keep, send = add_low(keep[:h], sent[:h]), add_low(keep[h:], sent[h:])
@@ -1039,6 +1049,7 @@
                 sent = swap_dp(send, order_a[k + 1])
             else:
                 x = rest_of_dp(add_low(keep, sent))
+                sent = swap_dp(x, order_a[3])
         state = (ext_carry, carry, gconv, ghead, rest, rd_rest)
 
     grad_inner = mm_tn(normed, rest[:, :width]).astype(BF16)
@@ -1046,7 +1057,8 @@
     keep, send = whole(
         partial(pack_late_kernel, order=order_b, heads=heads, state_width=state_width),
         (
-            scalars, grad_inner, grad_state, proj_inner, w_state_t, gain, gain_part, gconv, ghead, small
+            scalars, grad_inner, grad_state, proj_inner, w_state_t, gain, gain_part, gconv, ghead,
+            small, gather,
         ),
         [low(LATE_ROWS * SHARDS // 2, model), low(LATE_ROWS * SHARDS // 2, model)],
         [pltpu.VMEM((8 * SHARDS, model), F32)],
@@ -1054,48 +1066,50 @@
         3,
     )
 
-    keep, send = halve(keep, send, order_b[0])
-    rest, gz_late, tokens_late, oth_late = lax.optimization_barrier((rest, gz, tokens, oth_tokens, send))[:4]
-    back_args = (scalars, dgp, rest, gate_v, inner_v, state_v, step_weight)
-
     def halve_with(keep, send, bit, *work):
         got = after(swap_dp(send, bit), *work)
         h = keep.shape[0] // 2
         return add_low(keep[:h], got[:h]), add_low(keep[h:], got[h:])
 
+    back_args = (scalars, dgp, after(rest, send), gate_v, inner_v, state_v, step_weight)
     dn_oth = whole(
         partial(back_project_kernel, other=True), back_args, [low(rows, width_own)], [], "back_oth", 4
     )[0]
     rd_part = rd_gate[0] + rd_rest[0]
-    sent = swap_dp(x, order_a[3])
+    keep, send = halve_with(keep, send, order_b[0], dn_oth, rd_part)
     x = jnp.concatenate([x, sent])
-    keep, send = halve_with(keep, send, order_b[1], dn_oth, rd_part, x)
+    send, x = lax.optimization_barrier((send, x))
     dn_got = swap_mp(dn_oth)
     oth_rd = swap_mp(rd_part.reshape(8, rows // 8)).reshape(rows)
+
+    sent = swap_dp(x, order_a[2])
     dn_own = whole(
         partial(back_project_kernel, other=False), back_args, [full(rows, width_own)], [], "back_own", 4
     )[0]
-    x = after(x, send)
-    sent = swap_dp(x, order_a[2])
-    keep, send = halve_with(keep, send, order_b[2], dn_own)
+    keep, send = halve_with(keep, send, order_b[1], dn_own)
+    x = jnp.concatenate([x, sent])
+    send, x, gz_late, tokens_late, oth_late = lax.optimization_barrier((send, x, gz, tokens, oth_tokens))
+
+    sent = swap_dp(x, order_a[1])
+    branch_own = whole(
+        partial(branch_kernel, other=False), (scalars, gz_late, out_v), [full(rows, width_own)], [], "branch_own", 3
+    )[0]
+    keep, send = halve_with(keep, send, order_b[2], branch_own, dn_got)
 
     seq_mask = (jnp.arange(rows) < lengths[0]).astype(F32)[:, None]
     gate_inv = lax.rsqrt(sums[0] / inner_width + EPSILON)[:, None]
     tokens_f = tokens_late.astype(F32)
-    branch_own = whole(
-        partial(branch_kernel, other=False), (scalars, gz_late, out_v), [full(rows, width_own)], [], "branch_own", 3
-    )[0]
     block_out = (tokens_f + seq_mask * gate_inv * (branch_own + branch_got.astype(F32))).astype(BF16)
-    x = jnp.concatenate([x, sent])
-    z = rest_of_dp(add_low(keep, after(swap_dp(send, order_b[3]), block_out, x)))
+    z = rest_of_dp(add_low(keep, after(swap_dp(send, order_b[3]), block_out)))
     part = model // SHARDS
     tail = z[part:]
     tail_row = lax.broadcasted_iota(jnp.int32, (LATE_ROWS - part, 1), 0)
     alone = (tail_row >= LATE_ROWS - part - 8) & (tail_row < LATE_ROWS - part - 4)
     tail_f = tail.astype(F32)
     tail = jnp.where(alone, tail_f, tail_f + swap_mp(tail).astype(F32)).astype(BF16)
-    z = jnp.concatenate([z[:part], tail])
-    z = after(z, dn_got)
+    x = jnp.concatenate([x, sent])
+    z, x = lax.optimization_barrier((jnp.concatenate([z[:part], tail]), x))
+    sent = swap_dp(x, order_a[0])
 
     oth_f = oth_late.astype(F32)
     square = jnp.sum(tokens_f * tokens_f, axis=1, keepdims=True) + jnp.sum(
@@ -1109,21 +1123,32 @@
         - tokens_f * (inv * inv * ((rd_part + oth_rd)[:, None] / model))
     )
 
-    z = jnp.concatenate([z, swap_dp(z, order_b[3])])
-    z = jnp.concatenate([z, after(swap_dp(z, order_b[2]), grad_tokens)])
-    x = after(x, z)
-    x = jnp.concatenate([x, swap_dp(x, order_a[1])])
+    z = jnp.concatenate([z, after(swap_dp(z, order_b[3]), grad_tokens)])
     grad_proj_out, grad_proj_gate = whole(
         partial(unpack_early_kernel, order=order_a),
-        (scalars, x, swap_dp(x, order_a[0])),
+        (scalars, x, after(sent, z)),
         [full(width, model), full(model, width)],
         [],
         "unpack_early",
         4,
         in_vmem=False,
     )
+    z = jnp.concatenate([z, after(swap_dp(z, order_b[2]), grad_proj_out)])
     z = jnp.concatenate([z, swap_dp(z, order_b[1])])
-    grad_proj_inner, grad_proj_state, step, grad_conv_inner, singles, grad_conv_state = whole(
+    (
+        grad_proj_inner,
+        grad_proj_state,
+        step,
+        grad_conv_inner,
+        grad_conv_inner_bias,
+        grad_conv_state,
+        grad_conv_state_bias,
+        grad_gate_gain,
+        grad_step_bias,
+        grad_decay_log,
+        grad_skip,
+        grad_norm_gain,
+    ) = whole(
         partial(unpack_late_kernel, order=order_b, heads=heads),
         (scalars, z, swap_dp(z, order_b[0])),
         [
@@ -1131,35 +1156,36 @@
             full(model, state_width),
             full(heads, 2, model),
             full(4, width),
-            full(8, model),
+            full(1, width),
             full(4, state_width),
+            full(1, state_width),
+            full(1, width),
+            full(2, heads),
+            full(2, heads),
+            full(1, heads),
+            full(1, width_own),
         ],
         [pltpu.VMEM((state_width, model), F32), pltpu.VMEM((8 * SHARDS, model), F32)],
         "unpack_late",
         4,
         in_vmem=False,
     )
-    grad_norm_gain = lax.dynamic_slice_in_dim(singles[4], rank * width_own, width_own, 0)
-    grad_skip = jnp.sum(singles[2].reshape(heads, head_dim), axis=1)
-    grad_decay_log = singles[3, : 2 * heads].reshape(2, heads)
-    grad_step_bias = singles[3, LANES : LANES + 2 * heads].reshape(2, heads)
-
     return (
         block_out,
         grad_tokens,
-        grad_norm_gain,
+        grad_norm_gain[0],
         grad_proj_gate,
         grad_proj_inner,
         grad_proj_state,
         step.transpose(2, 1, 0),
         grad_conv_inner,
-        singles[0],
+        grad_conv_inner_bias[0],
         grad_conv_state,
-        singles[5, :state_width],
+        grad_conv_state_bias[0],
         grad_step_bias,
         grad_decay_log,
-        grad_skip,
-        singles[1],
+        grad_skip[0],
+        grad_gate_gain[0],
         grad_proj_out,
     )
 

time: 189 us -> 181 us (0.958)
  waiting for transfers between devices: 65 us -> 53.7 us
  starting transfers between devices: 19.1 us -> 25.6 us
  local copies, waits for them, and re-layouts: 14.6 us -> 11.3 us
    ppermute x16, waiting for transfers between devices: 51.4 us -> 39.1 us  [swap_dp(): return lax.ppermute(x, 'dp', [(i, i ^ 1 << bit) for i in range(size)])]
    ppermute x16, starting transfers between devices: 10.7 us -> 16.1 us  [swap_dp(): return lax.ppermute(x, 'dp', [(i, i ^ 1 << bit) for i in range(size)])]
    unnamed x27 -> x29, local copies, waits for them, and re-layouts: 7.96 us -> 7.91 us
  transfers between devices with their start and end apart: 24 -> 24, of which waited for: 15 -> 14; matrix products, arithmetic and copies ran while one was open for 7% -> 5% of each run, Pallas kernels for 28% -> 32%
where the time goes in v1:
time: 181 us
  Pallas kernels  75.3 us (42%)
  waiting for transfers between devices  53.7 us (30%)
  starting transfers between devices  25.6 us (14%)
  local copies, waits for them, and re-layouts  11.3 us (6%)
  other arithmetic  7.78 us (4%)
  matrix products  5.2 us (3%)
    pallas_call x8, Pallas kernels, call(): pl.pallas_call(looped, out_shape=[pltpu.VMEM(o.shape, o.dtype) for o in o...  56.5 us
    ppermute x16, waiting for transfers between devices, swap_dp(): return lax.ppermute(x, 'dp', [(i, i ^ 1 << bit) for i in range(size)])  39.1 us
    pallas_call x8, Pallas kernels, whole(): pl.pallas_call(kernel, out_shape=[pltpu.VMEM(o.shape, o.dtype) if in_vmem...  17.3 us
    ppermute x16, starting transfers between devices, swap_dp(): return lax.ppermute(x, 'dp', [(i, i ^ 1 << bit) for i in range(size)])  16.1 us
    ppermute x8, waiting for transfers between devices, swap_mp(): return lax.ppermute(x, 'mp', [(0, 1), (1, 0)])  14.6 us
    ppermute x8, starting transfers between devices, swap_mp(): return lax.ppermute(x, 'mp', [(0, 1), (1, 0)])  9.44 us
    unnamed x29, local copies, waits for them, and re-layouts  7.91 us
    dot_general x4, matrix products, mm_tn(): lax.dot_general(a, b, (((0,), (0,)), ((), ())), preferred_element_type=F32)  5.2 us
  transfers between devices with their start and end apart: 24, of which 14 were waited for; matrix products, arithmetic and copies ran while one was open for 5% of the time, Pallas kernels for 32%

profile of v1, /device:TPU:0, one launch (start us, length us, event | category | flops | bytes accessed | tf_op | source)
XLA Modules:
  0.0 180.6 jit_solution(9947587904642875538)
XLA Ops:
  1.3 3.0 %collective-permute-start.1 = (bf16[1,384]{1,0:T(2,128)(2,1)S(1)}, bf16[1,384]{1,0:T(2,128)(2,1)S(1)}, u32[]{:S(2)}, u32[]{:S(2)}) collective-permute-start(bf16[1,384]{1,0:T(2,128)(2,1)S(1)} %concatenate.56), channel_id=1, source_target_pairs={{0,1},{1,0},{2,3},{3,2},{4,5},{5,4},{6,7},{7,6},{8,9},{9,8},{10,11... | collective-permute-start | bytes 2312 | tf_op jit(solution)/shard_map/ppermute | solution.py:722
  19.2 4.3 %collective-permute-done.refs_1_ = bf16[1024,384]{1,0:T(8,128)(2,1)S(1)} collective-permute-done((bf16[1024,384]{1,0:T(8,128)(2,1)}, bf16[1024,384]{1,0:T(8,128)(2,1)S(1)}, u32[]{:S(2)}, u32[]{:S(2)}) %collective-permute-start) | collective-permute-done | bytes 786464 | tf_op jit(solution)/shard_map/ppermute | solution.py:722
  23.8 11.1 %project.1 = (bf16[1024,768]{1,0:T(8,128)(2,1)S(1)}, f32[1024,768]{1,0:T(8,128)S(1)}, bf16[1024,1024]{1,0:T(8,128)(2,1)S(1)}, bf16[1024,1024]{1,0:T(8,128)(2,1)S...) custom-call(s32[3]{0:T(128)S(1)} %pad_add_fusion.scalars, ...), custom_call_target="tpu_custom_call" | custom-call | flops 6000000000 | bytes 36000000 | tf_op jit(solution)/shard_map/project/pallas_call | solution.py:690
  35.0 7.0 %mix.1 = (f32[1024,768]{1,0:T(8,128)S(1)}, bf16[8,64,768]{2,1,0:T(8,128)(2,1)S(1)}) custom-call(s32[3]{0:T(128)S(1)} %pad_add_fusion.scalars, f32[1024,768]{1,0:T(8,128)S(1)} %get-tuple-element.126.refs_0_.refs_3_.refs_1_, bf16[1024,256]{1,0:T(8,128)(2,1)S(1)} %get-tuple-element.127.refs_1_.refs_8_.refs_2_, ...), custom_call_target="tpu_custom_call" | custom-call | flops 3500000000 | bytes 21000000 | tf_op jit(solution)/shard_map/mix/pallas_call | solution.py:690
  42.1 3.3 %gate.1 = (f32[1024,768]{1,0:T(8,128)S(1)}, bf16[1024,768]{1,0:T(8,128)(2,1)S(1)}, f32[8,1024]{1,0:T(8,128)S(1)}) custom-call(s32[3]{0:T(128)S(1)} %pad_add_fusion.scalars, f32[1024,768]{1,0:T(8,128)S(1)} %get-tuple-element.132.refs_0_.refs_2_, f32[1024,768]{1,0:T(8,128)S(1)} %get-tuple-element.133.refs_1_, ...), custom_call_target="tpu_custom_call" | custom-call | flops 1500000000 | bytes 9000000 | tf_op jit(solution)/shard_map/gate/pallas_call | solution.py:690
  45.3 1.7 collective-permute-start.3
  49.3 7.8 %gate_back.1 = (bf16[1024,768]{1,0:T(8,128)(2,1)S(1)}, bf16[1024,768]{1,0:T(8,128)(2,1)S(1)}, bf16[1024,768]{1,0:T(8,128)(2,1)S(1)}, f32[1024,128]{1,0:T(8,128)S...) custom-call(s32[3]{0:T(128)S(1)} %pad_add_fusion.scalars, ...), custom_call_target="tpu_custom_call" | custom-call | flops 4000000000 | bytes 24000000 | tf_op jit(solution)/shard_map/gate_back/pallas_call | solution.py:690
  61.6 1.8 collective-permute-start.6
  64.7 1.7 collective-permute-start.5
  66.7 6.7 %mix_back.4 = (bf16[1024,1152]{1,0:T(8,128)(2,1)S(1)}, f32[8,1024]{1,0:T(8,128)S(1)}, f32[8,1024]{1,0:T(8,128)S(1)}, f32[8,128]{1,0:T(8,128)S(1)}, f32[8,1024]{1,0:T(8,128)S(1)}, /*index=5*/f32[64,768]{1,0:T(8,128)S(1)}) custom-call(s32[3]{0:T(128)S(1)} %pad_add_fusion.scalars, ...), custom_call_target="tpu_custom_call", output_to_operand_aliasing={{0}: (22, {}), {1}: (23, {})} | custom-call | flops 3000000000 | bytes 18000000 | tf_op jit(solution)/shard_map/mix_back/pallas_call | solution.py:690
  73.3 6.6 %mix_back.5 = (bf16[1024,1152]{1,0:T(8,128)(2,1)S(1)}, f32[8,1024]{1,0:T(8,128)S(1)}, f32[8,1024]{1,0:T(8,128)S(1)}, f32[8,128]{1,0:T(8,128)S(1)}, f32[8,1024]{1,0:T(8,128)S(1)}, /*index=5*/f32[64,768]{1,0:T(8,128)S(1)}) custom-call(s32[3]{0:T(128)S(1)} %pad_add_fusion.scalars, ...), custom_call_target="tpu_custom_call", output_to_operand_aliasing={{0}: (22, {}), {1}: (23, {})} | custom-call | flops 3000000000 | bytes 18000000 | tf_op jit(solution)/shard_map/mix_back/pallas_call | solution.py:690
  81.7 1.8 %collective-permute-start.7 = (bf16[192,768]{1,0:T(8,128)(2,1)S(1)}, bf16[192,768]{1,0:T(8,128)(2,1)S(1)}, u32[]{:S(2)}, u32[]{:S(2)}) collective-permute-start(bf16[192,768]{1,0:T(8,128)(2,1)S(1)} %get-tuple-element.230), channel_id=1, source_target_pairs={{0,8},{2,10},{4,12},{6,14},{8,0},{10,2},{12,4},{14,6},{16,24},{18,... | collective-permute-start | bytes 884744 | tf_op jit(solution)/shard_map/ppermute | solution.py:727
  83.5 6.8 %mix_back.6 = (bf16[1024,1152]{1,0:T(8,128)(2,1)S(1)}, f32[8,1024]{1,0:T(8,128)S(1)}, f32[8,1024]{1,0:T(8,128)S(1)}, f32[8,128]{1,0:T(8,128)S(1)}, f32[8,1024]{1,0:T(8,128)S(1)}, /*index=5*/f32[64,768]{1,0:T(8,128)S(1)}) custom-call(s32[3]{0:T(128)S(1)} %pad_add_fusion.scalars, ...), custom_call_target="tpu_custom_call", output_to_operand_aliasing={{0}: (22, {}), {1}: (23, {})} | custom-call | flops 3000000000 | bytes 18000000 | tf_op jit(solution)/shard_map/mix_back/pallas_call | solution.py:690
  90.4 2.8 %collective-permute-start.8 = (bf16[96,768]{1,0:T(8,128)(2,1)S(1)}, bf16[96,768]{1,0:T(8,128)(2,1)S(1)}, u32[]{:S(2)}, u32[]{:S(2)}) collective-permute-start(bf16[96,768]{1,0:T(8,128)(2,1)S(1)} %add_convert_fusion.10), channel_id=1, source_target_pairs={{0,16},{2,18},{4,20},{6,22},{8,24},{10,26},{12,28},{14,30},{16,0},... | collective-permute-start | bytes 442376 | tf_op jit(solution)/shard_map/ppermute | solution.py:727
  93.2 7.1 %mix_back.7 = (bf16[1024,1152]{1,0:T(8,128)(2,1)S(1)}, f32[8,1024]{1,0:T(8,128)S(1)}, f32[8,1024]{1,0:T(8,128)S(1)}, f32[8,128]{1,0:T(8,128)S(1)}, f32[8,1024]{1,0:T(8,128)}, /*index=5*/f32[64,768]{1,0:T(8,128)}) custom-call(s32[3]{0:T(128)S(1)} %pad_add_fusion.scalars, ...), custom_call_target="tpu_custom_call", output_to_operand_aliasing={{0}: (22, {}), {1}: (23, {})} | custom-call | flops 3000000000 | bytes 18000000 | tf_op jit(solution)/shard_map/mix_back/pallas_call | solution.py:690
  104.7 2.8 %back_oth.1 = bf16[1024,384]{1,0:T(8,128)(2,1)S(1)} custom-call(s32[3]{0:T(128)S(1)} %pad_add_fusion.scalars, bf16[1024,768]{1,0:T(8,128)(2,1)S(1)} %get-tuple-element.144.dgp, bf16[1024,1152]{1,0:T(8,128)(2,1)S(1)} %get-tuple-element.189.rest, bf16[768,768]{1,0:T(8,128)(2,1)S(1)} %get-tuple-element.121.refs_3_.w_gate, ...), custom_call_target="tpu_custom_call" | custom-call | flops 2000000000 | bytes 12000000 | tf_op jit(solution)/shard_map/back_oth/pallas_call | solution.py:707
  107.5 7.3 %collective-permute-done.10 = bf16[96,768]{1,0:T(8,128)(2,1)S(1)} collective-permute-done((bf16[96,768]{1,0:T(8,128)(2,1)S(1)}, bf16[96,768]{1,0:T(8,128)(2,1)S(1)}, u32[]{:S(2)}, u32[]{:S(2)}) %collective-permute-start.10) | collective-permute-done | bytes 147488 | tf_op jit(solution)/shard_map/ppermute | solution.py:727
  118.7 2.8 %back_own.1 = f32[1024,384]{1,0:T(8,128)S(1)} custom-call(s32[3]{0:T(128)S(1)} %pad_add_fusion.scalars, bf16[1024,768]{1,0:T(8,128)(2,1)S(1)} %get-tuple-element.144.dgp, bf16[1024,1152]{1,0:T(8,128)(2,1)S(1)} %get-tuple-element.189.rest, bf16[768,768]{1,0:T(8,128)(2,1)S(1)} %get-tuple-element.121.refs_3_.w_gate, ...), custom_call_target="tpu_custom_call" | custom-call | flops 2000000000 | bytes 12000000 | tf_op jit(solution)/shard_map/back_own/pallas_call | solution.py:707
  121.5 2.2 %collective-permute-done.12 = bf16[192,768]{1,0:T(8,128)(2,1)S(1)} collective-permute-done((bf16[192,768]{1,0:T(8,128)(2,1)S(1)}, bf16[192,768]{1,0:T(8,128)(2,1)S(1)}, u32[]{:S(2)}, u32[]{:S(2)}) %collective-permute-start.12) | collective-permute-done | bytes 294944 | tf_op jit(solution)/shard_map/ppermute | solution.py:727
  123.7 3.2 %collective-permute-done.11 = bf16[288,768]{1,0:T(8,128)(2,1)S(1)} collective-permute-done((bf16[288,768]{1,0:T(8,128)(2,1)S(1)}, bf16[288,768]{1,0:T(8,128)(2,1)S(1)}, u32[]{:S(2)}, u32[]{:S(2)}) %collective-permute-start.11) | collective-permute-done | bytes 442400 | tf_op jit(solution)/shard_map/ppermute | solution.py:727
  132.3 4.5 %collective-permute-done.13 = bf16[1024,384]{1,0:T(8,128)(2,1)S(1)} collective-permute-done((bf16[1024,384]{1,0:T(8,128)(2,1)S(1)}, bf16[1024,384]{1,0:T(8,128)(2,1)S(1)}, u32[]{:S(2)}, u32[]{:S(2)}) %collective-permute-start.13) | collective-permute-done | bytes 786464 | tf_op jit(solution)/shard_map/ppermute | solution.py:722
  136.9 1.8 %collective-permute-start.16 = (bf16[72,768]{1,0:T(8,128)(2,1)S(1)}, bf16[72,768]{1,0:T(8,128)(2,1)S(1)}, u32[]{:S(2)}, u32[]{:S(2)}) collective-permute-start(bf16[72,768]{1,0:T(8,128)(2,1)S(1)} %add_convert_fusion.12), channel_id=1, source_target_pairs={{0,16},{2,18},{4,20},{6,22},{8,24},{10,26},{12,28},{14,30},{16,0},... | collective-permute-start | bytes 331784 | tf_op jit(solution)/shard_map/ppermute | solution.py:727
  138.7 2.0 %fusion.2 = (f32[1024,384]{1,0:T(8,128)}, bf16[1024,384]{1,0:T(8,128)(2,1)}) fusion(bf16[1024,384]{1,0:T(8,128)(2,1)S(1)} %copy-done.1, f32[1024,384]{1,0:T(8,128)S(1)} %back_own.1, bf16[1024,384]{1,0:T(8,128)(2,1)S(1)} %collective-permute-done.13, bf16[1024,384]{1,0:T(8,128)(2,1)S(1)} %copy-done.3, f32[1024]{0:T(1024)S(1)} %get-tuple-element.224, ...), kind=kLoop, calls=%fused_computation.5 | loop fusion | flops 5505024 | bytes 8664576 | tf_op jit(solution)/shard_map/sub | solution.py:1121
  140.7 1.9 %collective-permute-done.16 = bf16[72,768]{1,0:T(8,128)(2,1)S(1)} collective-permute-done((bf16[72,768]{1,0:T(8,128)(2,1)S(1)}, bf16[72,768]{1,0:T(8,128)(2,1)S(1)}, u32[]{:S(2)}, u32[]{:S(2)}) %collective-permute-start.16) | collective-permute-done | bytes 110624 | tf_op jit(solution)/shard_map/ppermute | solution.py:727
  143.2 3.4 %collective-permute-done.17 = bf16[24,768]{1,0:T(8,128)(2,1)S(1)} collective-permute-done((bf16[24,768]{1,0:T(8,128)(2,1)S(1)}, bf16[24,768]{1,0:T(8,128)(2,1)S(1)}, u32[]{:S(2)}, u32[]{:S(2)}) %collective-permute-start.17) | collective-permute-done | bytes 36896 | tf_op jit(solution)/shard_map/ppermute | solution.py:722
  146.9 1.9 %collective-permute-start.19 = (bf16[72,768]{1,0:T(8,128)(2,1)S(1)}, bf16[72,768]{1,0:T(8,128)(2,1)S(1)}, u32[]{:S(2)}, u32[]{:S(2)}) collective-permute-start(bf16[72,768]{1,0:T(8,128)(2,1)S(1)} %pad_maximum_fusion.4), channel_id=1, source_target_pairs={{0,16},{2,18},{4,20},{6,22},{8,24},{10,26},{12,28},{14,30},{16,0},... | collective-permute-start | bytes 331784 | tf_op jit(solution)/shard_map/ppermute | solution.py:727
  148.8 6.9 %collective-permute-done.19 = bf16[72,768]{1,0:T(8,128)(2,1)S(1)} collective-permute-done((bf16[72,768]{1,0:T(8,128)(2,1)S(1)}, bf16[72,768]{1,0:T(8,128)(2,1)S(1)}, u32[]{:S(2)}, u32[]{:S(2)}) %collective-permute-start.19) | collective-permute-done | bytes 110624 | tf_op jit(solution)/shard_map/ppermute | solution.py:727
  155.8 3.0 %unpack_early.1 = (f32[768,768]{1,0:T(8,128)}, f32[768,768]{1,0:T(8,128)}) custom-call(s32[3]{0:T(128)S(1)} %pad_add_fusion.scalars, bf16[768,768]{1,0:T(8,128)(2,1)S(1)} %pad_maximum_fusion.first, bf16[768,768]{1,0:T(8,128)(2,1)S(1)} %collective-permute-done.21.second), custom_call_target="tpu_custom_call" | custom-call | flops 2000000000 | bytes 12000000 | tf_op jit(solution)/shard_map/unpack_early/pallas_call | solution.py:707
  158.8 3.9 %collective-permute-done.20 = bf16[144,768]{1,0:T(8,128)(2,1)S(1)} collective-permute-done((bf16[144,768]{1,0:T(8,128)(2,1)S(1)}, bf16[144,768]{1,0:T(8,128)(2,1)S(1)}, u32[]{:S(2)}, u32[]{:S(2)}) %collective-permute-start.20) | collective-permute-done | bytes 221216 | tf_op jit(solution)/shard_map/ppermute | solution.py:727
  163.4 10.3 %collective-permute-done.22 = bf16[288,768]{1,0:T(8,128)(2,1)S(1)} collective-permute-done((bf16[288,768]{1,0:T(8,128)(2,1)S(1)}, bf16[288,768]{1,0:T(8,128)(2,1)S(1)}, u32[]{:S(2)}, u32[]{:S(2)}) %collective-permute-start.22) | collective-permute-done | bytes 442400 | tf_op jit(solution)/shard_map/ppermute | solution.py:727
  173.8 2.4 %collective-permute-done.23.second = bf16[576,768]{1,0:T(8,128)(2,1)S(1)} collective-permute-done((bf16[576,768]{1,0:T(8,128)(2,1)S(1)}, bf16[576,768]{1,0:T(8,128)(2,1)S(1)}, u32[]{:S(2)}, u32[]{:S(2)}) %collective-permute-start.23) | collective-permute-done | bytes 884768 | tf_op jit(solution)/shard_map/ppermute | solution.py:727
  176.2 2.6 %unpack_late.1 = (f32[768,768]{1,0:T(8,128)}, f32[768,256]{1,0:T(8,128)}, f32[12,2,768]{2,1,0:T(2,128)}, f32[4,768]{1,0:T(4,128)}, f32[1,768]{1,0:T(1,128)S(1)},...) custom-call(s32[3]{0:T(128)S(1)} %pad_add_fusion.scalars, ...), custom_call_target="tpu_custom_call" | custom-call | flops 2000000000 | bytes 12000000 | tf_op jit(solution)/shard_map/unpack_late/pallas_call | solution.py:707
  (117 shorter events, 42.3 us)
Async XLA Ops:
  1.3 17.8 %collective-permute-start.1 = (bf16[1,384]{1,0:T(2,128)(2,1)S(1)}, bf16[1,384]{1,0:T(2,128)(2,1)S(1)}, u32[]{:S(2)}, u32[]{:S(2)}) collective-permute-start(bf16[1,384]{1,0:T(2,128)(2,1)S(1)} %concatenate.56), channel_id=1, source_target_pairs={{0,1},{1,0},{2,3},{3,2},{4,5},{5,4},{6,7},{7,6},{8,9},{9,8},{10,11... | collective-permute-start | bytes 2312 | tf_op jit(solution)/shard_map/ppermute | solution.py:722
  4.3 19.2 %collective-permute-start = (bf16[1024,384]{1,0:T(8,128)(2,1)}, bf16[1024,384]{1,0:T(8,128)(2,1)S(1)}, u32[]{:S(2)}, u32[]{:S(2)}) collective-permute-start(bf16[1024,384]{1,0:T(8,128)(2,1)} %refs_0_.1), channel_id=1, source_target_pairs={{0,1},{1,0},{2,3},{3,2},{4,5},{5,4},{6,7},{7,6},{8,9},{9,8},{10,11... | collective-permute-start | bytes 2359304 | tf_op jit(solution)/shard_map/ppermute | solution.py:722
  13.8 1.3 copy-start.5
  23.5 18.5 %collective-permute-start.2 = (bf16[1024,384]{1,0:T(8,128)(2,1)S(1)}, bf16[1024,384]{1,0:T(8,128)(2,1)S(1)}, u32[]{:S(2)}, u32[]{:S(2)}) collective-permute-start(bf16[1024,384]{1,0:T(8,128)(2,1)S(1)} %copy-done.2), channel_id=1, source_target_pairs={{0,1},{1,0},{2,3},{3,2},{4,5},{5,4},{6,7},{7,6},{8,9},{9,8},{10,11... | collective-permute-start | bytes 2359304 | tf_op jit(solution)/shard_map/ppermute | solution.py:722
  35.0 7.1 %copy-start.10 = (bf16[1024,768]{1,0:T(8,128)(2,1)}, bf16[1024,768]{1,0:T(8,128)(2,1)S(1)}, u32[]{:S(2)}) copy-start(bf16[1024,768]{1,0:T(8,128)(2,1)S(1)} %get-tuple-element.125) | copy-start | bytes 4718596
  45.3 4.0 %collective-permute-start.3 = (f32[8,1024]{1,0:T(8,128)S(1)}, f32[8,1024]{1,0:T(8,128)S(1)}, u32[]{:S(2)}, u32[]{:S(2)}) collective-permute-start(f32[8,1024]{1,0:T(8,128)S(1)} %get-tuple-element.138), channel_id=1, source_target_pairs={{0,1},{1,0},{2,3},{3,2},{4,5},{5,4},{6,7},{7,6},{8,9},{9,8},{10,11... | collective-permute-start | bytes 98312 | tf_op jit(solution)/shard_map/ppermute | solution.py:722
  57.1 1.5 copy-start.11
  58.6 1.5 copy-start.7
  61.5 2.9 %collective-permute-start.4 = (bf16[768,768]{1,0:T(8,128)(2,1)S(1)}, bf16[768,768]{1,0:T(8,128)(2,1)S(1)}, u32[]{:S(2)}, u32[]{:S(2)}) collective-permute-start(bf16[768,768]{1,0:T(8,128)(2,1)S(1)} %get-tuple-element.146), channel_id=1, source_target_pairs={{0,2},{2,0},{4,6},{6,4},{8,10},{10,8},{12,14},{14,12},{16,18},{18,... | collective-permute-start | bytes 3538952 | tf_op jit(solution)/shard_map/ppermute | solution.py:727
  61.6 20.0 %collective-permute-start.6 = (bf16[1024,384]{1,0:T(8,128)(2,1)S(1)}, bf16[1024,384]{1,0:T(8,128)(2,1)S(1)}, u32[]{:S(2)}, u32[]{:S(2)}) collective-permute-start(bf16[1024,384]{1,0:T(8,128)(2,1)S(1)} %branch_oth.1), channel_id=1, source_target_pairs={{0,1},{1,0},{2,3},{3,2},{4,5},{5,4},{6,7},{7,6},{8,9},{9,8},{10,11... | collective-permute-start | bytes 2359304 | tf_op jit(solution)/shard_map/ppermute | solution.py:722
  64.7 16.8 %collective-permute-start.5 = (bf16[384,768]{1,0:T(8,128)(2,1)S(1)}, bf16[384,768]{1,0:T(8,128)(2,1)S(1)}, u32[]{:S(2)}, u32[]{:S(2)}) collective-permute-start(bf16[384,768]{1,0:T(8,128)(2,1)S(1)} %get-tuple-element.226), channel_id=1, source_target_pairs={{0,4},{2,6},{4,0},{6,2},{8,12},{10,14},{12,8},{14,10},{16,20},{18,... | collective-permute-start | bytes 1769480 | tf_op jit(solution)/shard_map/ppermute | solution.py:727
  80.0 3.6 %copy-start.12 = (bf16[384]{0:T(512)(128)(2,1)S(1)}, bf16[384]{0:T(512)(128)(2,1)}, u32[]{:S(2)}) copy-start(bf16[384]{0:T(512)(128)(2,1)} %param.18) | copy-start | bytes 2308
  81.7 8.7 %collective-permute-start.7 = (bf16[192,768]{1,0:T(8,128)(2,1)S(1)}, bf16[192,768]{1,0:T(8,128)(2,1)S(1)}, u32[]{:S(2)}, u32[]{:S(2)}) collective-permute-start(bf16[192,768]{1,0:T(8,128)(2,1)S(1)} %get-tuple-element.230), channel_id=1, source_target_pairs={{0,8},{2,10},{4,12},{6,14},{8,0},{10,2},{12,4},{14,6},{16,24},{18,... | collective-permute-start | bytes 884744 | tf_op jit(solution)/shard_map/ppermute | solution.py:727
  90.4 9.9 %collective-permute-start.8 = (bf16[96,768]{1,0:T(8,128)(2,1)S(1)}, bf16[96,768]{1,0:T(8,128)(2,1)S(1)}, u32[]{:S(2)}, u32[]{:S(2)}) collective-permute-start(bf16[96,768]{1,0:T(8,128)(2,1)S(1)} %add_convert_fusion.10), channel_id=1, source_target_pairs={{0,16},{2,18},{4,20},{6,22},{8,24},{10,26},{12,28},{14,30},{16,0},... | collective-permute-start | bytes 442376 | tf_op jit(solution)/shard_map/ppermute | solution.py:727
  101.2 1.5 copy-start.9
  104.2 10.6 %collective-permute-start.9 = (bf16[576,768]{1,0:T(8,128)(2,1)S(1)}, bf16[576,768]{1,0:T(8,128)(2,1)S(1)}, u32[]{:S(2)}, u32[]{:S(2)}) collective-permute-start(bf16[576,768]{1,0:T(8,128)(2,1)S(1)} %get-tuple-element.188), channel_id=1, source_target_pairs={{0,2},{2,0},{4,6},{6,4},{8,10},{10,8},{12,14},{14,12},{16,18},{18,... | collective-permute-start | bytes 2654216 | tf_op jit(solution)/shard_map/ppermute | solution.py:727
  104.4 10.4 %collective-permute-start.10 = (bf16[96,768]{1,0:T(8,128)(2,1)S(1)}, bf16[96,768]{1,0:T(8,128)(2,1)S(1)}, u32[]{:S(2)}, u32[]{:S(2)}) collective-permute-start(bf16[96,768]{1,0:T(8,128)(2,1)S(1)} %add_convert_fusion.8), channel_id=1, source_target_pairs={{0,16},{2,18},{4,20},{6,22},{8,24},{10,26},{12,28},{14,30},{16,0},... | collective-permute-start | bytes 442376 | tf_op jit(solution)/shard_map/ppermute | solution.py:727
  115.0 8.7 %collective-permute-start.12 = (bf16[192,768]{1,0:T(8,128)(2,1)S(1)}, bf16[192,768]{1,0:T(8,128)(2,1)S(1)}, u32[]{:S(2)}, u32[]{:S(2)}) collective-permute-start(bf16[192,768]{1,0:T(8,128)(2,1)S(1)} %pad_maximum_fusion.3), channel_id=1, source_target_pairs={{0,8},{2,10},{4,12},{6,14},{8,0},{10,2},{12,4},{14,6},{16,24},{18,... | collective-permute-start | bytes 884744 | tf_op jit(solution)/shard_map/ppermute | solution.py:727
  115.1 11.8 %collective-permute-start.11 = (bf16[288,768]{1,0:T(8,128)(2,1)S(1)}, bf16[288,768]{1,0:T(8,128)(2,1)S(1)}, u32[]{:S(2)}, u32[]{:S(2)}) collective-permute-start(bf16[288,768]{1,0:T(8,128)(2,1)S(1)} %get-tuple-element.192), channel_id=1, source_target_pairs={{0,4},{2,6},{4,0},{6,2},{8,12},{10,14},{12,8},{14,10},{16,20},{18,... | collective-permute-start | bytes 1327112 | tf_op jit(solution)/shard_map/ppermute | solution.py:727
  116.7 15.6 %collective-permute-start.14 = (f32[8,128]{1,0:T(8,128)S(1)}, f32[8,128]{1,0:T(8,128)S(1)}, u32[]{:S(2)}, u32[]{:S(2)}) collective-permute-start(f32[8,128]{1,0:T(8,128)S(1)} %bitcast.27), channel_id=1, source_target_pairs={{0,1},{1,0},{2,3},{3,2},{4,5},{5,4},{6,7},{7,6},{8,9},{9,8},{10,11... | collective-permute-start | bytes 12296 | tf_op jit(solution)/shard_map/ppermute | solution.py:722
  118.2 18.6 %collective-permute-start.13 = (bf16[1024,384]{1,0:T(8,128)(2,1)S(1)}, bf16[1024,384]{1,0:T(8,128)(2,1)S(1)}, u32[]{:S(2)}, u32[]{:S(2)}) collective-permute-start(bf16[1024,384]{1,0:T(8,128)(2,1)S(1)} %back_oth.1), channel_id=1, source_target_pairs={{0,1},{1,0},{2,3},{3,2},{4,5},{5,4},{6,7},{7,6},{8,9},{9,8},{10,11... | collective-permute-start | bytes 2359304 | tf_op jit(solution)/shard_map/ppermute | solution.py:722
  127.0 4.8 %copy-start.1 = (bf16[1024,384]{1,0:T(8,128)(2,1)S(1)}, bf16[1024,384]{1,0:T(8,128)(2,1)}, u32[]{:S(2)}) copy-start(bf16[1024,384]{1,0:T(8,128)(2,1)} %refs_0_.1) | copy-start | bytes 2359300
  127.1 19.7 %collective-permute-start.18 = (bf16[384,768]{1,0:T(8,128)(2,1)S(1)}, bf16[384,768]{1,0:T(8,128)(2,1)S(1)}, u32[]{:S(2)}, u32[]{:S(2)}) collective-permute-start(bf16[384,768]{1,0:T(8,128)(2,1)S(1)} %pad_maximum_fusion.1), channel_id=1, source_target_pairs={{0,4},{2,6},{4,0},{6,2},{8,12},{10,14},{12,8},{14,10},{16,20},{18,... | collective-permute-start | bytes 1769480 | tf_op jit(solution)/shard_map/ppermute | solution.py:727
  128.6 8.2 %collective-permute-start.15 = (bf16[144,768]{1,0:T(8,128)(2,1)S(1)}, bf16[144,768]{1,0:T(8,128)(2,1)S(1)}, u32[]{:S(2)}, u32[]{:S(2)}) collective-permute-start(bf16[144,768]{1,0:T(8,128)(2,1)S(1)} %get-tuple-element.201), channel_id=1, source_target_pairs={{0,8},{2,10},{4,12},{6,14},{8,0},{10,2},{12,4},{14,6},{16,24},{18,... | collective-permute-start | bytes 663560 | tf_op jit(solution)/shard_map/ppermute | solution.py:727
  131.8 6.9 %copy-start.3 = (bf16[1024,384]{1,0:T(8,128)(2,1)S(1)}, bf16[1024,384]{1,0:T(8,128)(2,1)}, u32[]{:S(2)}) copy-start(bf16[1024,384]{1,0:T(8,128)(2,1)} %refs_1_.1) | copy-start | bytes 2359300
  136.9 5.7 %collective-permute-start.16 = (bf16[72,768]{1,0:T(8,128)(2,1)S(1)}, bf16[72,768]{1,0:T(8,128)(2,1)S(1)}, u32[]{:S(2)}, u32[]{:S(2)}) collective-permute-start(bf16[72,768]{1,0:T(8,128)(2,1)S(1)} %add_convert_fusion.12), channel_id=1, source_target_pairs={{0,16},{2,18},{4,20},{6,22},{8,24},{10,26},{12,28},{14,30},{16,0},... | collective-permute-start | bytes 331784 | tf_op jit(solution)/shard_map/ppermute | solution.py:727
  142.6 4.0 %collective-permute-start.17 = (bf16[24,768]{1,0:T(8,128)(2,1)S(1)}, bf16[24,768]{1,0:T(8,128)(2,1)S(1)}, u32[]{:S(2)}, u32[]{:S(2)}) collective-permute-start(bf16[24,768]{1,0:T(8,128)(2,1)S(1)} %slice.136), channel_id=1, source_target_pairs={{0,1},{1,0},{2,3},{3,2},{4,5},{5,4},{6,7},{7,6},{8,9},{9,8},{10,11... | collective-permute-start | bytes 110600 | tf_op jit(solution)/shard_map/ppermute | solution.py:722
  146.9 8.9 %collective-permute-start.21 = (bf16[768,768]{1,0:T(8,128)(2,1)S(1)}, bf16[768,768]{1,0:T(8,128)(2,1)S(1)}, u32[]{:S(2)}, u32[]{:S(2)}) collective-permute-start(bf16[768,768]{1,0:T(8,128)(2,1)S(1)} %pad_maximum_fusion.first), channel_id=1, source_target_pairs={{0,2},{2,0},{4,6},{6,4},{8,10},{10,8},{12,14},{14,12},{16,18},{18,... | collective-permute-start | bytes 3538952 | tf_op jit(solution)/shard_map/ppermute | solution.py:727
  146.9 8.7 %collective-permute-start.19 = (bf16[72,768]{1,0:T(8,128)(2,1)S(1)}, bf16[72,768]{1,0:T(8,128)(2,1)S(1)}, u32[]{:S(2)}, u32[]{:S(2)}) collective-permute-start(bf16[72,768]{1,0:T(8,128)(2,1)S(1)} %pad_maximum_fusion.4), channel_id=1, source_target_pairs={{0,16},{2,18},{4,20},{6,22},{8,24},{10,26},{12,28},{14,30},{16,0},... | collective-permute-start | bytes 331784 | tf_op jit(solution)/shard_map/ppermute | solution.py:727
  155.7 7.1 %collective-permute-start.20 = (bf16[144,768]{1,0:T(8,128)(2,1)S(1)}, bf16[144,768]{1,0:T(8,128)(2,1)S(1)}, u32[]{:S(2)}, u32[]{:S(2)}) collective-permute-start(bf16[144,768]{1,0:T(8,128)(2,1)S(1)} %get-tuple-element.236), channel_id=1, source_target_pairs={{0,8},{2,10},{4,12},{6,14},{8,0},{10,2},{12,4},{14,6},{16,24},{18,... | collective-permute-start | bytes 663560 | tf_op jit(solution)/shard_map/ppermute | solution.py:727
  162.8 10.9 %collective-permute-start.22 = (bf16[288,768]{1,0:T(8,128)(2,1)S(1)}, bf16[288,768]{1,0:T(8,128)(2,1)S(1)}, u32[]{:S(2)}, u32[]{:S(2)}) collective-permute-start(bf16[288,768]{1,0:T(8,128)(2,1)S(1)} %pad_maximum_fusion.2), channel_id=1, source_target_pairs={{0,4},{2,6},{4,0},{6,2},{8,12},{10,14},{12,8},{14,10},{16,20},{18,... | collective-permute-start | bytes 1327112 | tf_op jit(solution)/shard_map/ppermute | solution.py:727
  173.7 2.5 %collective-permute-start.23 = (bf16[576,768]{1,0:T(8,128)(2,1)S(1)}, bf16[576,768]{1,0:T(8,128)(2,1)S(1)}, u32[]{:S(2)}, u32[]{:S(2)}) collective-permute-start(bf16[576,768]{1,0:T(8,128)(2,1)S(1)} %constant_dynamic-update-slice_fusion.2.first), channel_id=1, source_target_pairs={{0,2},{2,0},{4,6},{6,4},{8,10},{10,8},{12,14},{14,12},{16,18},{18,... | collective-permute-start | bytes 2654216 | tf_op jit(solution)/shard_map/ppermute | solution.py:727
  (5 other events, 5.8 us)

commit v2 on v1

--- a/solution.py
+++ b/solution.py
@@ -35,6 +35,11 @@
 def split_two(v):
     hi = v.astype(BF16)
     return hi, (v - hi.astype(F32)).astype(BF16)
+
+
+def split_three(v):
+    hi, mid = split_two(v)
+    return hi, mid, (v - hi.astype(F32) - mid.astype(F32)).astype(BF16)
 
 
 def expand(v, spread):
@@ -314,8 +319,8 @@
 
 def back_kernel(
     i, scalars, g, act, sact, hs, xd, row_in, hf, hb, gb, gf, dc, pre, slope, conv, head_par, spread, gather,
-    ext_in, carry_in, gconv_in, ghead_in, _rest, _rd, rest_ref, rd_ref, gconv_ref, ghead_ref, ext_out,
-    carry, ext, stack, xs, rsum,
+    ext_in, carry_in, gconv_in, _rest, _rates, _rd, rest_ref, rates_ref, rd_ref, gconv_ref, ext_out,
+    carry, ext, stack, xs, rsum, csum,
     *, heads, width, state_width, block, top,
 ):
     blk = top - i
@@ -326,27 +331,22 @@
         ext[block:, :] = ext_in[...]
         carry[...] = carry_in[...]
         gconv_ref[...] = gconv_in[...]
-        ghead_ref[...] = ghead_in[...]
-        stack[3 * CHUNK : 4 * CHUNK, width:] = jnp.zeros((CHUNK, width), BF16)
         rsum[...] = jnp.zeros_like(rsum)
+        csum[...] = jnp.zeros_like(csum)
 
     n = state_width // 4
-    conv_width = width + state_width
     r = lax.broadcasted_iota(jnp.int32, (CHUNK, CHUNK), 0)
     c = lax.broadcasted_iota(jnp.int32, (CHUNK, CHUNK), 1)
     later = c > r
     earlier = c < r
-    rev = (c >= r).astype(F32)
-    tri = (c <= r).astype(F32)
     is_fwd_all = lax.broadcasted_iota(jnp.int32, (block, LANES), 1) < heads
     is_fwd = lax.broadcasted_iota(jnp.int32, (CHUNK, LANES), 1) < heads
     mask = row_mask(blk, block, scalars[0])
-    dt_all = hs[:, LANES : 2 * LANES]
     cum_all = hs[:, 2 * LANES : 3 * LANES]
     tot_all = hs[:, 3 * LANES :]
     wide = expand(
         jnp.concatenate(
-            [jnp.exp(jnp.where(is_fwd_all, tot_all - cum_all, cum_all)), dt_all * mask]
+            [jnp.exp(jnp.where(is_fwd_all, tot_all - cum_all, cum_all)), hs[:, LANES : 2 * LANES] * mask]
             + [jnp.exp(tot_all[k * CHUNK : k * CHUNK + 8]) for k in range(per)]
             + [eight(head_par[2:3, :])],
             axis=0,
@@ -354,12 +354,9 @@
         spread[...],
     )
     skip = wide[2 * block + 8 * per : 2 * block + 8 * per + 1]
-    rd_parts = []
     for c_idx in reversed(range(per)):
         rows = slice(c_idx * CHUNK, (c_idx + 1) * CHUNK)
         rows_dt = slice(block + c_idx * CHUNK, block + (c_idx + 1) * CHUNK)
-        z = hs[rows, 0:LANES]
-        dt = dt_all[rows]
         cumx = cum_all[rows] * LOG2_E
         cum_t = jnp.transpose(cumx)
         sact_c = sact[rows, :]
@@ -367,6 +364,7 @@
         b_b, c_b = sact_c[:, 2 * n : 3 * n], sact_c[:, 3 * n :]
         s_f = jnp.where(later, mm_nt(b_f, c_f), 0.0)
         s_b = jnp.where(earlier, mm_nt(b_b, c_b), 0.0)
+        s_all = s_f + s_b
         grad_f = carry[...]
         grad_f_low = grad_f.astype(BF16)
         grad_b_low = gb[c_idx]
@@ -377,7 +375,7 @@
             hb[c_idx].astype(F32) * grad_b_low.astype(F32), axis=0, keepdims=True
         )
         e_hi, e_lo = split_two(eight(jnp.concatenate([edge_f, edge_b], axis=1)))
-        stack[4 * CHUNK :, :] = jnp.concatenate([e_hi, e_lo], axis=0)
+        stack[2 * CHUNK :, :] = jnp.concatenate([e_hi, e_lo], axis=0)
         carry[...] = grad_f * keep_f + gf[c_idx]
         in_f = mm(b_f, grad_f_low)
         in_b = mm(b_b, grad_b_low)
@@ -399,17 +397,23 @@
                         cumx[:, heads + h : heads + h + 1] - cum_t[heads + h : heads + h + 1, :],
                     )
                 )
-                low_f = (s_f * damp).astype(BF16)
-                low_b = (s_b * damp).astype(BF16)
-                w_f.append(low_f)
-                w_b.append(low_b)
-                dw_f = dw[q * CHUNK : (q + 1) * CHUNK]
-                dw_b = dw[(2 + q) * CHUNK : (3 + q) * CHUNK]
-                d_scores = d_scores + jnp.where(later, dw_f, dw_b) * damp
-                rsum[h : h + 1, :] = jnp.sum(dw_f * low_f.astype(F32), axis=0, keepdims=True)
-                rsum[heads + h : heads + h + 1, :] = -jnp.sum(
-                    dw_b * low_b.astype(F32), axis=0, keepdims=True
+                w_f.append((s_f * damp).astype(BF16))
+                w_b.append((s_b * damp).astype(BF16))
+                part = jnp.where(
+                    later, dw[q * CHUNK : (q + 1) * CHUNK], dw[(2 + q) * CHUNK : (3 + q) * CHUNK]
                 )
+                part = part * damp
+                d_scores = d_scores + part
+                e_all = part * s_all
+                e_fwd = jnp.where(later, e_all, 0.0)
+                sum_all = jnp.sum(e_all, axis=0, keepdims=True)
+                sum_fwd = jnp.sum(e_fwd, axis=0, keepdims=True)
+                rsum[h : h + 1, :] = sum_fwd
+                rsum[heads + h : heads + h + 1, :] = sum_fwd - sum_all
+                sum_all = jnp.sum(e_all, axis=1, keepdims=True)
+                sum_fwd = jnp.sum(e_fwd, axis=1, keepdims=True)
+                csum[:, h : h + 1] = -sum_fwd
+                csum[:, heads + h : heads + h + 1] = sum_all - sum_fwd
             dx = mm(
                 jnp.concatenate(
                     [jnp.concatenate(w_f, axis=1), jnp.concatenate(w_b, axis=1)], axis=0
@@ -418,24 +422,19 @@
             )
             edge_pf = wide[rows, lanes]
             edge_pb = wide[rows, lanes_b]
-            intra_f = dx[:CHUNK]
             inter_f = edge_pf * in_f[:, lanes]
-            dx_f = intra_f + inter_f
-            dx_b = dx[CHUNK:] + edge_pb * in_b[:, lanes]
+            inter_b = edge_pb * in_b[:, lanes]
+            dx_f = dx[:CHUNK] + inter_f
+            dx_b = dx[CHUNK:] + inter_b
             xf = xf_pair.astype(F32)
             xb = xb_pair.astype(F32)
             xs[:, lanes] = (xf * edge_pf).astype(BF16)
             xs[:, lanes_b] = (xb * edge_pb).astype(BF16)
             act_p = act[rows, lanes]
-            hi, lo = split_two(-(xf * intra_f))
-            stack[0:CHUNK, lanes] = hi
-            stack[CHUNK : 2 * CHUNK, lanes] = lo
-            hi, lo = split_two(xb * dx_b)
-            stack[0:CHUNK, lanes_b] = hi
-            stack[CHUNK : 2 * CHUNK, lanes_b] = lo
-            stack[2 * CHUNK : 3 * CHUNK, lanes] = (act_p * dx_f).astype(BF16)
-            stack[2 * CHUNK : 3 * CHUNK, lanes_b] = (act_p * dx_b).astype(BF16)
-            stack[3 * CHUNK : 4 * CHUNK, lanes] = (xf * inter_f).astype(BF16)
+            stack[0:CHUNK, lanes] = (act_p * dx_f).astype(BF16)
+            stack[0:CHUNK, lanes_b] = (act_p * dx_b).astype(BF16)
+            stack[CHUNK : 2 * CHUNK, lanes] = (xf * inter_f).astype(BF16)
+            stack[CHUNK : 2 * CHUNK, lanes_b] = (xb * inter_b).astype(BF16)
             d_inner = (
                 skip[:, lanes] * g_pair.astype(F32)
                 + wide[rows_dt, lanes] * dx_f
@@ -452,24 +451,14 @@
         ext[rows, width:] = d_state * slope[rows, width:].astype(F32)
         head_sums = mm(stack[...], gather[...])
         rin = row_in[rows, :]
-        d_cum = (
-            head_sums[0:CHUNK]
-            + head_sums[CHUNK : 2 * CHUNK]
-            + jnp.transpose(rsum[...])
-            + jnp.where(is_fwd, rin, 0.0)
+        ahead = head_sums[CHUNK : 2 * CHUNK]
+        rates_ref[rows, 0:LANES] = (
+            jnp.transpose(rsum[...]) + csum[...] + jnp.where(is_fwd, rin, ahead)
         )
-        d_run = head_sums[3 * CHUNK : 4 * CHUNK] + jnp.where(is_fwd, 0.0, rin)
-        edge = head_sums[4 * CHUNK : 4 * CHUNK + 1] + head_sums[4 * CHUNK + 8 : 4 * CHUNK + 9]
-        back_run = jnp.dot(rev, d_cum, precision=HIGHEST, preferred_element_type=F32)
-        run = jnp.dot(tri, d_run, precision=HIGHEST, preferred_element_type=F32)
-        d_rate = jnp.where(is_fwd, back_run + run - d_run, back_run - d_cum + run) + edge
-        neg = head_par[1:2, :]
-        d_step = neg * d_rate + mask[rows] * head_sums[2 * CHUNK : 3 * CHUNK]
-        d_z = d_step / (1.0 + jnp.exp(-z))
-        ghead_ref[0:1, :] += jnp.sum(d_rate * (neg * dt), axis=0, keepdims=True)
-        ghead_ref[1:2, :] += jnp.sum(d_z, axis=0, keepdims=True)
-        rest_ref[rows, conv_width:] = d_z.astype(BF16)
-        rd_parts.append(jnp.sum(d_z * (z - head_par[0:1, :]), axis=1, keepdims=True))
+        rates_ref[rows, LANES : 2 * LANES] = jnp.where(is_fwd, ahead, rin)
+        rates_ref[rows, 2 * LANES : 3 * LANES] = head_sums[0:CHUNK] * mask[rows]
+        edge = head_sums[2 * CHUNK : 2 * CHUNK + 1] + head_sums[2 * CHUNK + 8 : 2 * CHUNK + 9]
+        rates_ref[rows, 3 * LANES :] = jnp.broadcast_to(edge, (CHUNK, LANES))
 
     prev = pre[...].astype(F32)
     whole_ext = ext[...]
@@ -481,13 +470,44 @@
         moved = pltpu.roll(whole_ext, block + 8 - (3 - j), 0)[:block]
         acc = acc + conv[j : j + 1, :] * moved
         gconv_ref[j : j + 1, :] += jnp.sum(moved * prev, axis=0, keepdims=True)
-    rest_ref[:, 0:conv_width] = acc.astype(BF16)
-    rd = jnp.sum(acc * prev, axis=1, keepdims=True) + jnp.concatenate(rd_parts[::-1], axis=0)
+    rest_ref[...] = acc.astype(BF16)
+    rd = jnp.sum(acc * prev, axis=1, keepdims=True)
     rd_ref[...] = to_row(rd, jnp.zeros_like(rd))
     ext[block:, :] = ext[0:8, :]
     ext_out[...] = ext[0:8, :]
 
 
+def rates_kernel(i, scalars, rates, hs, rd_a, rd_b, head_par, dz_ref, ghead_ref, rd_ref, *, heads, block):
+    @pl.when(i == 0)
+    def _():
+        ghead_ref[...] = jnp.zeros_like(ghead_ref)
+
+    r = lax.broadcasted_iota(jnp.int32, (CHUNK, CHUNK), 0)
+    c = lax.broadcasted_iota(jnp.int32, (CHUNK, CHUNK), 1)
+    tri = jnp.where(c <= r, 1.0, 0.0).astype(BF16)
+    is_fwd = lax.broadcasted_iota(jnp.int32, (CHUNK, LANES), 1) < heads
+    neg = head_par[1:2, :]
+    for c_idx in range(block // CHUNK):
+        rows = slice(c_idx * CHUNK, (c_idx + 1) * CHUNK)
+        d_cum = rates[rows, 0:LANES]
+        d_run = rates[rows, LANES : 2 * LANES]
+        sums = mm(tri, jnp.concatenate([*split_three(d_cum), *split_two(d_run)], axis=1))
+        ahead = sums[:, 0:LANES] + sums[:, LANES : 2 * LANES] + sums[:, 2 * LANES : 3 * LANES]
+        run = sums[:, 3 * LANES : 4 * LANES] + sums[:, 4 * LANES :]
+        behind = ahead[CHUNK - 1 :, :] - ahead
+        d_rate = jnp.where(is_fwd, behind + d_cum + run - d_run, behind + run)
+        d_rate = d_rate + rates[rows, 3 * LANES :]
+        z = hs[rows, 0:LANES]
+        d_step = neg * d_rate + rates[rows, 2 * LANES : 3 * LANES]
+        d_z = d_step / (1.0 + jnp.exp(-z))
+        dt = hs[rows, LANES : 2 * LANES]
+        ghead_ref[0:1, :] += jnp.sum(d_rate * (neg * dt), axis=0, keepdims=True)
+        ghead_ref[1:2, :] += jnp.sum(d_z, axis=0, keepdims=True)
+        dz_ref[rows, :] = d_z.astype(BF16)
+        rd = jnp.sum(d_z * (z - head_par[0:1, :]), axis=1, keepdims=True)
+        rd_ref[:, rows] = rd_a[:, rows] + rd_b[:, rows] + to_row(rd, jnp.zeros_like(rd))
+
+
 def columns_of(scalars, other, size):
     rank = scalars[1]
     return pl.ds(pl.multiple_of((1 - rank if other else rank) * size, LANES), size)
@@ -499,17 +519,23 @@
 
 
 def back_project_kernel(
-    scalars, dgp, rest, w_gate, w_inner, w_state, w_step, out_ref, *, other
+    scalars, dgp, rest, dz, rd, w_gate, w_inner, w_state, w_step, out_ref, *, other
 ):
-    at = columns_of(scalars, other, out_ref.shape[1])
+    rows, size = dgp.shape[0], out_ref.shape[1]
+    at = columns_of(scalars, other, size)
     a = w_inner.shape[1]
-    b = a + w_state.shape[1]
-    out_ref[...] = (
+    out_ref[0:rows, :] = (
         mm_nt(dgp[...], w_gate[at, :])
         + mm_nt(rest[:, 0:a], w_inner[at, :])
-        + mm_nt(rest[:, a:b], w_state[at, :])
-        + mm_nt(rest[:, b:], w_step[at, :])
+        + mm_nt(rest[:, a:], w_state[at, :])
+        + mm_nt(dz[...], w_step[at, :])
     ).astype(out_ref.dtype)
+    if other:
+        part = rows // 4
+        lines = jnp.concatenate([rd[0:1, k * part : (k + 1) * part] for k in range(4)], axis=0)
+        lines = jnp.concatenate(split_three(lines) + (jnp.zeros((4, part), BF16),), axis=0)
+        out_ref[rows : rows + 16, 0:part] = lines
+        out_ref[rows : rows + 16, part:] = jnp.zeros((16, size - part), BF16)
 
 
 def home_of(r, me, order):
@@ -549,16 +575,18 @@
 
 
 def pack_late_kernel(
-    scalars, inner, state, w_inner, w_state_t, gain, gain_part, gconv, ghead, small, gather,
+    scalars, inner, state, step_low, w_inner, w_state_t, gain, gain_part, gconv, ghead, small, gather,
     keep_ref, send_ref, misc, *, order, heads, state_width,
 ):
     model, width = w_inner.shape
     hi, lo = split_two(inner[...].astype(F32) * w_inner[...].astype(F32))
     ones = jnp.ones((8, hi.shape[1]), BF16)
     gain_row = (mm_nt(ones, hi) + mm_nt(ones, lo) + gain_part[...])[0:1]
-    gain_row += jnp.sum(state[...].astype(F32) * w_state_t[...].astype(F32), axis=0, keepdims=True)
+    step = step_low[...].astype(F32)
+    w_t = w_state_t[...].astype(F32)
+    gain_row += jnp.sum(state[...].astype(F32) * w_t[:state_width], axis=0, keepdims=True)
+    gain_row += jnp.sum(step * w_t[state_width:], axis=0, keepdims=True)
     gain_row = gain_row / gain[...]
-    step = state[state_width:, :].astype(F32)
     misc[...] = jnp.zeros_like(misc)
 
     def put_single(k, row):
@@ -671,7 +699,7 @@
     return ref
 
 
-def call(kernel, blocks, ins, out_views, out_shape, scratch, name, us, aliases=None):
+def call(kernel, blocks, ins, out_views, out_shape, scratch, name, aliases=None, us=0.0):
     views = [view for _, view in ins[1:]] + out_views
     arrays = [ins[0]] + [
         pltpu.with_memory_space_constraint(x, pltpu.VMEM) if view is not fixed else x
@@ -702,7 +730,7 @@
     )(*arrays)
 
 
-def whole(kernel, args, out_shape, scratch, name, us, in_vmem=True):
+def whole(kernel, args, out_shape, scratch, name, in_vmem=True, us=0.0):
     vmem = pl.BlockSpec(memory_space=pltpu.VMEM)
     return pl.pallas_call(
         kernel,
@@ -846,7 +874,7 @@
         ],
         [pltpu.VMEM((block + 8, conv_width), F32), pltpu.VMEM((n, width), F32)],
         "project",
-        12,
+        us=12,
     )
 
     block = MIX_BLOCK
@@ -870,7 +898,7 @@
         [full(rows, width), low(chunks, n, width)],
         [pltpu.VMEM((n, width), F32)],
         "mix",
-        7,
+        us=7,
     )
 
     block = GATE_BLOCK
@@ -891,12 +919,12 @@
         [full(rows, width), low(rows, width), full(8, rows)],
         [],
         "gate",
-        3,
+        us=3,
     )
 
     oth_sums = swap_mp(sums)
     branch_oth = whole(
-        partial(branch_kernel, other=True), (scalars, gz, out_v), [low(rows, width_own)], [], "branch_oth", 3
+        partial(branch_kernel, other=True), (scalars, gz, out_v), [low(rows, width_own)], [], "branch_oth", us=3
     )[0]
     sums = sums + oth_sums
     branch_got = swap_mp(after(branch_oth, sums))
@@ -936,7 +964,7 @@
         ],
         [pltpu.VMEM((n, width), F32), pltpu.VMEM((block, 2 * width), BF16)],
         "gate_back",
-        8,
+        us=8,
     )
 
     def back_part(first, count, g, state):
@@ -961,7 +989,8 @@
             (head_par, fixed),
             (spread, fixed),
             (gather, fixed),
-            *[(x, fixed) for x in state[:4]],
+            *[(x, fixed) for x in state[:3]],
+            (state[3], here),
             (state[4], here),
             (state[5], here_lanes),
         ]
@@ -969,24 +998,25 @@
             partial(back_kernel, block=block, top=first, **sizes),
             count,
             ins,
-            [here, here_lanes, fixed, fixed, fixed, fixed],
+            [here, here, here_lanes, fixed, fixed, fixed],
             [
-                low(rows, conv_width + LANES),
+                low(rows, conv_width),
+                full(rows, 4 * LANES),
                 full(8, rows),
                 full(8, conv_width),
-                full(8, LANES),
                 full(8, conv_width),
                 full(n, width),
             ],
             [
                 pltpu.VMEM((block + 8, conv_width), F32),
-                pltpu.VMEM((4 * CHUNK + 16, 2 * width), BF16),
+                pltpu.VMEM((2 * CHUNK + 16, 2 * width), BF16),
                 pltpu.VMEM((CHUNK, 2 * width), BF16),
                 pltpu.VMEM((LANES, CHUNK), F32),
+                pltpu.VMEM((CHUNK, LANES), F32),
             ],
             "mix_back",
-            3 * count,
-            aliases={len(ins) - 2: 0, len(ins) - 1: 1},
+            us=3 * count,
+            aliases={len(ins) - 3: 0, len(ins) - 2: 1, len(ins) - 1: 2},
         )
 
     order_a, order_b = (0, 1, 2, 3), (0, 1, 2, 3)
@@ -998,7 +1028,6 @@
         [low(width, model), low(width, model), full(8, model)],
         [],
         "pack_early",
-        3,
     )
 
     def halve(keep, send, bit):
@@ -1020,12 +1049,12 @@
         jnp.zeros((8, conv_width), F32),
         jnp.zeros((n, width), F32),
         jnp.zeros((8, conv_width), F32),
-        jnp.zeros((8, LANES), F32),
     )
     keep, send = halve(keep, send, order_a[0])
     state = (
         *zeros,
-        jnp.zeros((rows, conv_width + LANES), BF16),
+        jnp.zeros((rows, conv_width), BF16),
+        jnp.zeros((rows, 4 * LANES), F32),
         jnp.zeros((8, rows), F32),
     )
     parts = 4
@@ -1034,11 +1063,11 @@
     sent, x = swap_dp(send, order_a[1]), None
     for k in range(parts):
         outs = back_part((parts - k) * count - 1, count, g, state)
-        rest, rd_rest, gconv, ghead, ext_carry, carry = outs
+        rest, rates, rd_rest, gconv, ext_carry, carry = outs
         if k == 1:
+            sent, carry = lax.optimization_barrier((sent, carry))
+        elif k == 2:
             sent, carry, branch_got = lax.optimization_barrier((sent, carry, branch_got))
-        elif k == 2:
-            sent, carry = lax.optimization_barrier((sent, carry))
         elif k == 3:
             sent, rest = lax.optimization_barrier((sent, rest))
         if k > 0:
@@ -1049,21 +1078,39 @@
                 sent = swap_dp(send, order_a[k + 1])
             else:
                 x = rest_of_dp(add_low(keep, sent))
-                sent = swap_dp(x, order_a[3])
-        state = (ext_carry, carry, gconv, ghead, rest, rd_rest)
-
+        state = (ext_carry, carry, gconv, rest, rates, rd_rest)
+
+    block = GATE_BLOCK
+    rates, x, rest = lax.optimization_barrier((rates, x, rest))
+    sent = swap_dp(x, order_a[3])
+    dz, ghead, rd_part = call(
+        partial(rates_kernel, heads=heads, block=block),
+        rows // block,
+        [
+            scalars,
+            (rates, rows_of(block)),
+            (hs, rows_of(block)),
+            (rd_gate, lanes_of(block)),
+            (rd_rest, lanes_of(block)),
+            (head_par, fixed),
+        ],
+        [rows_of(block), fixed, lanes_of(block)],
+        [low(rows, LANES), full(8, LANES), full(8, rows)],
+        [],
+        "rates",
+    )
     grad_inner = mm_tn(normed, rest[:, :width]).astype(BF16)
     grad_state = mm_tn(rest[:, width:], normed).astype(BF16)
+    grad_step = mm_tn(dz, normed).astype(BF16)
     keep, send = whole(
         partial(pack_late_kernel, order=order_b, heads=heads, state_width=state_width),
         (
-            scalars, grad_inner, grad_state, proj_inner, w_state_t, gain, gain_part, gconv, ghead,
+            scalars, grad_inner, grad_state, grad_step, inner_v, w_state_t, gain, gain_part, gconv, ghead,
             small, gather,
         ),
         [low(LATE_ROWS * SHARDS // 2, model), low(LATE_ROWS * SHARDS // 2, model)],
         [pltpu.VMEM((8 * SHARDS, model), F32)],
         "pack_late",
-        3,
     )
 
     def halve_with(keep, send, bit, *work):
@@ -1071,20 +1118,19 @@
         h = keep.shape[0] // 2
         return add_low(keep[:h], got[:h]), add_low(keep[h:], got[h:])
 
-    back_args = (scalars, dgp, after(rest, send), gate_v, inner_v, state_v, step_weight)
-    dn_oth = whole(
-        partial(back_project_kernel, other=True), back_args, [low(rows, width_own)], [], "back_oth", 4
-    )[0]
-    rd_part = rd_gate[0] + rd_rest[0]
-    keep, send = halve_with(keep, send, order_b[0], dn_oth, rd_part)
     x = jnp.concatenate([x, sent])
     send, x = lax.optimization_barrier((send, x))
+    keep, send = halve_with(keep, send, order_b[0])
+    send, x, rest = lax.optimization_barrier((send, x, rest))
+    back_args = (scalars, dgp, rest, dz, rd_part, gate_v, inner_v, state_v, step_weight)
+    dn_oth = whole(
+        partial(back_project_kernel, other=True), back_args, [low(rows + 16, width_own)], [], "back_oth"
+    )[0]
     dn_got = swap_mp(dn_oth)
-    oth_rd = swap_mp(rd_part.reshape(8, rows // 8)).reshape(rows)
 
     sent = swap_dp(x, order_a[2])
     dn_own = whole(
-        partial(back_project_kernel, other=False), back_args, [full(rows, width_own)], [], "back_own", 4
+        partial(back_project_kernel, other=False), (*back_args[:2], after(rest, dn_oth), *back_args[3:]), [full(rows, width_own)], [], "back_own"
     )[0]
     keep, send = halve_with(keep, send, order_b[1], dn_own)
     x = jnp.concatenate([x, sent])
@@ -1092,15 +1138,15 @@
 
     sent = swap_dp(x, order_a[1])
     branch_own = whole(
-        partial(branch_kernel, other=False), (scalars, gz_late, out_v), [full(rows, width_own)], [], "branch_own", 3
+        partial(branch_kernel, other=False), (scalars, gz_late, out_v), [full(rows, width_own)], [], "branch_own"
     )[0]
-    keep, send = halve_with(keep, send, order_b[2], branch_own, dn_got)
+    keep, send = halve_with(keep, send, order_b[2], branch_own)
 
     seq_mask = (jnp.arange(rows) < lengths[0]).astype(F32)[:, None]
     gate_inv = lax.rsqrt(sums[0] / inner_width + EPSILON)[:, None]
     tokens_f = tokens_late.astype(F32)
     block_out = (tokens_f + seq_mask * gate_inv * (branch_own + branch_got.astype(F32))).astype(BF16)
-    z = rest_of_dp(add_low(keep, after(swap_dp(send, order_b[3]), block_out)))
+    z = rest_of_dp(add_low(keep, after(swap_dp(send, order_b[3]), block_out, dn_got)))
     part = model // SHARDS
     tail = z[part:]
     tail_row = lax.broadcasted_iota(jnp.int32, (LATE_ROWS - part, 1), 0)
@@ -1116,11 +1162,15 @@
         oth_f * oth_f, axis=1, keepdims=True
     )
     inv = lax.rsqrt(square / model + EPSILON)
-    grad_full = dn_own + dn_got.astype(F32)
+    part = rows // 4
+    lines = dn_got[rows:, :part].astype(F32)
+    oth_rd = (lines[0:4] + lines[4:8] + lines[8:12]).reshape(rows)
+    rd_both = rd_part[0] + oth_rd
+    grad_full = dn_own + dn_got[:rows].astype(F32)
     grad_tokens = (
         cotangent.astype(F32)
         + inv * (grad_full * norm_gain.astype(F32)[None])
-        - tokens_f * (inv * inv * ((rd_part + oth_rd)[:, None] / model))
+        - tokens_f * (inv * inv * (rd_both[:, None] / model))
     )
 
     z = jnp.concatenate([z, after(swap_dp(z, order_b[3]), grad_tokens)])
@@ -1130,7 +1180,6 @@
         [full(width, model), full(model, width)],
         [],
         "unpack_early",
-        4,
         in_vmem=False,
     )
     z = jnp.concatenate([z, after(swap_dp(z, order_b[2]), grad_proj_out)])
@@ -1167,7 +1216,6 @@
         ],
         [pltpu.VMEM((state_width, model), F32), pltpu.VMEM((8 * SHARDS, model), F32)],
         "unpack_late",
-        4,
         in_vmem=False,
     )
     return (

time: 181 us -> 176 us (0.972)
  starting transfers between devices: 25.6 us -> 21.6 us
    ppermute x16, starting transfers between devices: 16.1 us -> 12.3 us  [swap_dp(): return lax.ppermute(x, 'dp', [(i, i ^ 1 << bit) for i in range(size)])]
    ppermute x8 -> x7, waiting for transfers between devices: 14.6 us -> 11.5 us  [swap_mp(): return lax.ppermute(x, 'mp', [(0, 1), (1, 0)])]
    ppermute x16, waiting for transfers between devices: 39.1 us -> 41.1 us  [swap_dp(): return lax.ppermute(x, 'dp', [(i, i ^ 1 << bit) for i in range(size)])]
    pallas_call x8 -> x9, Pallas kernels: 56.5 us -> 55.9 us  [call(): pl.pallas_call(looped, out_shape=[pltpu.VMEM(o.shape, o.dtype) for o in o...]
    dot_general x4 -> x5, matrix products: 5.2 us -> 5.45 us  [mm_tn(): lax.dot_general(a, b, (((0,), (0,)), ((), ())), preferred_element_type=F32)]
    ppermute x8 -> x7, starting transfers between devices: 9.44 us -> 9.29 us  [swap_mp(): return lax.ppermute(x, 'mp', [(0, 1), (1, 0)])]
    unnamed x29 -> x24, local copies, waits for them, and re-layouts: 7.91 us -> 7.9 us
  transfers between devices with their start and end apart: 24 -> 23, of which waited for: 14 -> 16; matrix products, arithmetic and copies ran while one was open for 5% -> 5% of each run, Pallas kernels for 32% -> 34%
where the time goes in v2:
time: 176 us
  Pallas kernels  74.7 us (42%)
  waiting for transfers between devices  52.6 us (30%)
  starting transfers between devices  21.6 us (12%)
  local copies, waits for them, and re-layouts  11.7 us (7%)
  other arithmetic  7.79 us (4%)
  matrix products  5.45 us (3%)
  between operations  1.79 us (1%)
    pallas_call x9, Pallas kernels, call(): pl.pallas_call(looped, out_shape=[pltpu.VMEM(o.shape, o.dtype) for o in o...  55.9 us
    ppermute x16, waiting for transfers between devices, swap_dp(): return lax.ppermute(x, 'dp', [(i, i ^ 1 << bit) for i in range(size)])  41.1 us
    pallas_call x8, Pallas kernels, whole(): pl.pallas_call(kernel, out_shape=[pltpu.VMEM(o.shape, o.dtype) if in_vmem...  17.3 us
    ppermute x16, starting transfers between devices, swap_dp(): return lax.ppermute(x, 'dp', [(i, i ^ 1 << bit) for i in range(size)])  12.3 us
    ppermute x7, waiting for transfers between devices, swap_mp(): return lax.ppermute(x, 'mp', [(0, 1), (1, 0)])  11.5 us
    ppermute x7, starting transfers between devices, swap_mp(): return lax.ppermute(x, 'mp', [(0, 1), (1, 0)])  9.29 us
    unnamed x24, local copies, waits for them, and re-layouts  7.9 us
    dot_general x5, matrix products, mm_tn(): lax.dot_general(a, b, (((0,), (0,)), ((), ())), preferred_element_type=F32)  5.45 us
  transfers between devices with their start and end apart: 23, of which 16 were waited for; matrix products, arithmetic and copies ran while one was open for 5% of the time, Pallas kernels for 34%

profile of v2, /device:TPU:0, one launch (start us, length us, event | category | flops | bytes accessed | tf_op | source)
XLA Modules:
  0.0 175.5 jit_solution(12936997378011732584)
XLA Ops:
  1.3 3.0 %collective-permute-start.1 = (bf16[1,384]{1,0:T(2,128)(2,1)S(1)}, bf16[1,384]{1,0:T(2,128)(2,1)S(1)}, u32[]{:S(2)}, u32[]{:S(2)}) collective-permute-start(bf16[1,384]{1,0:T(2,128)(2,1)S(1)} %concatenate.56), channel_id=1, source_target_pairs={{0,1},{1,0},{2,3},{3,2},{4,5},{5,4},{6,7},{7,6},{8,9},{9,8},{10,11... | collective-permute-start | bytes 2312 | tf_op jit(solution)/shard_map/ppermute | solution.py:750
  19.2 4.3 %collective-permute-done.refs_1_ = bf16[1024,384]{1,0:T(8,128)(2,1)S(1)} collective-permute-done((bf16[1024,384]{1,0:T(8,128)(2,1)}, bf16[1024,384]{1,0:T(8,128)(2,1)S(1)}, u32[]{:S(2)}, u32[]{:S(2)}) %collective-permute-start) | collective-permute-done | bytes 786464 | tf_op jit(solution)/shard_map/ppermute | solution.py:750
  23.8 11.1 %project.1 = (bf16[1024,768]{1,0:T(8,128)(2,1)S(1)}, f32[1024,768]{1,0:T(8,128)S(1)}, bf16[1024,1024]{1,0:T(8,128)(2,1)S(1)}, bf16[1024,1024]{1,0:T(8,128)(2,1)S...) custom-call(s32[3]{0:T(128)S(1)} %pad_add_fusion.scalars, ...), custom_call_target="tpu_custom_call" | custom-call | flops 6000000000 | bytes 36000000 | tf_op jit(solution)/shard_map/project/pallas_call | solution.py:718
  35.0 7.1 %mix.1 = (f32[1024,768]{1,0:T(8,128)S(1)}, bf16[8,64,768]{2,1,0:T(8,128)(2,1)S(1)}) custom-call(s32[3]{0:T(128)S(1)} %pad_add_fusion.scalars, f32[1024,768]{1,0:T(8,128)S(1)} %get-tuple-element.134.refs_0_.refs_3_.refs_1_, bf16[1024,256]{1,0:T(8,128)(2,1)S(1)} %get-tuple-element.135.refs_1_.refs_8_.refs_2_, ...), custom_call_target="tpu_custom_call" | custom-call | flops 3500000000 | bytes 21000000 | tf_op jit(solution)/shard_map/mix/pallas_call | solution.py:718
  42.0 3.4 %gate.1 = (f32[1024,768]{1,0:T(8,128)S(1)}, bf16[1024,768]{1,0:T(8,128)(2,1)S(1)}, f32[8,1024]{1,0:T(8,128)S(1)}) custom-call(s32[3]{0:T(128)S(1)} %pad_add_fusion.scalars, f32[1024,768]{1,0:T(8,128)S(1)} %get-tuple-element.140.refs_0_.refs_2_, f32[1024,768]{1,0:T(8,128)S(1)} %get-tuple-element.141.refs_1_, ...), custom_call_target="tpu_custom_call" | custom-call | flops 1500000000 | bytes 9000000 | tf_op jit(solution)/shard_map/gate/pallas_call | solution.py:718
  45.5 1.7 collective-permute-start.3
  49.4 7.9 %gate_back.1 = (bf16[1024,768]{1,0:T(8,128)(2,1)S(1)}, bf16[1024,768]{1,0:T(8,128)(2,1)S(1)}, bf16[1024,768]{1,0:T(8,128)(2,1)S(1)}, f32[1024,128]{1,0:T(8,128)S...) custom-call(s32[3]{0:T(128)S(1)} %pad_add_fusion.scalars, ...), custom_call_target="tpu_custom_call" | custom-call | flops 4000000000 | bytes 24000000 | tf_op jit(solution)/shard_map/gate_back/pallas_call | solution.py:718
  61.8 2.8 %collective-permute-done.4 = bf16[768,768]{1,0:T(8,128)(2,1)S(1)} collective-permute-done((bf16[768,768]{1,0:T(8,128)(2,1)S(1)}, bf16[768,768]{1,0:T(8,128)(2,1)S(1)}, u32[]{:S(2)}, u32[]{:S(2)}) %collective-permute-start.4) | collective-permute-done | bytes 1179680 | tf_op jit(solution)/shard_map/ppermute | solution.py:755
  65.0 1.7 collective-permute-start.5
  68.8 5.8 %mix_back.4 = (bf16[1024,1024]{1,0:T(8,128)(2,1)S(1)}, f32[1024,512]{1,0:T(8,128)S(1)}, f32[8,1024]{1,0:T(8,128)S(1)}, f32[8,1024]{1,0:T(8,128)S(1)}, f32[8,1024]{1,0:T(8,128)S(1)}, /*index=5*/f32[64,768]{1,0:T(8,128)S(1)}) custom-call(s32[3]{0:T(128)S(1)} %pad_add_fusion.scalars, ...), custom_call_target="tpu_custom_call", output_to_operand_aliasing={{0}: (21, {}), {1}: (22, {}), {2}: (23, {})} | custom-call | flops 3000000000 | bytes 18000000 | tf_op jit(solution)/shard_map/mix_back/pallas_call | solution.py:718
  74.6 5.8 %mix_back.5 = (bf16[1024,1024]{1,0:T(8,128)(2,1)S(1)}, f32[1024,512]{1,0:T(8,128)S(1)}, f32[8,1024]{1,0:T(8,128)S(1)}, f32[8,1024]{1,0:T(8,128)S(1)}, f32[8,1024]{1,0:T(8,128)S(1)}, /*index=5*/f32[64,768]{1,0:T(8,128)S(1)}) custom-call(s32[3]{0:T(128)S(1)} %pad_add_fusion.scalars, ...), custom_call_target="tpu_custom_call", output_to_operand_aliasing={{0}: (21, {}), {1}: (22, {}), {2}: (23, {})} | custom-call | flops 3000000000 | bytes 18000000 | tf_op jit(solution)/shard_map/mix_back/pallas_call | solution.py:718
  80.6 1.8 %collective-permute-start.6 = (bf16[192,768]{1,0:T(8,128)(2,1)S(1)}, bf16[192,768]{1,0:T(8,128)(2,1)S(1)}, u32[]{:S(2)}, u32[]{:S(2)}) collective-permute-start(bf16[192,768]{1,0:T(8,128)(2,1)S(1)} %get-tuple-element.247), channel_id=1, source_target_pairs={{0,8},{2,10},{4,12},{6,14},{8,0},{10,2},{12,4},{14,6},{16,24},{18,... | collective-permute-start | bytes 884744 | tf_op jit(solution)/shard_map/ppermute | solution.py:755
  82.4 6.0 %mix_back.6 = (bf16[1024,1024]{1,0:T(8,128)(2,1)S(1)}, f32[1024,512]{1,0:T(8,128)S(1)}, f32[8,1024]{1,0:T(8,128)S(1)}, f32[8,1024]{1,0:T(8,128)S(1)}, f32[8,1024]{1,0:T(8,128)S(1)}, /*index=5*/f32[64,768]{1,0:T(8,128)S(1)}) custom-call(s32[3]{0:T(128)S(1)} %pad_add_fusion.scalars, ...), custom_call_target="tpu_custom_call", output_to_operand_aliasing={{0}: (21, {}), {1}: (22, {}), {2}: (23, {})} | custom-call | flops 3000000000 | bytes 18000000 | tf_op jit(solution)/shard_map/mix_back/pallas_call | solution.py:718
  89.2 2.7 %collective-permute-start.8 = (bf16[96,768]{1,0:T(8,128)(2,1)S(1)}, bf16[96,768]{1,0:T(8,128)(2,1)S(1)}, u32[]{:S(2)}, u32[]{:S(2)}) collective-permute-start(bf16[96,768]{1,0:T(8,128)(2,1)S(1)} %add_convert_fusion.10), channel_id=1, source_target_pairs={{0,16},{2,18},{4,20},{6,22},{8,24},{10,26},{12,28},{14,30},{16,0},... | collective-permute-start | bytes 442376 | tf_op jit(solution)/shard_map/ppermute | solution.py:755
  91.9 6.3 %mix_back.7 = (bf16[1024,1024]{1,0:T(8,128)(2,1)S(1)}, f32[1024,512]{1,0:T(8,128)S(1)}, f32[8,1024]{1,0:T(8,128)S(1)}, f32[8,1024]{1,0:T(8,128)S(1)}, f32[8,1024]{1,0:T(8,128)}, /*index=5*/f32[64,768]{1,0:T(8,128)}) custom-call(s32[3]{0:T(128)S(1)} %pad_add_fusion.scalars, ...), custom_call_target="tpu_custom_call", output_to_operand_aliasing={{0}: (21, {}), {1}: (22, {}), {2}: (23, {})} | custom-call | flops 3000000000 | bytes 18000000 | tf_op jit(solution)/shard_map/mix_back/pallas_call | solution.py:718
  100.7 2.4 %rates.1 = (bf16[1024,128]{1,0:T(8,128)(2,1)S(1)}, f32[8,128]{1,0:T(8,128)S(1)}, f32[8,1024]{1,0:T(8,128)S(1)}) custom-call(s32[3]{0:T(128)S(1)} %pad_add_fusion.scalars, f32[1024,512]{1,0:T(8,128)S(1)} %get-tuple-element.193.refs_0_, f32[1024,512]{1,0:T(8,128)S(1)} %get-tuple-element.136.refs_2_.refs_7_.refs_3_.refs_1_, ...), custom_call_target="tpu_custom_call" | custom-call | tf_op jit(solution)/shard_map/rates/pallas_call | solution.py:718
  105.2 3.7 %collective-permute-done.9 = bf16[96,768]{1,0:T(8,128)(2,1)S(1)} collective-permute-done((bf16[96,768]{1,0:T(8,128)(2,1)S(1)}, bf16[96,768]{1,0:T(8,128)(2,1)S(1)}, u32[]{:S(2)}, u32[]{:S(2)}) %collective-permute-start.9) | collective-permute-done | bytes 147488 | tf_op jit(solution)/shard_map/ppermute | solution.py:755
  109.0 2.4 %collective-permute-done.10 = bf16[576,768]{1,0:T(8,128)(2,1)S(1)} collective-permute-done((bf16[576,768]{1,0:T(8,128)(2,1)S(1)}, bf16[576,768]{1,0:T(8,128)(2,1)S(1)}, u32[]{:S(2)}, u32[]{:S(2)}) %collective-permute-start.10) | collective-permute-done | bytes 884768 | tf_op jit(solution)/shard_map/ppermute | solution.py:755
  112.5 2.8 %back_oth.1 = bf16[1040,384]{1,0:T(8,128)(2,1)S(1)} custom-call(s32[3]{0:T(128)S(1)} %pad_add_fusion.scalars, bf16[1024,768]{1,0:T(8,128)(2,1)S(1)} %get-tuple-element.153.dgp, bf16[1024,1024]{1,0:T(8,128)(2,1)S(1)} %get-tuple-element.210.rest, bf16[1024,128]{1,0:T(8,128)(2,1)S(1)} %get-tuple-element.196.dz, f32[8,1024]{1,0:T(8,128)S(1)} %get-tuple-element.209.rd, ...), custom_call_target="tpu_custom_call" | custom-call | tf_op jit(solution)/shard_map/back_oth/pallas_call | solution.py:735
  116.9 2.8 %back_own.1 = f32[1024,384]{1,0:T(8,128)S(1)} custom-call(s32[3]{0:T(128)S(1)} %pad_add_fusion.scalars, bf16[1024,768]{1,0:T(8,128)(2,1)S(1)} %get-tuple-element.153.dgp, bf16[1024,1024]{1,0:T(8,128)(2,1)S(1)} %get-tuple-element.210.rest, bf16[1024,128]{1,0:T(8,128)(2,1)S(1)} %get-tuple-element.196.dz, f32[8,1024]{1,0:T(8,128)S(1)} %get-tuple-element.209.rd, ...), custom_call_target="tpu_custom_call" | custom-call | tf_op jit(solution)/shard_map/back_own/pallas_call | solution.py:735
  121.3 2.6 %collective-permute-done.11 = bf16[288,768]{1,0:T(8,128)(2,1)S(1)} collective-permute-done((bf16[288,768]{1,0:T(8,128)(2,1)S(1)}, bf16[288,768]{1,0:T(8,128)(2,1)S(1)}, u32[]{:S(2)}, u32[]{:S(2)}) %collective-permute-start.11) | collective-permute-done | bytes 442400 | tf_op jit(solution)/shard_map/ppermute | solution.py:755
  126.9 3.8 %collective-permute-done.14 = bf16[144,768]{1,0:T(8,128)(2,1)S(1)} collective-permute-done((bf16[144,768]{1,0:T(8,128)(2,1)S(1)}, bf16[144,768]{1,0:T(8,128)(2,1)S(1)}, u32[]{:S(2)}, u32[]{:S(2)}) %collective-permute-start.14) | collective-permute-done | bytes 221216 | tf_op jit(solution)/shard_map/ppermute | solution.py:755
  131.4 3.6 %collective-permute-done.13 = bf16[1040,384]{1,0:T(8,128)(2,1)S(1)} collective-permute-done((bf16[1040,384]{1,0:T(8,128)(2,1)S(1)}, bf16[1040,384]{1,0:T(8,128)(2,1)S(1)}, u32[]{:S(2)}, u32[]{:S(2)}) %collective-permute-start.13) | collective-permute-done | bytes 798752 | tf_op jit(solution)/shard_map/ppermute | solution.py:750
  135.0 2.0 %fusion.2 = (f32[1024,384]{1,0:T(8,128)}, bf16[1024,384]{1,0:T(8,128)(2,1)}) fusion(bf16[1024,384]{1,0:T(8,128)(2,1)S(1)} %copy-done.1, f32[1024,384]{1,0:T(8,128)S(1)} %back_own.1, bf16[1024,384]{1,0:T(8,128)(2,1)S(1)} %copy-done.5, bf16[1040,384]{1,0:T(8,128)(2,1)S(1)} %collective-permute-done.13, f32[1024]{0:T(1024)S(1)} %get-tuple-element.240, ...), kind=kLoop, calls=%fused_computation.5 | loop fusion | flops 5505024 | bytes 8664576 | tf_op jit(solution)/shard_map/sub | solution.py:1171
  138.7 2.8 %collective-permute-done.16 = bf16[24,768]{1,0:T(8,128)(2,1)S(1)} collective-permute-done((bf16[24,768]{1,0:T(8,128)(2,1)S(1)}, bf16[24,768]{1,0:T(8,128)(2,1)S(1)}, u32[]{:S(2)}, u32[]{:S(2)}) %collective-permute-start.16) | collective-permute-done | bytes 36896 | tf_op jit(solution)/shard_map/ppermute | solution.py:750
  141.8 2.0 %collective-permute-start.18 = (bf16[72,768]{1,0:T(8,128)(2,1)S(1)}, bf16[72,768]{1,0:T(8,128)(2,1)S(1)}, u32[]{:S(2)}, u32[]{:S(2)}) collective-permute-start(bf16[72,768]{1,0:T(8,128)(2,1)S(1)} %pad_maximum_fusion.4), channel_id=1, source_target_pairs={{0,16},{2,18},{4,20},{6,22},{8,24},{10,26},{12,28},{14,30},{16,0},... | collective-permute-start | bytes 331784 | tf_op jit(solution)/shard_map/ppermute | solution.py:755
  143.9 6.7 %collective-permute-done.18 = bf16[72,768]{1,0:T(8,128)(2,1)S(1)} collective-permute-done((bf16[72,768]{1,0:T(8,128)(2,1)S(1)}, bf16[72,768]{1,0:T(8,128)(2,1)S(1)}, u32[]{:S(2)}, u32[]{:S(2)}) %collective-permute-start.18) | collective-permute-done | bytes 110624 | tf_op jit(solution)/shard_map/ppermute | solution.py:755
  150.7 3.0 %unpack_early.1 = (f32[768,768]{1,0:T(8,128)}, f32[768,768]{1,0:T(8,128)}) custom-call(s32[3]{0:T(128)S(1)} %pad_add_fusion.scalars, bf16[768,768]{1,0:T(8,128)(2,1)S(1)} %pad_maximum_fusion.first, bf16[768,768]{1,0:T(8,128)(2,1)S(1)} %collective-permute-done.20.second), custom_call_target="tpu_custom_call" | custom-call | tf_op jit(solution)/shard_map/unpack_early/pallas_call | solution.py:735
  153.7 3.9 %collective-permute-done.19 = bf16[144,768]{1,0:T(8,128)(2,1)S(1)} collective-permute-done((bf16[144,768]{1,0:T(8,128)(2,1)S(1)}, bf16[144,768]{1,0:T(8,128)(2,1)S(1)}, u32[]{:S(2)}, u32[]{:S(2)}) %collective-permute-start.19) | collective-permute-done | bytes 221216 | tf_op jit(solution)/shard_map/ppermute | solution.py:755
  158.6 10.0 %collective-permute-done.21 = bf16[288,768]{1,0:T(8,128)(2,1)S(1)} collective-permute-done((bf16[288,768]{1,0:T(8,128)(2,1)S(1)}, bf16[288,768]{1,0:T(8,128)(2,1)S(1)}, u32[]{:S(2)}, u32[]{:S(2)}) %collective-permute-start.21) | collective-permute-done | bytes 442400 | tf_op jit(solution)/shard_map/ppermute | solution.py:755
  168.7 2.4 %collective-permute-done.22.second = bf16[576,768]{1,0:T(8,128)(2,1)S(1)} collective-permute-done((bf16[576,768]{1,0:T(8,128)(2,1)S(1)}, bf16[576,768]{1,0:T(8,128)(2,1)S(1)}, u32[]{:S(2)}, u32[]{:S(2)}) %collective-permute-start.22) | collective-permute-done | bytes 884768 | tf_op jit(solution)/shard_map/ppermute | solution.py:755
  171.1 2.6 %unpack_late.1 = (f32[768,768]{1,0:T(8,128)}, f32[768,256]{1,0:T(8,128)}, f32[12,2,768]{2,1,0:T(2,128)}, f32[4,768]{1,0:T(4,128)}, f32[1,768]{1,0:T(1,128)S(1)},...) custom-call(s32[3]{0:T(128)S(1)} %pad_add_fusion.scalars, ...), custom_call_target="tpu_custom_call" | custom-call | tf_op jit(solution)/shard_map/unpack_late/pallas_call | solution.py:735
  (114 shorter events, 42.4 us)
Async XLA Ops:
  1.3 17.8 %collective-permute-start.1 = (bf16[1,384]{1,0:T(2,128)(2,1)S(1)}, bf16[1,384]{1,0:T(2,128)(2,1)S(1)}, u32[]{:S(2)}, u32[]{:S(2)}) collective-permute-start(bf16[1,384]{1,0:T(2,128)(2,1)S(1)} %concatenate.56), channel_id=1, source_target_pairs={{0,1},{1,0},{2,3},{3,2},{4,5},{5,4},{6,7},{7,6},{8,9},{9,8},{10,11... | collective-permute-start | bytes 2312 | tf_op jit(solution)/shard_map/ppermute | solution.py:750
  4.3 19.2 %collective-permute-start = (bf16[1024,384]{1,0:T(8,128)(2,1)}, bf16[1024,384]{1,0:T(8,128)(2,1)S(1)}, u32[]{:S(2)}, u32[]{:S(2)}) collective-permute-start(bf16[1024,384]{1,0:T(8,128)(2,1)} %refs_0_.1), channel_id=1, source_target_pairs={{0,1},{1,0},{2,3},{3,2},{4,5},{5,4},{6,7},{7,6},{8,9},{9,8},{10,11... | collective-permute-start | bytes 2359304 | tf_op jit(solution)/shard_map/ppermute | solution.py:750
  10.6 1.1 copy-start
  11.7 1.3 copy-start.2
  13.0 1.1 copy-start.4
  15.1 1.3 copy-start.7
  16.4 1.3 copy-start.8
  23.5 18.5 %collective-permute-start.2 = (bf16[1024,384]{1,0:T(8,128)(2,1)S(1)}, bf16[1024,384]{1,0:T(8,128)(2,1)S(1)}, u32[]{:S(2)}, u32[]{:S(2)}) collective-permute-start(bf16[1024,384]{1,0:T(8,128)(2,1)S(1)} %copy-done.4), channel_id=1, source_target_pairs={{0,1},{1,0},{2,3},{3,2},{4,5},{5,4},{6,7},{7,6},{8,9},{9,8},{10,11... | collective-permute-start | bytes 2359304 | tf_op jit(solution)/shard_map/ppermute | solution.py:750
  45.5 4.0 %collective-permute-start.3 = (f32[8,1024]{1,0:T(8,128)S(1)}, f32[8,1024]{1,0:T(8,128)S(1)}, u32[]{:S(2)}, u32[]{:S(2)}) collective-permute-start(f32[8,1024]{1,0:T(8,128)S(1)} %get-tuple-element.145), channel_id=1, source_target_pairs={{0,1},{1,0},{2,3},{3,2},{4,5},{5,4},{6,7},{7,6},{8,9},{9,8},{10,11... | collective-permute-start | bytes 98312 | tf_op jit(solution)/shard_map/ppermute | solution.py:750
  58.8 1.5 copy-start.3
  61.7 2.9 %collective-permute-start.4 = (bf16[768,768]{1,0:T(8,128)(2,1)S(1)}, bf16[768,768]{1,0:T(8,128)(2,1)S(1)}, u32[]{:S(2)}, u32[]{:S(2)}) collective-permute-start(bf16[768,768]{1,0:T(8,128)(2,1)S(1)} %get-tuple-element.155), channel_id=1, source_target_pairs={{0,2},{2,0},{4,6},{6,4},{8,10},{10,8},{12,14},{14,12},{16,18},{18,... | collective-permute-start | bytes 3538952 | tf_op jit(solution)/shard_map/ppermute | solution.py:755
  65.0 15.5 %collective-permute-start.5 = (bf16[384,768]{1,0:T(8,128)(2,1)S(1)}, bf16[384,768]{1,0:T(8,128)(2,1)S(1)}, u32[]{:S(2)}, u32[]{:S(2)}) collective-permute-start(bf16[384,768]{1,0:T(8,128)(2,1)S(1)} %get-tuple-element.243), channel_id=1, source_target_pairs={{0,4},{2,6},{4,0},{6,2},{8,12},{10,14},{12,8},{14,10},{16,20},{18,... | collective-permute-start | bytes 1769480 | tf_op jit(solution)/shard_map/ppermute | solution.py:755
  66.7 21.7 %collective-permute-start.7 = (bf16[1024,384]{1,0:T(8,128)(2,1)S(1)}, bf16[1024,384]{1,0:T(8,128)(2,1)S(1)}, u32[]{:S(2)}, u32[]{:S(2)}) collective-permute-start(bf16[1024,384]{1,0:T(8,128)(2,1)S(1)} %branch_oth.1), channel_id=1, source_target_pairs={{0,1},{1,0},{2,3},{3,2},{4,5},{5,4},{6,7},{7,6},{8,9},{9,8},{10,11... | collective-permute-start | bytes 2359304 | tf_op jit(solution)/shard_map/ppermute | solution.py:750
  80.6 8.6 %collective-permute-start.6 = (bf16[192,768]{1,0:T(8,128)(2,1)S(1)}, bf16[192,768]{1,0:T(8,128)(2,1)S(1)}, u32[]{:S(2)}, u32[]{:S(2)}) collective-permute-start(bf16[192,768]{1,0:T(8,128)(2,1)S(1)} %get-tuple-element.247), channel_id=1, source_target_pairs={{0,8},{2,10},{4,12},{6,14},{8,0},{10,2},{12,4},{14,6},{16,24},{18,... | collective-permute-start | bytes 884744 | tf_op jit(solution)/shard_map/ppermute | solution.py:755
  89.2 8.9 %collective-permute-start.8 = (bf16[96,768]{1,0:T(8,128)(2,1)S(1)}, bf16[96,768]{1,0:T(8,128)(2,1)S(1)}, u32[]{:S(2)}, u32[]{:S(2)}) collective-permute-start(bf16[96,768]{1,0:T(8,128)(2,1)S(1)} %add_convert_fusion.10), channel_id=1, source_target_pairs={{0,16},{2,18},{4,20},{6,22},{8,24},{10,26},{12,28},{14,30},{16,0},... | collective-permute-start | bytes 442376 | tf_op jit(solution)/shard_map/ppermute | solution.py:755
  100.3 8.6 %collective-permute-start.9 = (bf16[96,768]{1,0:T(8,128)(2,1)S(1)}, bf16[96,768]{1,0:T(8,128)(2,1)S(1)}, u32[]{:S(2)}, u32[]{:S(2)}) collective-permute-start(bf16[96,768]{1,0:T(8,128)(2,1)S(1)} %add_convert_fusion.8), channel_id=1, source_target_pairs={{0,16},{2,18},{4,20},{6,22},{8,24},{10,26},{12,28},{14,30},{16,0},... | collective-permute-start | bytes 442376 | tf_op jit(solution)/shard_map/ppermute | solution.py:755
  105.1 7.4 %copy-start.9 = (bf16[384]{0:T(512)(128)(2,1)S(1)}, bf16[384]{0:T(512)(128)(2,1)}, u32[]{:S(2)}) copy-start(bf16[384]{0:T(512)(128)(2,1)} %param.18) | copy-start | bytes 2308
  108.9 2.5 %collective-permute-start.10 = (bf16[576,768]{1,0:T(8,128)(2,1)S(1)}, bf16[576,768]{1,0:T(8,128)(2,1)S(1)}, u32[]{:S(2)}, u32[]{:S(2)}) collective-permute-start(bf16[576,768]{1,0:T(8,128)(2,1)S(1)} %get-tuple-element.205), channel_id=1, source_target_pairs={{0,2},{2,0},{4,6},{6,4},{8,10},{10,8},{12,14},{14,12},{16,18},{18,... | collective-permute-start | bytes 2654216 | tf_op jit(solution)/shard_map/ppermute | solution.py:755
  111.6 12.3 %collective-permute-start.11 = (bf16[288,768]{1,0:T(8,128)(2,1)S(1)}, bf16[288,768]{1,0:T(8,128)(2,1)S(1)}, u32[]{:S(2)}, u32[]{:S(2)}) collective-permute-start(bf16[288,768]{1,0:T(8,128)(2,1)S(1)} %get-tuple-element.207), channel_id=1, source_target_pairs={{0,4},{2,6},{4,0},{6,2},{8,12},{10,14},{12,8},{14,10},{16,20},{18,... | collective-permute-start | bytes 1327112 | tf_op jit(solution)/shard_map/ppermute | solution.py:755
  112.5 8.8 %collective-permute-start.12 = (bf16[192,768]{1,0:T(8,128)(2,1)S(1)}, bf16[192,768]{1,0:T(8,128)(2,1)S(1)}, u32[]{:S(2)}, u32[]{:S(2)}) collective-permute-start(bf16[192,768]{1,0:T(8,128)(2,1)S(1)} %pad_maximum_fusion.3), channel_id=1, source_target_pairs={{0,8},{2,10},{4,12},{6,14},{8,0},{10,2},{12,4},{14,6},{16,24},{18,... | collective-permute-start | bytes 884744 | tf_op jit(solution)/shard_map/ppermute | solution.py:755
  115.4 19.6 %collective-permute-start.13 = (bf16[1040,384]{1,0:T(8,128)(2,1)S(1)}, bf16[1040,384]{1,0:T(8,128)(2,1)S(1)}, u32[]{:S(2)}, u32[]{:S(2)}) collective-permute-start(bf16[1040,384]{1,0:T(8,128)(2,1)S(1)} %back_oth.1), channel_id=1, source_target_pairs={{0,1},{1,0},{2,3},{3,2},{4,5},{5,4},{6,7},{7,6},{8,9},{9,8},{10,11... | collective-permute-start | bytes 2396168 | tf_op jit(solution)/shard_map/ppermute | solution.py:750
  124.0 6.7 %collective-permute-start.14 = (bf16[144,768]{1,0:T(8,128)(2,1)S(1)}, bf16[144,768]{1,0:T(8,128)(2,1)S(1)}, u32[]{:S(2)}, u32[]{:S(2)}) collective-permute-start(bf16[144,768]{1,0:T(8,128)(2,1)S(1)} %get-tuple-element.217), channel_id=1, source_target_pairs={{0,8},{2,10},{4,12},{6,14},{8,0},{10,2},{12,4},{14,6},{16,24},{18,... | collective-permute-start | bytes 663560 | tf_op jit(solution)/shard_map/ppermute | solution.py:755
  124.1 2.4 %copy-start.1 = (bf16[1024,384]{1,0:T(8,128)(2,1)S(1)}, bf16[1024,384]{1,0:T(8,128)(2,1)}, u32[]{:S(2)}) copy-start(bf16[1024,384]{1,0:T(8,128)(2,1)} %refs_0_.1) | copy-start | bytes 2359300
  124.2 17.5 %collective-permute-start.17 = (bf16[384,768]{1,0:T(8,128)(2,1)S(1)}, bf16[384,768]{1,0:T(8,128)(2,1)S(1)}, u32[]{:S(2)}, u32[]{:S(2)}) collective-permute-start(bf16[384,768]{1,0:T(8,128)(2,1)S(1)} %pad_maximum_fusion.1), channel_id=1, source_target_pairs={{0,4},{2,6},{4,0},{6,2},{8,12},{10,14},{12,8},{14,10},{16,20},{18,... | collective-permute-start | bytes 1769480 | tf_op jit(solution)/shard_map/ppermute | solution.py:755
  126.5 8.5 %copy-start.5 = (bf16[1024,384]{1,0:T(8,128)(2,1)S(1)}, bf16[1024,384]{1,0:T(8,128)(2,1)}, u32[]{:S(2)}) copy-start(bf16[1024,384]{1,0:T(8,128)(2,1)} %refs_1_.1) | copy-start | bytes 2359300
  130.8 6.7 %collective-permute-start.15 = (bf16[72,768]{1,0:T(8,128)(2,1)S(1)}, bf16[72,768]{1,0:T(8,128)(2,1)S(1)}, u32[]{:S(2)}, u32[]{:S(2)}) collective-permute-start(bf16[72,768]{1,0:T(8,128)(2,1)S(1)} %add_convert_fusion.12), channel_id=1, source_target_pairs={{0,16},{2,18},{4,20},{6,22},{8,24},{10,26},{12,28},{14,30},{16,0},... | collective-permute-start | bytes 331784 | tf_op jit(solution)/shard_map/ppermute | solution.py:755
  137.5 4.0 %collective-permute-start.16 = (bf16[24,768]{1,0:T(8,128)(2,1)S(1)}, bf16[24,768]{1,0:T(8,128)(2,1)S(1)}, u32[]{:S(2)}, u32[]{:S(2)}) collective-permute-start(bf16[24,768]{1,0:T(8,128)(2,1)S(1)} %slice.159), channel_id=1, source_target_pairs={{0,1},{1,0},{2,3},{3,2},{4,5},{5,4},{6,7},{7,6},{8,9},{9,8},{10,11... | collective-permute-start | bytes 110600 | tf_op jit(solution)/shard_map/ppermute | solution.py:750
  141.7 8.9 %collective-permute-start.20 = (bf16[768,768]{1,0:T(8,128)(2,1)S(1)}, bf16[768,768]{1,0:T(8,128)(2,1)S(1)}, u32[]{:S(2)}, u32[]{:S(2)}) collective-permute-start(bf16[768,768]{1,0:T(8,128)(2,1)S(1)} %pad_maximum_fusion.first), channel_id=1, source_target_pairs={{0,2},{2,0},{4,6},{6,4},{8,10},{10,8},{12,14},{14,12},{16,18},{18,... | collective-permute-start | bytes 3538952 | tf_op jit(solution)/shard_map/ppermute | solution.py:755
  141.8 8.7 %collective-permute-start.18 = (bf16[72,768]{1,0:T(8,128)(2,1)S(1)}, bf16[72,768]{1,0:T(8,128)(2,1)S(1)}, u32[]{:S(2)}, u32[]{:S(2)}) collective-permute-start(bf16[72,768]{1,0:T(8,128)(2,1)S(1)} %pad_maximum_fusion.4), channel_id=1, source_target_pairs={{0,16},{2,18},{4,20},{6,22},{8,24},{10,26},{12,28},{14,30},{16,0},... | collective-permute-start | bytes 331784 | tf_op jit(solution)/shard_map/ppermute | solution.py:755
  150.6 7.1 %collective-permute-start.19 = (bf16[144,768]{1,0:T(8,128)(2,1)S(1)}, bf16[144,768]{1,0:T(8,128)(2,1)S(1)}, u32[]{:S(2)}, u32[]{:S(2)}) collective-permute-start(bf16[144,768]{1,0:T(8,128)(2,1)S(1)} %get-tuple-element.252), channel_id=1, source_target_pairs={{0,8},{2,10},{4,12},{6,14},{8,0},{10,2},{12,4},{14,6},{16,24},{18,... | collective-permute-start | bytes 663560 | tf_op jit(solution)/shard_map/ppermute | solution.py:755
  157.7 10.9 %collective-permute-start.21 = (bf16[288,768]{1,0:T(8,128)(2,1)S(1)}, bf16[288,768]{1,0:T(8,128)(2,1)S(1)}, u32[]{:S(2)}, u32[]{:S(2)}) collective-permute-start(bf16[288,768]{1,0:T(8,128)(2,1)S(1)} %pad_maximum_fusion.2), channel_id=1, source_target_pairs={{0,4},{2,6},{4,0},{6,2},{8,12},{10,14},{12,8},{14,10},{16,20},{18,... | collective-permute-start | bytes 1327112 | tf_op jit(solution)/shard_map/ppermute | solution.py:755
  168.6 2.5 %collective-permute-start.22 = (bf16[576,768]{1,0:T(8,128)(2,1)S(1)}, bf16[576,768]{1,0:T(8,128)(2,1)S(1)}, u32[]{:S(2)}, u32[]{:S(2)}) collective-permute-start(bf16[576,768]{1,0:T(8,128)(2,1)S(1)} %constant_dynamic-update-slice_fusion.2.first), channel_id=1, source_target_pairs={{0,2},{2,0},{4,6},{6,4},{8,10},{10,8},{12,14},{14,12},{16,18},{18,... | collective-permute-start | bytes 2654216 | tf_op jit(solution)/shard_map/ppermute | solution.py:755
  (1 other events, 1.0 us)

commit v3 on v2

--- a/solution.py
+++ b/solution.py
@@ -9,7 +9,7 @@
 
 EPSILON = 1e-05
 CHUNK = 128
-PROJECT_BLOCK, MIX_BLOCK, GATE_BLOCK, BACK_BLOCK = 256, 256, 256, 128
+PROJECT_BLOCK, MIX_BLOCK, GATE_BLOCK, BACK_BLOCK, RATES_BLOCK = 256, 256, 256, 128, 512
 LANES = 128
 F32 = jnp.float32
 BF16 = jnp.bfloat16
@@ -547,6 +547,13 @@
     return j
 
 
+def lanes_in(orders, width):
+    size = width // len(orders)
+    return [
+        (r, slice(k * size, (k + 1) * size), order) for k, order in enumerate(orders) for r in range(SHARDS)
+    ]
+
+
 def pack_early_kernel(
     scalars, grad_out, grad_gate, w_gate, keep_ref, send_ref, gain_ref, *, order
 ):
@@ -576,7 +583,7 @@
 
 def pack_late_kernel(
     scalars, inner, state, step_low, w_inner, w_state_t, gain, gain_part, gconv, ghead, small, gather,
-    keep_ref, send_ref, misc, *, order, heads, state_width,
+    keep_ref, send_ref, misc, *, orders, heads, state_width,
 ):
     model, width = w_inner.shape
     hi, lo = split_two(inner[...].astype(F32) * w_inner[...].astype(F32))
@@ -615,37 +622,41 @@
     part = model // SHARDS
     part_s = state_width // SHARDS
     rows = part + part_s + 8
-    for r in range(SHARDS):
+    for r, cols, order in lanes_in(orders, model):
         j = home_of(r, scalars[2], order)
         out = keep_ref if r < SHARDS // 2 else send_ref
         at = (r % (SHARDS // 2)) * rows
-        out[at : at + part, :] = inner[pl.ds(pl.multiple_of(j * part, part), part), :]
-        out[at + part : at + part + part_s, :] = state[
-            pl.ds(pl.multiple_of(j * part_s, part_s), part_s), :
+        out[at : at + part, cols] = inner[pl.ds(pl.multiple_of(j * part, part), part), cols]
+        out[at + part : at + part + part_s, cols] = state[
+            pl.ds(pl.multiple_of(j * part_s, part_s), part_s), cols
         ]
-        out[at + part + part_s : at + rows, :] = misc[
-            pl.ds(pl.multiple_of(j * 8, 8), 8), :
+        out[at + part + part_s : at + rows, cols] = misc[
+            pl.ds(pl.multiple_of(j * 8, 8), 8), cols
         ].astype(BF16)
 
 
 def unpack_late_kernel(
     scalars, first, second, inner_ref, state_ref, step_ref, convi_ref, convi_b_ref, convs_ref, convs_b_ref,
-    gg_ref, bias_ref, decay_ref, skip_ref, gain_ref, state, misc, *, order, heads,
+    gg_ref, bias_ref, decay_ref, skip_ref, gain_ref, state, misc, *, orders, heads,
 ):
     model = inner_ref.shape[0]
     state_width = state_ref.shape[1]
     part = model // SHARDS
     part_s = state_width // SHARDS
     rows = part + part_s + 8
-    for r in range(SHARDS):
+    for r, cols, order in lanes_in(orders, model):
         j = home_of(r, scalars[2], order)
         src = first if r < SHARDS // 2 else second
         at = (r % (SHARDS // 2)) * rows
-        inner_ref[pl.ds(pl.multiple_of(j * part, part), part), :] = src[at : at + part, :].astype(F32)
-        state[pl.ds(pl.multiple_of(j * part_s, part_s), part_s), :] = src[
-            at + part : at + part + part_s, :
+        inner_ref[pl.ds(pl.multiple_of(j * part, part), part), cols] = src[at : at + part, cols].astype(
+            F32
+        )
+        state[pl.ds(pl.multiple_of(j * part_s, part_s), part_s), cols] = src[
+            at + part : at + part + part_s, cols
         ].astype(F32)
-        misc[pl.ds(pl.multiple_of(j * 8, 8), 8), :] = src[at + part + part_s : at + rows, :].astype(F32)
+        misc[pl.ds(pl.multiple_of(j * 8, 8), 8), cols] = src[at + part + part_s : at + rows, cols].astype(
+            F32
+        )
     state_ref[...] = jnp.transpose(state[...])
 
     def single(k):
@@ -658,8 +669,8 @@
     at = 2 * heads
     for k in range(4):
         convi_ref[k : k + 1, :] = single(at + k)
-    convi_b_ref[...] = single(at + 4)
-    gg_ref[...] = single(at + 5)
+    convi_b_ref[...] = single(at + 4).reshape(convi_b_ref.shape)
+    gg_ref[...] = single(at + 5).reshape(gg_ref.shape)
     head_row = single(at + 6)
     for d in range(2):
         decay_ref[d : d + 1, :] = head_row[:, d * heads : (d + 1) * heads]
@@ -675,7 +686,7 @@
     half = model // 2
     gain_ref[...] = jnp.where(
         scalars[1] == 0, misc[at : at + 1, :half], misc[at : at + 1, half:]
-    )
+    ).reshape(gain_ref.shape)
 
 
 def place(i, top):
@@ -1019,7 +1030,7 @@
             aliases={len(ins) - 3: 0, len(ins) - 2: 1, len(ins) - 1: 2},
         )
 
-    order_a, order_b = (0, 1, 2, 3), (0, 1, 2, 3)
+    order_a, orders_b = (0, 1, 2, 3), ((0, 1, 2, 3), (0, 2, 1, 3))
     grad_out = mm_tn(gz, dbr).astype(BF16)
     grad_gate = mm_tn(normed, dgp).astype(BF16)
     keep, send, gain_part = whole(
@@ -1080,7 +1091,7 @@
                 x = rest_of_dp(add_low(keep, sent))
         state = (ext_carry, carry, gconv, rest, rates, rd_rest)
 
-    block = GATE_BLOCK
+    block = RATES_BLOCK
     rates, x, rest = lax.optimization_barrier((rates, x, rest))
     sent = swap_dp(x, order_a[3])
     dz, ghead, rd_part = call(
@@ -1103,7 +1114,7 @@
     grad_state = mm_tn(rest[:, width:], normed).astype(BF16)
     grad_step = mm_tn(dz, normed).astype(BF16)
     keep, send = whole(
-        partial(pack_late_kernel, order=order_b, heads=heads, state_width=state_width),
+        partial(pack_late_kernel, orders=orders_b, heads=heads, state_width=state_width),
         (
             scalars, grad_inner, grad_state, grad_step, inner_v, w_state_t, gain, gain_part, gconv, ghead,
             small, gather,
@@ -1113,50 +1124,62 @@
         "pack_late",
     )
 
-    def halve_with(keep, send, bit, *work):
-        got = after(swap_dp(send, bit), *work)
-        h = keep.shape[0] // 2
-        return add_low(keep[:h], got[:h]), add_low(keep[h:], got[h:])
-
-    x = jnp.concatenate([x, sent])
-    send, x = lax.optimization_barrier((send, x))
-    keep, send = halve_with(keep, send, order_b[0])
-    send, x, rest = lax.optimization_barrier((send, x, rest))
     back_args = (scalars, dgp, rest, dz, rd_part, gate_v, inner_v, state_v, step_weight)
     dn_oth = whole(
         partial(back_project_kernel, other=True), back_args, [low(rows + 16, width_own)], [], "back_oth"
     )[0]
+    x = jnp.concatenate([x, sent])
+    send, x, dn_oth = lax.optimization_barrier((send, x, dn_oth))
+    got = swap_dp(send, 0)
+    sent = swap_dp(x, order_a[2])
+    h, c = keep.shape[0] // 2, model // 2
+    keeps = [add_low(keep[:h, :c], got[:h, :c]), add_low(keep[:h, c:], got[:h, c:])]
+    sends = [add_low(keep[h:, :c], got[h:, :c]), add_low(keep[h:, c:], got[h:, c:])]
+    sends[0], sends[1], rest, gz_late = lax.optimization_barrier((sends[0], sends[1], rest, gz))
     dn_got = swap_mp(dn_oth)
 
-    sent = swap_dp(x, order_a[2])
     dn_own = whole(
-        partial(back_project_kernel, other=False), (*back_args[:2], after(rest, dn_oth), *back_args[3:]), [full(rows, width_own)], [], "back_own"
+        partial(back_project_kernel, other=False), (*back_args[:2], rest, *back_args[3:]),
+        [full(rows, width_own)], [], "back_own"
     )[0]
-    keep, send = halve_with(keep, send, order_b[1], dn_own)
-    x = jnp.concatenate([x, sent])
-    send, x, gz_late, tokens_late, oth_late = lax.optimization_barrier((send, x, gz, tokens, oth_tokens))
-
+    branch_own = whole(
+        partial(branch_kernel, other=False), (scalars, gz_late, out_v), [full(rows, width_own)], [],
+        "branch_own"
+    )[0]
+    for level in (1, 2):
+        gots = [swap_dp(v, order[level]) for v, order in zip(sends, orders_b)]
+        if level == 1:
+            gots[0], gots[1], dn_own, branch_own = lax.optimization_barrier(
+                (gots[0], gots[1], dn_own, branch_own)
+            )
+        else:
+            x = jnp.concatenate([x, sent])
+            gots[0], gots[1], x = lax.optimization_barrier((gots[0], gots[1], x))
+        h = keeps[0].shape[0] // 2
+        pairs = list(zip(keeps, gots))
+        if level == 1:
+            keeps = [add_low(k[:h], v[:h]) for k, v in pairs]
+            sends = [add_low(k[h:], v[h:]) for k, v in pairs]
+        else:
+            keep = jnp.concatenate([add_low(k[:h], v[:h]) for k, v in pairs], axis=1)
+            send = jnp.concatenate([add_low(k[h:], v[h:]) for k, v in pairs], axis=1)
+    send, x, tokens_late, oth_late = lax.optimization_barrier((send, x, tokens, oth_tokens))
     sent = swap_dp(x, order_a[1])
-    branch_own = whole(
-        partial(branch_kernel, other=False), (scalars, gz_late, out_v), [full(rows, width_own)], [], "branch_own"
-    )[0]
-    keep, send = halve_with(keep, send, order_b[2], branch_own)
 
     seq_mask = (jnp.arange(rows) < lengths[0]).astype(F32)[:, None]
     gate_inv = lax.rsqrt(sums[0] / inner_width + EPSILON)[:, None]
     tokens_f = tokens_late.astype(F32)
     block_out = (tokens_f + seq_mask * gate_inv * (branch_own + branch_got.astype(F32))).astype(BF16)
-    z = rest_of_dp(add_low(keep, after(swap_dp(send, order_b[3]), block_out, dn_got)))
+
+    got, block_out, dn_got = lax.optimization_barrier((swap_dp(send, 3), block_out, dn_got))
+    z = rest_of_dp(add_low(keep, got))
     part = model // SHARDS
     tail = z[part:]
     tail_row = lax.broadcasted_iota(jnp.int32, (LATE_ROWS - part, 1), 0)
     alone = (tail_row >= LATE_ROWS - part - 8) & (tail_row < LATE_ROWS - part - 4)
     tail_f = tail.astype(F32)
     tail = jnp.where(alone, tail_f, tail_f + swap_mp(tail).astype(F32)).astype(BF16)
-    x = jnp.concatenate([x, sent])
-    z, x = lax.optimization_barrier((jnp.concatenate([z[:part], tail]), x))
-    sent = swap_dp(x, order_a[0])
-
+    z = jnp.concatenate([z[:part], tail])
     oth_f = oth_late.astype(F32)
     square = jnp.sum(tokens_f * tokens_f, axis=1, keepdims=True) + jnp.sum(
         oth_f * oth_f, axis=1, keepdims=True
@@ -1173,17 +1196,24 @@
         - tokens_f * (inv * inv * (rd_both[:, None] / model))
     )
 
-    z = jnp.concatenate([z, after(swap_dp(z, order_b[3]), grad_tokens)])
+    x = jnp.concatenate([x, sent])
+    got, grad_tokens, x = lax.optimization_barrier((swap_dp(z, 3), grad_tokens, x))
+    sent = swap_dp(x, order_a[0])
+    z = jnp.concatenate([z, got])
+    zs = [z[:, :c], z[:, c:]]
+    gots = [swap_dp(v, order[2]) for v, order in zip(zs, orders_b)]
+    zs = [jnp.concatenate([v, g]) for v, g in zip(zs, gots)]
     grad_proj_out, grad_proj_gate = whole(
         partial(unpack_early_kernel, order=order_a),
-        (scalars, x, after(sent, z)),
+        (scalars, x, after(sent, *zs)),
         [full(width, model), full(model, width)],
         [],
         "unpack_early",
         in_vmem=False,
     )
-    z = jnp.concatenate([z, after(swap_dp(z, order_b[2]), grad_proj_out)])
-    z = jnp.concatenate([z, swap_dp(z, order_b[1])])
+    gots = [swap_dp(v, order[1]) for v, order in zip(zs, orders_b)]
+    gots[0], gots[1], grad_proj_out = lax.optimization_barrier((gots[0], gots[1], grad_proj_out))
+    z = jnp.concatenate([jnp.concatenate([v, g]) for v, g in zip(zs, gots)], axis=1)
     (
         grad_proj_inner,
         grad_proj_state,
@@ -1198,21 +1228,21 @@
         grad_skip,
         grad_norm_gain,
     ) = whole(
-        partial(unpack_late_kernel, order=order_b, heads=heads),
-        (scalars, z, swap_dp(z, order_b[0])),
+        partial(unpack_late_kernel, orders=orders_b, heads=heads),
+        (scalars, z, swap_dp(z, 0)),
         [
             full(model, width),
             full(model, state_width),
             full(heads, 2, model),
             full(4, width),
-            full(1, width),
+            full(width),
             full(4, state_width),
             full(1, state_width),
-            full(1, width),
+            full(width),
             full(2, heads),
             full(2, heads),
             full(1, heads),
-            full(1, width_own),
+            full(width_own),
         ],
         [pltpu.VMEM((state_width, model), F32), pltpu.VMEM((8 * SHARDS, model), F32)],
         "unpack_late",
@@ -1221,19 +1251,19 @@
     return (
         block_out,
         grad_tokens,
-        grad_norm_gain[0],
+        grad_norm_gain,
         grad_proj_gate,
         grad_proj_inner,
         grad_proj_state,
         step.transpose(2, 1, 0),
         grad_conv_inner,
-        grad_conv_inner_bias[0],
+        grad_conv_inner_bias,
         grad_conv_state,
         grad_conv_state_bias[0],
         grad_step_bias,
         grad_decay_log,
         grad_skip[0],
-        grad_gate_gain[0],
+        grad_gate_gain,
         grad_proj_out,
     )
 

time: 176 us -> 167 us (0.949)
  waiting for transfers between devices: 52.6 us -> 39.6 us
  starting transfers between devices: 21.6 us -> 26.9 us
    ppermute x16 -> x20, waiting for transfers between devices: 41.1 us -> 32.2 us  [swap_dp(): return lax.ppermute(x, 'dp', [(i, i ^ 1 << bit) for i in range(size)])]
    ppermute x16 -> x20, starting transfers between devices: 12.3 us -> 17.2 us  [swap_dp(): return lax.ppermute(x, 'dp', [(i, i ^ 1 << bit) for i in range(size)])]
    ppermute x7, waiting for transfers between devices: 11.5 us -> 7.33 us  [swap_mp(): return lax.ppermute(x, 'mp', [(0, 1), (1, 0)])]
    pallas_call x3 -> x0, other arithmetic: 1.81 us -> none  [whole(): pl.pallas_call(kernel, out_shape=[pltpu.VMEM(o.shape, o.dtype) if in_vmem...]
    unnamed x24 -> x22, local copies, waits for them, and re-layouts: 7.9 us -> 7.87 us
  transfers between devices with their start and end apart: 23 -> 27, of which waited for: 16 -> 19; matrix products, arithmetic and copies ran while one was open for 5% -> 6% of each run, Pallas kernels for 34% -> 35%
where the time goes in v3:
time: 167 us
  Pallas kernels  74.3 us (44%)
  waiting for transfers between devices  39.6 us (24%)
  starting transfers between devices  26.9 us (16%)
  local copies, waits for them, and re-layouts  11.6 us (7%)
  other arithmetic  7 us (4%)
  matrix products  5.44 us (3%)
  between operations  1.96 us (1%)
    pallas_call x9, Pallas kernels, call(): pl.pallas_call(looped, out_shape=[pltpu.VMEM(o.shape, o.dtype) for o in o...  55.3 us
    ppermute x20, waiting for transfers between devices, swap_dp(): return lax.ppermute(x, 'dp', [(i, i ^ 1 << bit) for i in range(size)])  32.2 us
    pallas_call x8, Pallas kernels, whole(): pl.pallas_call(kernel, out_shape=[pltpu.VMEM(o.shape, o.dtype) if in_vmem...  17.5 us
    ppermute x20, starting transfers between devices, swap_dp(): return lax.ppermute(x, 'dp', [(i, i ^ 1 << bit) for i in range(size)])  17.2 us
    ppermute x7, starting transfers between devices, swap_mp(): return lax.ppermute(x, 'mp', [(0, 1), (1, 0)])  9.72 us
    unnamed x22, local copies, waits for them, and re-layouts  7.87 us
    ppermute x7, waiting for transfers between devices, swap_mp(): return lax.ppermute(x, 'mp', [(0, 1), (1, 0)])  7.33 us
    dot_general x5, matrix products, mm_tn(): lax.dot_general(a, b, (((0,), (0,)), ((), ())), preferred_element_type=F32)  5.44 us
  transfers between devices with their start and end apart: 27, of which 19 were waited for; matrix products, arithmetic and copies ran while one was open for 6% of the time, Pallas kernels for 35%

profile of v3, /device:TPU:0, one launch (start us, length us, event | category | flops | bytes accessed | tf_op | source)
XLA Modules:
  0.0 166.8 jit_solution(13381259536925549529)
XLA Ops:
  1.3 3.0 %collective-permute-start.1 = (bf16[1,384]{1,0:T(2,128)(2,1)S(1)}, bf16[1,384]{1,0:T(2,128)(2,1)S(1)}, u32[]{:S(2)}, u32[]{:S(2)}) collective-permute-start(bf16[1,384]{1,0:T(2,128)(2,1)S(1)} %concatenate.72), channel_id=1, source_target_pairs={{0,1},{1,0},{2,3},{3,2},{4,5},{5,4},{6,7},{7,6},{8,9},{9,8},{10,11... | collective-permute-start | bytes 2312 | tf_op jit(solution)/shard_map/ppermute | solution.py:761
  19.2 4.3 %collective-permute-done.refs_1_ = bf16[1024,384]{1,0:T(8,128)(2,1)S(1)} collective-permute-done((bf16[1024,384]{1,0:T(8,128)(2,1)}, bf16[1024,384]{1,0:T(8,128)(2,1)S(1)}, u32[]{:S(2)}, u32[]{:S(2)}) %collective-permute-start) | collective-permute-done | bytes 786464 | tf_op jit(solution)/shard_map/ppermute | solution.py:761
  23.8 11.1 %project.1 = (bf16[1024,768]{1,0:T(8,128)(2,1)S(1)}, f32[1024,768]{1,0:T(8,128)S(1)}, bf16[1024,1024]{1,0:T(8,128)(2,1)S(1)}, bf16[1024,1024]{1,0:T(8,128)(2,1)S...) custom-call(s32[3]{0:T(128)S(1)} %pad_add_fusion.scalars, ...), custom_call_target="tpu_custom_call" | custom-call | flops 6000000000 | bytes 36000000 | tf_op jit(solution)/shard_map/project/pallas_call | solution.py:729
  35.0 7.1 %mix.1 = (f32[1024,768]{1,0:T(8,128)S(1)}, bf16[8,64,768]{2,1,0:T(8,128)(2,1)S(1)}) custom-call(s32[3]{0:T(128)S(1)} %pad_add_fusion.scalars, f32[1024,768]{1,0:T(8,128)S(1)} %get-tuple-element.143.refs_0_.refs_3_.refs_1_, bf16[1024,256]{1,0:T(8,128)(2,1)S(1)} %get-tuple-element.144.refs_1_.refs_8_.refs_2_, ...), custom_call_target="tpu_custom_call" | custom-call | flops 3500000000 | bytes 21000000 | tf_op jit(solution)/shard_map/mix/pallas_call | solution.py:729
  42.0 3.4 %gate.1 = (f32[1024,768]{1,0:T(8,128)S(1)}, bf16[1024,768]{1,0:T(8,128)(2,1)S(1)}, f32[8,1024]{1,0:T(8,128)S(1)}) custom-call(s32[3]{0:T(128)S(1)} %pad_add_fusion.scalars, f32[1024,768]{1,0:T(8,128)S(1)} %get-tuple-element.149.refs_0_.refs_2_, f32[1024,768]{1,0:T(8,128)S(1)} %get-tuple-element.150.refs_1_, ...), custom_call_target="tpu_custom_call" | custom-call | flops 1500000000 | bytes 9000000 | tf_op jit(solution)/shard_map/gate/pallas_call | solution.py:729
  45.5 1.7 %collective-permute-start.3 = (f32[8,1024]{1,0:T(8,128)S(1)}, f32[8,1024]{1,0:T(8,128)S(1)}, u32[]{:S(2)}, u32[]{:S(2)}) collective-permute-start(f32[8,1024]{1,0:T(8,128)S(1)} %get-tuple-element.154), channel_id=1, source_target_pairs={{0,1},{1,0},{2,3},{3,2},{4,5},{5,4},{6,7},{7,6},{8,9},{9,8},{10,11... | collective-permute-start | bytes 98312 | tf_op jit(solution)/shard_map/ppermute | solution.py:761
  49.4 7.9 %gate_back.1 = (bf16[1024,768]{1,0:T(8,128)(2,1)S(1)}, bf16[1024,768]{1,0:T(8,128)(2,1)S(1)}, bf16[1024,768]{1,0:T(8,128)(2,1)S(1)}, f32[1024,128]{1,0:T(8,128)S...) custom-call(s32[3]{0:T(128)S(1)} %pad_add_fusion.scalars, ...), custom_call_target="tpu_custom_call" | custom-call | flops 4000000000 | bytes 24000000 | tf_op jit(solution)/shard_map/gate_back/pallas_call | solution.py:729
  61.8 2.8 %collective-permute-done.4 = bf16[768,768]{1,0:T(8,128)(2,1)S(1)} collective-permute-done((bf16[768,768]{1,0:T(8,128)(2,1)S(1)}, bf16[768,768]{1,0:T(8,128)(2,1)S(1)}, u32[]{:S(2)}, u32[]{:S(2)}) %collective-permute-start.4) | collective-permute-done | bytes 1179680 | tf_op jit(solution)/shard_map/ppermute | solution.py:766
  65.0 1.7 %collective-permute-start.5 = (bf16[384,768]{1,0:T(8,128)(2,1)S(1)}, bf16[384,768]{1,0:T(8,128)(2,1)S(1)}, u32[]{:S(2)}, u32[]{:S(2)}) collective-permute-start(bf16[384,768]{1,0:T(8,128)(2,1)S(1)} %get-tuple-element.261), channel_id=1, source_target_pairs={{0,4},{2,6},{4,0},{6,2},{8,12},{10,14},{12,8},{14,10},{16,20},{18,... | collective-permute-start | bytes 1769480 | tf_op jit(solution)/shard_map/ppermute | solution.py:766
  68.8 5.8 %mix_back.4 = (bf16[1024,1024]{1,0:T(8,128)(2,1)S(1)}, f32[1024,512]{1,0:T(8,128)S(1)}, f32[8,1024]{1,0:T(8,128)S(1)}, f32[8,1024]{1,0:T(8,128)S(1)}, f32[8,1024]{1,0:T(8,128)S(1)}, /*index=5*/f32[64,768]{1,0:T(8,128)S(1)}) custom-call(s32[3]{0:T(128)S(1)} %pad_add_fusion.scalars, ...), custom_call_target="tpu_custom_call", output_to_operand_aliasing={{0}: (21, {}), {1}: (22, {}), {2}: (23, {})} | custom-call | flops 3000000000 | bytes 18000000 | tf_op jit(solution)/shard_map/mix_back/pallas_call | solution.py:729
  74.6 5.8 %mix_back.5 = (bf16[1024,1024]{1,0:T(8,128)(2,1)S(1)}, f32[1024,512]{1,0:T(8,128)S(1)}, f32[8,1024]{1,0:T(8,128)S(1)}, f32[8,1024]{1,0:T(8,128)S(1)}, f32[8,1024]{1,0:T(8,128)S(1)}, /*index=5*/f32[64,768]{1,0:T(8,128)S(1)}) custom-call(s32[3]{0:T(128)S(1)} %pad_add_fusion.scalars, ...), custom_call_target="tpu_custom_call", output_to_operand_aliasing={{0}: (21, {}), {1}: (22, {}), {2}: (23, {})} | custom-call | flops 3000000000 | bytes 18000000 | tf_op jit(solution)/shard_map/mix_back/pallas_call | solution.py:729
  80.6 1.8 %collective-permute-start.6 = (bf16[192,768]{1,0:T(8,128)(2,1)S(1)}, bf16[192,768]{1,0:T(8,128)(2,1)S(1)}, u32[]{:S(2)}, u32[]{:S(2)}) collective-permute-start(bf16[192,768]{1,0:T(8,128)(2,1)S(1)} %get-tuple-element.267), channel_id=1, source_target_pairs={{0,8},{2,10},{4,12},{6,14},{8,0},{10,2},{12,4},{14,6},{16,24},{18,... | collective-permute-start | bytes 884744 | tf_op jit(solution)/shard_map/ppermute | solution.py:766
  82.4 6.0 %mix_back.6 = (bf16[1024,1024]{1,0:T(8,128)(2,1)S(1)}, f32[1024,512]{1,0:T(8,128)S(1)}, f32[8,1024]{1,0:T(8,128)S(1)}, f32[8,1024]{1,0:T(8,128)S(1)}, f32[8,1024]{1,0:T(8,128)S(1)}, /*index=5*/f32[64,768]{1,0:T(8,128)S(1)}) custom-call(s32[3]{0:T(128)S(1)} %pad_add_fusion.scalars, ...), custom_call_target="tpu_custom_call", output_to_operand_aliasing={{0}: (21, {}), {1}: (22, {}), {2}: (23, {})} | custom-call | flops 3000000000 | bytes 18000000 | tf_op jit(solution)/shard_map/mix_back/pallas_call | solution.py:729
  89.2 2.7 %collective-permute-start.8 = (bf16[96,768]{1,0:T(8,128)(2,1)S(1)}, bf16[96,768]{1,0:T(8,128)(2,1)S(1)}, u32[]{:S(2)}, u32[]{:S(2)}) collective-permute-start(bf16[96,768]{1,0:T(8,128)(2,1)S(1)} %add_convert_fusion.10), channel_id=1, source_target_pairs={{0,16},{2,18},{4,20},{6,22},{8,24},{10,26},{12,28},{14,30},{16,0},... | collective-permute-start | bytes 442376 | tf_op jit(solution)/shard_map/ppermute | solution.py:766
  91.9 6.3 %mix_back.7 = (bf16[1024,1024]{1,0:T(8,128)(2,1)S(1)}, f32[1024,512]{1,0:T(8,128)S(1)}, f32[8,1024]{1,0:T(8,128)S(1)}, f32[8,1024]{1,0:T(8,128)S(1)}, f32[8,1024]{1,0:T(8,128)}, /*index=5*/f32[64,768]{1,0:T(8,128)}) custom-call(s32[3]{0:T(128)S(1)} %pad_add_fusion.scalars, ...), custom_call_target="tpu_custom_call", output_to_operand_aliasing={{0}: (21, {}), {1}: (22, {}), {2}: (23, {})} | custom-call | flops 3000000000 | bytes 18000000 | tf_op jit(solution)/shard_map/mix_back/pallas_call | solution.py:729
  100.7 1.9 %rates.1 = (bf16[1024,128]{1,0:T(8,128)(2,1)S(1)}, f32[8,128]{1,0:T(8,128)S(1)}, f32[8,1024]{1,0:T(8,128)S(1)}) custom-call(s32[3]{0:T(128)S(1)} %pad_add_fusion.scalars, f32[1024,512]{1,0:T(8,128)S(1)} %get-tuple-element.202.refs_0_, f32[1024,512]{1,0:T(8,128)S(1)} %get-tuple-element.145.refs_2_.refs_7_.refs_3_.refs_1_, ...), custom_call_target="tpu_custom_call" | custom-call | tf_op jit(solution)/shard_map/rates/pallas_call | solution.py:729
  102.6 2.8 %back_oth.1 = bf16[1040,384]{1,0:T(8,128)(2,1)S(1)} custom-call(s32[3]{0:T(128)S(1)} %pad_add_fusion.scalars, bf16[1024,768]{1,0:T(8,128)(2,1)S(1)} %get-tuple-element.162.dgp, bf16[1024,1024]{1,0:T(8,128)(2,1)S(1)} %get-tuple-element.218.rest, bf16[1024,128]{1,0:T(8,128)(2,1)S(1)} %get-tuple-element.205.dz, f32[8,1024]{1,0:T(8,128)S(1)} %get-tuple-element.214.rd, ...), custom_call_target="tpu_custom_call" | custom-call | tf_op jit(solution)/shard_map/back_oth/pallas_call | solution.py:746
  109.1 2.4 %collective-permute-done.10 = bf16[576,768]{1,0:T(8,128)(2,1)S(1)} collective-permute-done((bf16[576,768]{1,0:T(8,128)(2,1)S(1)}, bf16[576,768]{1,0:T(8,128)(2,1)S(1)}, u32[]{:S(2)}, u32[]{:S(2)}) %collective-permute-start.10) | collective-permute-done | bytes 884768 | tf_op jit(solution)/shard_map/ppermute | solution.py:766
  112.5 2.3 %collective-permute-start.12 = (bf16[288,384]{1,0:T(8,128)(2,1)S(1)}, bf16[288,384]{1,0:T(8,128)(2,1)S(1)}, u32[]{:S(2)}, u32[]{:S(2)}) collective-permute-start(bf16[288,384]{1,0:T(8,128)(2,1)S(1)} %get-tuple-element.217), channel_id=1, source_target_pairs={{0,8},{2,10},{4,12},{6,14},{8,0},{10,2},{12,4},{14,6},{16,24},{18,... | collective-permute-start | bytes 663560 | tf_op jit(solution)/shard_map/ppermute | solution.py:766
  117.9 2.8 %back_own.1 = f32[1024,384]{1,0:T(8,128)S(1)} custom-call(s32[3]{0:T(128)S(1)} %pad_add_fusion.scalars, bf16[1024,768]{1,0:T(8,128)(2,1)S(1)} %get-tuple-element.162.dgp, bf16[1024,1024]{1,0:T(8,128)(2,1)S(1)} %get-tuple-element.218.rest, bf16[1024,128]{1,0:T(8,128)(2,1)S(1)} %get-tuple-element.205.dz, f32[8,1024]{1,0:T(8,128)S(1)} %get-tuple-element.214.rd, ...), custom_call_target="tpu_custom_call" | custom-call | tf_op jit(solution)/shard_map/back_own/pallas_call | solution.py:746
  121.1 2.1 %collective-permute-start.13 = (bf16[144,384]{1,0:T(8,128)(2,1)S(1)}, bf16[144,384]{1,0:T(8,128)(2,1)S(1)}, u32[]{:S(2)}, u32[]{:S(2)}) collective-permute-start(bf16[144,384]{1,0:T(8,128)(2,1)S(1)} %get-tuple-element.271), channel_id=1, source_target_pairs={{0,8},{2,10},{4,12},{6,14},{8,0},{10,2},{12,4},{14,6},{16,24},{18,... | collective-permute-start | bytes 331784 | tf_op jit(solution)/shard_map/ppermute | solution.py:766
  124.1 3.3 %collective-permute-done.15 = bf16[192,768]{1,0:T(8,128)(2,1)S(1)} collective-permute-done((bf16[192,768]{1,0:T(8,128)(2,1)S(1)}, bf16[192,768]{1,0:T(8,128)(2,1)S(1)}, u32[]{:S(2)}, u32[]{:S(2)}) %collective-permute-start.15) | collective-permute-done | bytes 294944 | tf_op jit(solution)/shard_map/ppermute | solution.py:766
  134.2 2.6 %collective-permute-done.16 = bf16[72,768]{1,0:T(8,128)(2,1)S(1)} collective-permute-done((bf16[72,768]{1,0:T(8,128)(2,1)S(1)}, bf16[72,768]{1,0:T(8,128)(2,1)S(1)}, u32[]{:S(2)}, u32[]{:S(2)}) %collective-permute-start.16) | collective-permute-done | bytes 110624 | tf_op jit(solution)/shard_map/ppermute | solution.py:766
  136.9 1.7 collective-permute-start.18
  138.5 1.7 %fusion.2 = f32[1024,384]{1,0:T(8,128)} fusion(bf16[1024,384]{1,0:T(8,128)(2,1)S(1)} %copy-done.1, f32[1024,384]{1,0:T(8,128)S(1)} %back_own.1, bf16[1024,384]{1,0:T(8,128)(2,1)S(1)} %copy-done.5, f32[1024]{0:T(1024)S(1)} %get-tuple-element.258, f32[384]{0:T(512)S(1)} %convert_element_type.314, bf16[1040,384]{1,0:T(8,128)(2,1)S(1)} %collective-permute-done.17, ...), kind=kLoop, calls=%fused_computation.5 | loop fusion | flops 3538944 | bytes 5514752 | tf_op jit(solution)/shard_map/sub | solution.py:1194
  141.1 2.6 %collective-permute-done.20 = bf16[384,768]{1,0:T(8,128)(2,1)S(1)} collective-permute-done((bf16[384,768]{1,0:T(8,128)(2,1)S(1)}, bf16[384,768]{1,0:T(8,128)(2,1)S(1)}, u32[]{:S(2)}, u32[]{:S(2)}) %collective-permute-start.20) | collective-permute-done | bytes 589856 | tf_op jit(solution)/shard_map/ppermute | solution.py:766
  143.7 4.1 %collective-permute-done.19 = bf16[72,768]{1,0:T(8,128)(2,1)S(1)} collective-permute-done((bf16[72,768]{1,0:T(8,128)(2,1)S(1)}, bf16[72,768]{1,0:T(8,128)(2,1)S(1)}, u32[]{:S(2)}, u32[]{:S(2)}) %collective-permute-start.19) | collective-permute-done | bytes 110624 | tf_op jit(solution)/shard_map/ppermute | solution.py:766
  149.3 4.2 %collective-permute-done.23 = bf16[144,384]{1,0:T(8,128)(2,1)S(1)} collective-permute-done((bf16[144,384]{1,0:T(8,128)(2,1)S(1)}, bf16[144,384]{1,0:T(8,128)(2,1)S(1)}, u32[]{:S(2)}, u32[]{:S(2)}) %collective-permute-start.23) | collective-permute-done | bytes 110624 | tf_op jit(solution)/shard_map/ppermute | solution.py:766
  155.3 3.0 %unpack_early.1 = (f32[768,768]{1,0:T(8,128)}, f32[768,768]{1,0:T(8,128)}) custom-call(s32[3]{0:T(128)S(1)} %pad_add_fusion.scalars, bf16[768,768]{1,0:T(8,128)(2,1)S(1)} %pad_maximum_fusion.first, bf16[768,768]{1,0:T(8,128)(2,1)S(1)} %collective-permute-done.25.second), custom_call_target="tpu_custom_call" | custom-call | tf_op jit(solution)/shard_map/unpack_early/pallas_call | solution.py:746
  158.3 2.3 %collective-permute-done.24 = bf16[288,384]{1,0:T(8,128)(2,1)S(1)} collective-permute-done((bf16[288,384]{1,0:T(8,128)(2,1)S(1)}, bf16[288,384]{1,0:T(8,128)(2,1)S(1)}, u32[]{:S(2)}, u32[]{:S(2)}) %collective-permute-start.24) | collective-permute-done | bytes 221216 | tf_op jit(solution)/shard_map/ppermute | solution.py:766
  161.4 2.4 %collective-permute-done.26.second = bf16[576,768]{1,0:T(8,128)(2,1)S(1)} collective-permute-done((bf16[576,768]{1,0:T(8,128)(2,1)S(1)}, bf16[576,768]{1,0:T(8,128)(2,1)S(1)}, u32[]{:S(2)}, u32[]{:S(2)}) %collective-permute-start.26) | collective-permute-done | bytes 884768 | tf_op jit(solution)/shard_map/ppermute | solution.py:766
  163.9 2.7 %unpack_late.1 = (f32[768,768]{1,0:T(8,128)}, f32[768,256]{1,0:T(8,128)}, f32[12,2,768]{2,1,0:T(2,128)}, f32[4,768]{1,0:T(4,128)}, f32[768]{0:T(1024)}, /*index=...) custom-call(s32[3]{0:T(128)S(1)} %pad_add_fusion.scalars, ...), custom_call_target="tpu_custom_call" | custom-call | tf_op jit(solution)/shard_map/unpack_late/pallas_call | solution.py:746
  (122 shorter events, 48.5 us)
Async XLA Ops:
  1.3 17.8 %collective-permute-start.1 = (bf16[1,384]{1,0:T(2,128)(2,1)S(1)}, bf16[1,384]{1,0:T(2,128)(2,1)S(1)}, u32[]{:S(2)}, u32[]{:S(2)}) collective-permute-start(bf16[1,384]{1,0:T(2,128)(2,1)S(1)} %concatenate.72), channel_id=1, source_target_pairs={{0,1},{1,0},{2,3},{3,2},{4,5},{5,4},{6,7},{7,6},{8,9},{9,8},{10,11... | collective-permute-start | bytes 2312 | tf_op jit(solution)/shard_map/ppermute | solution.py:761
  4.3 19.2 %collective-permute-start = (bf16[1024,384]{1,0:T(8,128)(2,1)}, bf16[1024,384]{1,0:T(8,128)(2,1)S(1)}, u32[]{:S(2)}, u32[]{:S(2)}) collective-permute-start(bf16[1024,384]{1,0:T(8,128)(2,1)} %refs_0_.1), channel_id=1, source_target_pairs={{0,1},{1,0},{2,3},{3,2},{4,5},{5,4},{6,7},{7,6},{8,9},{9,8},{10,11... | collective-permute-start | bytes 2359304 | tf_op jit(solution)/shard_map/ppermute | solution.py:761
  15.1 1.3 copy-start.7
  23.5 18.5 %collective-permute-start.2 = (bf16[1024,384]{1,0:T(8,128)(2,1)S(1)}, bf16[1024,384]{1,0:T(8,128)(2,1)S(1)}, u32[]{:S(2)}, u32[]{:S(2)}) collective-permute-start(bf16[1024,384]{1,0:T(8,128)(2,1)S(1)} %copy-done.4), channel_id=1, source_target_pairs={{0,1},{1,0},{2,3},{3,2},{4,5},{5,4},{6,7},{7,6},{8,9},{9,8},{10,11... | collective-permute-start | bytes 2359304 | tf_op jit(solution)/shard_map/ppermute | solution.py:761
  45.5 4.0 %collective-permute-start.3 = (f32[8,1024]{1,0:T(8,128)S(1)}, f32[8,1024]{1,0:T(8,128)S(1)}, u32[]{:S(2)}, u32[]{:S(2)}) collective-permute-start(f32[8,1024]{1,0:T(8,128)S(1)} %get-tuple-element.154), channel_id=1, source_target_pairs={{0,1},{1,0},{2,3},{3,2},{4,5},{5,4},{6,7},{7,6},{8,9},{9,8},{10,11... | collective-permute-start | bytes 98312 | tf_op jit(solution)/shard_map/ppermute | solution.py:761
  58.8 1.5 copy-start.3
  61.7 2.9 %collective-permute-start.4 = (bf16[768,768]{1,0:T(8,128)(2,1)S(1)}, bf16[768,768]{1,0:T(8,128)(2,1)S(1)}, u32[]{:S(2)}, u32[]{:S(2)}) collective-permute-start(bf16[768,768]{1,0:T(8,128)(2,1)S(1)} %get-tuple-element.164), channel_id=1, source_target_pairs={{0,2},{2,0},{4,6},{6,4},{8,10},{10,8},{12,14},{14,12},{16,18},{18,... | collective-permute-start | bytes 3538952 | tf_op jit(solution)/shard_map/ppermute | solution.py:766
  65.0 15.5 %collective-permute-start.5 = (bf16[384,768]{1,0:T(8,128)(2,1)S(1)}, bf16[384,768]{1,0:T(8,128)(2,1)S(1)}, u32[]{:S(2)}, u32[]{:S(2)}) collective-permute-start(bf16[384,768]{1,0:T(8,128)(2,1)S(1)} %get-tuple-element.261), channel_id=1, source_target_pairs={{0,4},{2,6},{4,0},{6,2},{8,12},{10,14},{12,8},{14,10},{16,20},{18,... | collective-permute-start | bytes 1769480 | tf_op jit(solution)/shard_map/ppermute | solution.py:766
  66.7 21.7 %collective-permute-start.7 = (bf16[1024,384]{1,0:T(8,128)(2,1)S(1)}, bf16[1024,384]{1,0:T(8,128)(2,1)S(1)}, u32[]{:S(2)}, u32[]{:S(2)}) collective-permute-start(bf16[1024,384]{1,0:T(8,128)(2,1)S(1)} %branch_oth.1), channel_id=1, source_target_pairs={{0,1},{1,0},{2,3},{3,2},{4,5},{5,4},{6,7},{7,6},{8,9},{9,8},{10,11... | collective-permute-start | bytes 2359304 | tf_op jit(solution)/shard_map/ppermute | solution.py:761
  80.6 8.6 %collective-permute-start.6 = (bf16[192,768]{1,0:T(8,128)(2,1)S(1)}, bf16[192,768]{1,0:T(8,128)(2,1)S(1)}, u32[]{:S(2)}, u32[]{:S(2)}) collective-permute-start(bf16[192,768]{1,0:T(8,128)(2,1)S(1)} %get-tuple-element.267), channel_id=1, source_target_pairs={{0,8},{2,10},{4,12},{6,14},{8,0},{10,2},{12,4},{14,6},{16,24},{18,... | collective-permute-start | bytes 884744 | tf_op jit(solution)/shard_map/ppermute | solution.py:766
  89.2 8.9 %collective-permute-start.8 = (bf16[96,768]{1,0:T(8,128)(2,1)S(1)}, bf16[96,768]{1,0:T(8,128)(2,1)S(1)}, u32[]{:S(2)}, u32[]{:S(2)}) collective-permute-start(bf16[96,768]{1,0:T(8,128)(2,1)S(1)} %add_convert_fusion.10), channel_id=1, source_target_pairs={{0,16},{2,18},{4,20},{6,22},{8,24},{10,26},{12,28},{14,30},{16,0},... | collective-permute-start | bytes 442376 | tf_op jit(solution)/shard_map/ppermute | solution.py:766
  100.3 8.6 %collective-permute-start.9 = (bf16[96,768]{1,0:T(8,128)(2,1)S(1)}, bf16[96,768]{1,0:T(8,128)(2,1)S(1)}, u32[]{:S(2)}, u32[]{:S(2)}) collective-permute-start(bf16[96,768]{1,0:T(8,128)(2,1)S(1)} %add_convert_fusion.8), channel_id=1, source_target_pairs={{0,16},{2,18},{4,20},{6,22},{8,24},{10,26},{12,28},{14,30},{16,0},... | collective-permute-start | bytes 442376 | tf_op jit(solution)/shard_map/ppermute | solution.py:766
  105.8 3.2 %copy-start.9 = (bf16[384]{0:T(512)(128)(2,1)S(1)}, bf16[384]{0:T(512)(128)(2,1)}, u32[]{:S(2)}) copy-start(bf16[384]{0:T(512)(128)(2,1)} %param.18) | copy-start | bytes 2308
  108.9 2.5 %collective-permute-start.10 = (bf16[576,768]{1,0:T(8,128)(2,1)S(1)}, bf16[576,768]{1,0:T(8,128)(2,1)S(1)}, u32[]{:S(2)}, u32[]{:S(2)}) collective-permute-start(bf16[576,768]{1,0:T(8,128)(2,1)S(1)} %get-tuple-element.215), channel_id=1, source_target_pairs={{0,2},{2,0},{4,6},{6,4},{8,10},{10,8},{12,14},{14,12},{16,18},{18,... | collective-permute-start | bytes 2654216 | tf_op jit(solution)/shard_map/ppermute | solution.py:766
  111.7 9.1 %collective-permute-start.11 = (bf16[288,384]{1,0:T(8,128)(2,1)S(1)}, bf16[288,384]{1,0:T(8,128)(2,1)S(1)}, u32[]{:S(2)}, u32[]{:S(2)}) collective-permute-start(bf16[288,384]{1,0:T(8,128)(2,1)S(1)} %get-tuple-element.216), channel_id=1, source_target_pairs={{0,4},{2,6},{4,0},{6,2},{8,12},{10,14},{12,8},{14,10},{16,20},{18,... | collective-permute-start | bytes 663560 | tf_op jit(solution)/shard_map/ppermute | solution.py:766
  112.5 8.5 %collective-permute-start.12 = (bf16[288,384]{1,0:T(8,128)(2,1)S(1)}, bf16[288,384]{1,0:T(8,128)(2,1)S(1)}, u32[]{:S(2)}, u32[]{:S(2)}) collective-permute-start(bf16[288,384]{1,0:T(8,128)(2,1)S(1)} %get-tuple-element.217), channel_id=1, source_target_pairs={{0,8},{2,10},{4,12},{6,14},{8,0},{10,2},{12,4},{14,6},{16,24},{18,... | collective-permute-start | bytes 663560 | tf_op jit(solution)/shard_map/ppermute | solution.py:766
  114.8 12.6 %collective-permute-start.15 = (bf16[192,768]{1,0:T(8,128)(2,1)S(1)}, bf16[192,768]{1,0:T(8,128)(2,1)S(1)}, u32[]{:S(2)}, u32[]{:S(2)}) collective-permute-start(bf16[192,768]{1,0:T(8,128)(2,1)S(1)} %pad_maximum_fusion.2), channel_id=1, source_target_pairs={{0,8},{2,10},{4,12},{6,14},{8,0},{10,2},{12,4},{14,6},{16,24},{18,... | collective-permute-start | bytes 884744 | tf_op jit(solution)/shard_map/ppermute | solution.py:766
  114.9 19.3 %collective-permute-start.17 = (bf16[1040,384]{1,0:T(8,128)(2,1)S(1)}, bf16[1040,384]{1,0:T(8,128)(2,1)S(1)}, u32[]{:S(2)}, u32[]{:S(2)}) collective-permute-start(bf16[1040,384]{1,0:T(8,128)(2,1)S(1)} %back_oth.1), channel_id=1, source_target_pairs={{0,1},{1,0},{2,3},{3,2},{4,5},{5,4},{6,7},{7,6},{8,9},{9,8},{10,11... | collective-permute-start | bytes 2396168 | tf_op jit(solution)/shard_map/ppermute | solution.py:761
  121.1 9.9 %copy-start.1 = (bf16[1024,384]{1,0:T(8,128)(2,1)S(1)}, bf16[1024,384]{1,0:T(8,128)(2,1)}, u32[]{:S(2)}) copy-start(bf16[1024,384]{1,0:T(8,128)(2,1)} %refs_0_.1) | copy-start | bytes 2359300
  121.1 7.8 %collective-permute-start.13 = (bf16[144,384]{1,0:T(8,128)(2,1)S(1)}, bf16[144,384]{1,0:T(8,128)(2,1)S(1)}, u32[]{:S(2)}, u32[]{:S(2)}) collective-permute-start(bf16[144,384]{1,0:T(8,128)(2,1)S(1)} %get-tuple-element.271), channel_id=1, source_target_pairs={{0,8},{2,10},{4,12},{6,14},{8,0},{10,2},{12,4},{14,6},{16,24},{18,... | collective-permute-start | bytes 331784 | tf_op jit(solution)/shard_map/ppermute | solution.py:766
  123.3 5.6 %collective-permute-start.14 = (bf16[144,384]{1,0:T(8,128)(2,1)S(1)}, bf16[144,384]{1,0:T(8,128)(2,1)S(1)}, u32[]{:S(2)}, u32[]{:S(2)}) collective-permute-start(bf16[144,384]{1,0:T(8,128)(2,1)S(1)} %get-tuple-element.272), channel_id=1, source_target_pairs={{0,4},{2,6},{4,0},{6,2},{8,12},{10,14},{12,8},{14,10},{16,20},{18,... | collective-permute-start | bytes 331784 | tf_op jit(solution)/shard_map/ppermute | solution.py:766
  129.0 14.6 %collective-permute-start.20 = (bf16[384,768]{1,0:T(8,128)(2,1)S(1)}, bf16[384,768]{1,0:T(8,128)(2,1)S(1)}, u32[]{:S(2)}, u32[]{:S(2)}) collective-permute-start(bf16[384,768]{1,0:T(8,128)(2,1)S(1)} %pad_maximum_fusion.1), channel_id=1, source_target_pairs={{0,4},{2,6},{4,0},{6,2},{8,12},{10,14},{12,8},{14,10},{16,20},{18,... | collective-permute-start | bytes 1769480 | tf_op jit(solution)/shard_map/ppermute | solution.py:766
  129.8 7.0 %collective-permute-start.16 = (bf16[72,768]{1,0:T(8,128)(2,1)S(1)}, bf16[72,768]{1,0:T(8,128)(2,1)S(1)}, u32[]{:S(2)}, u32[]{:S(2)}) collective-permute-start(bf16[72,768]{1,0:T(8,128)(2,1)S(1)} %pad_maximum_fusion.6), channel_id=1, source_target_pairs={{0,16},{2,18},{4,20},{6,22},{8,24},{10,26},{12,28},{14,30},{16,0},... | collective-permute-start | bytes 331784 | tf_op jit(solution)/shard_map/ppermute | solution.py:766
  132.3 6.2 %copy-start.5 = (bf16[1024,384]{1,0:T(8,128)(2,1)S(1)}, bf16[1024,384]{1,0:T(8,128)(2,1)}, u32[]{:S(2)}) copy-start(bf16[1024,384]{1,0:T(8,128)(2,1)} %refs_1_.1) | copy-start | bytes 2359300
  136.9 4.0 %collective-permute-start.18 = (bf16[24,768]{1,0:T(8,128)(2,1)S(1)}, bf16[24,768]{1,0:T(8,128)(2,1)S(1)}, u32[]{:S(2)}, u32[]{:S(2)}) collective-permute-start(bf16[24,768]{1,0:T(8,128)(2,1)S(1)} %slice.216), channel_id=1, source_target_pairs={{0,1},{1,0},{2,3},{3,2},{4,5},{5,4},{6,7},{7,6},{8,9},{9,8},{10,11... | collective-permute-start | bytes 110600 | tf_op jit(solution)/shard_map/ppermute | solution.py:761
  141.0 6.8 %collective-permute-start.19 = (bf16[72,768]{1,0:T(8,128)(2,1)S(1)}, bf16[72,768]{1,0:T(8,128)(2,1)S(1)}, u32[]{:S(2)}, u32[]{:S(2)}) collective-permute-start(bf16[72,768]{1,0:T(8,128)(2,1)S(1)} %pad_maximum_fusion.7), channel_id=1, source_target_pairs={{0,16},{2,18},{4,20},{6,22},{8,24},{10,26},{12,28},{14,30},{16,0},... | collective-permute-start | bytes 331784 | tf_op jit(solution)/shard_map/ppermute | solution.py:766
  147.8 7.4 %collective-permute-start.25 = (bf16[768,768]{1,0:T(8,128)(2,1)S(1)}, bf16[768,768]{1,0:T(8,128)(2,1)S(1)}, u32[]{:S(2)}, u32[]{:S(2)}) collective-permute-start(bf16[768,768]{1,0:T(8,128)(2,1)S(1)} %pad_maximum_fusion.first), channel_id=1, source_target_pairs={{0,2},{2,0},{4,6},{6,4},{8,10},{10,8},{12,14},{14,12},{16,18},{18,... | collective-permute-start | bytes 3538952 | tf_op jit(solution)/shard_map/ppermute | solution.py:766
  147.9 5.5 %collective-permute-start.23 = (bf16[144,384]{1,0:T(8,128)(2,1)S(1)}, bf16[144,384]{1,0:T(8,128)(2,1)S(1)}, u32[]{:S(2)}, u32[]{:S(2)}) collective-permute-start(bf16[144,384]{1,0:T(8,128)(2,1)S(1)} %get-tuple-element.274), channel_id=1, source_target_pairs={{0,4},{2,6},{4,0},{6,2},{8,12},{10,14},{12,8},{14,10},{16,20},{18,... | collective-permute-start | bytes 331784 | tf_op jit(solution)/shard_map/ppermute | solution.py:766
  149.3 5.2 %collective-permute-start.21 = (bf16[144,384]{1,0:T(8,128)(2,1)S(1)}, bf16[144,384]{1,0:T(8,128)(2,1)S(1)}, u32[]{:S(2)}, u32[]{:S(2)}) collective-permute-start(bf16[144,384]{1,0:T(8,128)(2,1)S(1)} %get-tuple-element.275), channel_id=1, source_target_pairs={{0,8},{2,10},{4,12},{6,14},{8,0},{10,2},{12,4},{14,6},{16,24},{18,... | collective-permute-start | bytes 331784 | tf_op jit(solution)/shard_map/ppermute | solution.py:766
  153.4 7.1 %collective-permute-start.24 = (bf16[288,384]{1,0:T(8,128)(2,1)S(1)}, bf16[288,384]{1,0:T(8,128)(2,1)S(1)}, u32[]{:S(2)}, u32[]{:S(2)}) collective-permute-start(bf16[288,384]{1,0:T(8,128)(2,1)S(1)} %pad_maximum_fusion.5), channel_id=1, source_target_pairs={{0,8},{2,10},{4,12},{6,14},{8,0},{10,2},{12,4},{14,6},{16,24},{18,... | collective-permute-start | bytes 663560 | tf_op jit(solution)/shard_map/ppermute | solution.py:766
  154.5 6.8 %collective-permute-start.22 = (bf16[288,384]{1,0:T(8,128)(2,1)S(1)}, bf16[288,384]{1,0:T(8,128)(2,1)S(1)}, u32[]{:S(2)}, u32[]{:S(2)}) collective-permute-start(bf16[288,384]{1,0:T(8,128)(2,1)S(1)} %pad_maximum_fusion.4), channel_id=1, source_target_pairs={{0,4},{2,6},{4,0},{6,2},{8,12},{10,14},{12,8},{14,10},{16,20},{18,... | collective-permute-start | bytes 663560 | tf_op jit(solution)/shard_map/ppermute | solution.py:766
  161.4 2.5 %collective-permute-start.26 = (bf16[576,768]{1,0:T(8,128)(2,1)S(1)}, bf16[576,768]{1,0:T(8,128)(2,1)S(1)}, u32[]{:S(2)}, u32[]{:S(2)}) collective-permute-start(bf16[576,768]{1,0:T(8,128)(2,1)S(1)} %maximum_maximum_fusion.first), channel_id=1, source_target_pairs={{0,2},{2,0},{4,6},{6,4},{8,10},{10,8},{12,14},{14,12},{16,18},{18,... | collective-permute-start | bytes 2654216 | tf_op jit(solution)/shard_map/ppermute | solution.py:766
  (5 other events, 5.8 us)

commit v4 on v3

--- a/solution.py
+++ b/solution.py
@@ -1041,14 +1041,6 @@
         "pack_early",
     )
 
-    def halve(keep, send, bit):
-        got = swap_dp(send, bit)
-        h = keep.shape[0] // 2
-        return add_low(keep[:h], got[:h]), add_low(keep[h:], got[h:])
-
-    def finish(keep, send, bit):
-        return rest_of_dp(add_low(keep, swap_dp(send, bit)))
-
     def rest_of_dp(x):
         extra = SHARDS
         while extra < lax.axis_size("dp"):
@@ -1061,7 +1053,13 @@
         jnp.zeros((n, width), F32),
         jnp.zeros((8, conv_width), F32),
     )
-    keep, send = halve(keep, send, order_a[0])
+    branch_own = whole(
+        partial(branch_kernel, other=False), (scalars, after(gz, send), out_v), [full(rows, width_own)], [],
+        "branch_own"
+    )[0]
+    got, branch_own = lax.optimization_barrier((swap_dp(send, order_a[0]), branch_own))
+    h = keep.shape[0] // 2
+    keep, send = add_low(keep[:h], got[:h]), add_low(keep[h:], got[h:])
     state = (
         *zeros,
         jnp.zeros((rows, conv_width), BF16),
@@ -1135,26 +1133,18 @@
     h, c = keep.shape[0] // 2, model // 2
     keeps = [add_low(keep[:h, :c], got[:h, :c]), add_low(keep[:h, c:], got[:h, c:])]
     sends = [add_low(keep[h:, :c], got[h:, :c]), add_low(keep[h:, c:], got[h:, c:])]
-    sends[0], sends[1], rest, gz_late = lax.optimization_barrier((sends[0], sends[1], rest, gz))
+    sends[0], sends[1], rest = lax.optimization_barrier((sends[0], sends[1], rest))
     dn_got = swap_mp(dn_oth)
 
     dn_own = whole(
         partial(back_project_kernel, other=False), (*back_args[:2], rest, *back_args[3:]),
         [full(rows, width_own)], [], "back_own"
     )[0]
-    branch_own = whole(
-        partial(branch_kernel, other=False), (scalars, gz_late, out_v), [full(rows, width_own)], [],
-        "branch_own"
-    )[0]
     for level in (1, 2):
         gots = [swap_dp(v, order[level]) for v, order in zip(sends, orders_b)]
         if level == 1:
-            gots[0], gots[1], dn_own, branch_own = lax.optimization_barrier(
-                (gots[0], gots[1], dn_own, branch_own)
-            )
-        else:
+            gots[0], gots[1], dn_own, sent = lax.optimization_barrier((gots[0], gots[1], dn_own, sent))
             x = jnp.concatenate([x, sent])
-            gots[0], gots[1], x = lax.optimization_barrier((gots[0], gots[1], x))
         h = keeps[0].shape[0] // 2
         pairs = list(zip(keeps, gots))
         if level == 1:
@@ -1196,8 +1186,8 @@
         - tokens_f * (inv * inv * (rd_both[:, None] / model))
     )
 
+    got, grad_tokens, sent = lax.optimization_barrier((swap_dp(z, 3), grad_tokens, sent))
     x = jnp.concatenate([x, sent])
-    got, grad_tokens, x = lax.optimization_barrier((swap_dp(z, 3), grad_tokens, x))
     sent = swap_dp(x, order_a[0])
     z = jnp.concatenate([z, got])
     zs = [z[:, :c], z[:, c:]]

time: 167 us -> 166 us (level)
  waiting for transfers between devices: 39.6 us -> 35.9 us
  starting transfers between devices: 26.9 us -> 29.6 us
    ppermute x20, waiting for transfers between devices: 32.2 us -> 28.4 us  [swap_dp(): return lax.ppermute(x, 'dp', [(i, i ^ 1 << bit) for i in range(size)])]
    ppermute x20, starting transfers between devices: 17.2 us -> 20 us  [swap_dp(): return lax.ppermute(x, 'dp', [(i, i ^ 1 << bit) for i in range(size)])]
    unnamed x22 -> x23, local copies, waits for them, and re-layouts: 7.87 us -> 7.91 us
  transfers between devices with their start and end apart: 27 -> 27, of which waited for: 19 -> 18; matrix products, arithmetic and copies ran while one was open for 6% -> 6% of each run, Pallas kernels for 35% -> 35%
where the time goes in v4:
time: 166 us
  Pallas kernels  74.3 us (45%)
  waiting for transfers between devices  35.9 us (22%)
  starting transfers between devices  29.6 us (18%)
  local copies, waits for them, and re-layouts  11.7 us (7%)
  other arithmetic  6.91 us (4%)
  matrix products  5.44 us (3%)
  between operations  1.99 us (1%)
    pallas_call x9, Pallas kernels, call(): pl.pallas_call(looped, out_shape=[pltpu.VMEM(o.shape, o.dtype) for o in o...  55.4 us
    ppermute x20, waiting for transfers between devices, swap_dp(): return lax.ppermute(x, 'dp', [(i, i ^ 1 << bit) for i in range(size)])  28.4 us
    ppermute x20, starting transfers between devices, swap_dp(): return lax.ppermute(x, 'dp', [(i, i ^ 1 << bit) for i in range(size)])  20 us
    pallas_call x8, Pallas kernels, whole(): pl.pallas_call(kernel, out_shape=[pltpu.VMEM(o.shape, o.dtype) if in_vmem...  17.5 us
    ppermute x7, starting transfers between devices, swap_mp(): return lax.ppermute(x, 'mp', [(0, 1), (1, 0)])  9.59 us
    unnamed x23, local copies, waits for them, and re-layouts  7.91 us
    ppermute x7, waiting for transfers between devices, swap_mp(): return lax.ppermute(x, 'mp', [(0, 1), (1, 0)])  7.52 us
    dot_general x5, matrix products, mm_tn(): lax.dot_general(a, b, (((0,), (0,)), ((), ())), preferred_element_type=F32)  5.44 us
  transfers between devices with their start and end apart: 27, of which 18 were waited for; matrix products, arithmetic and copies ran while one was open for 6% of the time, Pallas kernels for 35%

profile of v4, /device:TPU:0, one launch (start us, length us, event | category | flops | bytes accessed | tf_op | source)
XLA Modules:
  0.0 165.9 jit_solution(343652702540172672)
XLA Ops:
  1.3 3.0 %collective-permute-start.1 = (bf16[1,384]{1,0:T(2,128)(2,1)S(1)}, bf16[1,384]{1,0:T(2,128)(2,1)S(1)}, u32[]{:S(2)}, u32[]{:S(2)}) collective-permute-start(bf16[1,384]{1,0:T(2,128)(2,1)S(1)} %concatenate.72), channel_id=1, source_target_pairs={{0,1},{1,0},{2,3},{3,2},{4,5},{5,4},{6,7},{7,6},{8,9},{9,8},{10,11... | collective-permute-start | bytes 2312 | tf_op jit(solution)/shard_map/ppermute | solution.py:761
  19.2 4.3 %collective-permute-done.refs_1_ = bf16[1024,384]{1,0:T(8,128)(2,1)S(1)} collective-permute-done((bf16[1024,384]{1,0:T(8,128)(2,1)}, bf16[1024,384]{1,0:T(8,128)(2,1)S(1)}, u32[]{:S(2)}, u32[]{:S(2)}) %collective-permute-start) | collective-permute-done | bytes 786464 | tf_op jit(solution)/shard_map/ppermute | solution.py:761
  23.8 11.1 %project.1 = (bf16[1024,768]{1,0:T(8,128)(2,1)S(1)}, f32[1024,768]{1,0:T(8,128)S(1)}, bf16[1024,1024]{1,0:T(8,128)(2,1)S(1)}, bf16[1024,1024]{1,0:T(8,128)(2,1)S...) custom-call(s32[3]{0:T(128)S(1)} %pad_add_fusion.scalars, ...), custom_call_target="tpu_custom_call" | custom-call | flops 6000000000 | bytes 36000000 | tf_op jit(solution)/shard_map/project/pallas_call | solution.py:729
  35.0 7.1 %mix.1 = (f32[1024,768]{1,0:T(8,128)S(1)}, bf16[8,64,768]{2,1,0:T(8,128)(2,1)S(1)}) custom-call(s32[3]{0:T(128)S(1)} %pad_add_fusion.scalars, f32[1024,768]{1,0:T(8,128)S(1)} %get-tuple-element.142.refs_0_.refs_3_.refs_1_, bf16[1024,256]{1,0:T(8,128)(2,1)S(1)} %get-tuple-element.143.refs_1_.refs_8_.refs_2_, ...), custom_call_target="tpu_custom_call" | custom-call | flops 3500000000 | bytes 21000000 | tf_op jit(solution)/shard_map/mix/pallas_call | solution.py:729
  42.0 3.5 %gate.1 = (f32[1024,768]{1,0:T(8,128)S(1)}, bf16[1024,768]{1,0:T(8,128)(2,1)S(1)}, f32[8,1024]{1,0:T(8,128)S(1)}) custom-call(s32[3]{0:T(128)S(1)} %pad_add_fusion.scalars, f32[1024,768]{1,0:T(8,128)S(1)} %get-tuple-element.148.refs_0_.refs_2_, f32[1024,768]{1,0:T(8,128)S(1)} %get-tuple-element.149.refs_1_, ...), custom_call_target="tpu_custom_call" | custom-call | flops 1500000000 | bytes 9000000 | tf_op jit(solution)/shard_map/gate/pallas_call | solution.py:729
  45.5 1.7 %collective-permute-start.3 = (f32[8,1024]{1,0:T(8,128)S(1)}, f32[8,1024]{1,0:T(8,128)S(1)}, u32[]{:S(2)}, u32[]{:S(2)}) collective-permute-start(f32[8,1024]{1,0:T(8,128)S(1)} %get-tuple-element.153), channel_id=1, source_target_pairs={{0,1},{1,0},{2,3},{3,2},{4,5},{5,4},{6,7},{7,6},{8,9},{9,8},{10,11... | collective-permute-start | bytes 98312 | tf_op jit(solution)/shard_map/ppermute | solution.py:761
  49.5 7.9 %gate_back.1 = (bf16[1024,768]{1,0:T(8,128)(2,1)S(1)}, bf16[1024,768]{1,0:T(8,128)(2,1)S(1)}, bf16[1024,768]{1,0:T(8,128)(2,1)S(1)}, f32[1024,128]{1,0:T(8,128)S...) custom-call(s32[3]{0:T(128)S(1)} %pad_add_fusion.scalars, ...), custom_call_target="tpu_custom_call" | custom-call | flops 4000000000 | bytes 24000000 | tf_op jit(solution)/shard_map/gate_back/pallas_call | solution.py:729
  65.1 1.7 %collective-permute-start.5 = (bf16[384,768]{1,0:T(8,128)(2,1)S(1)}, bf16[384,768]{1,0:T(8,128)(2,1)S(1)}, u32[]{:S(2)}, u32[]{:S(2)}) collective-permute-start(bf16[384,768]{1,0:T(8,128)(2,1)S(1)} %get-tuple-element.259), channel_id=1, source_target_pairs={{0,4},{2,6},{4,0},{6,2},{8,12},{10,14},{12,8},{14,10},{16,20},{18,... | collective-permute-start | bytes 1769480 | tf_op jit(solution)/shard_map/ppermute | solution.py:766
  68.9 5.8 %mix_back.4 = (bf16[1024,1024]{1,0:T(8,128)(2,1)S(1)}, f32[1024,512]{1,0:T(8,128)S(1)}, f32[8,1024]{1,0:T(8,128)S(1)}, f32[8,1024]{1,0:T(8,128)S(1)}, f32[8,1024]{1,0:T(8,128)S(1)}, /*index=5*/f32[64,768]{1,0:T(8,128)S(1)}) custom-call(s32[3]{0:T(128)S(1)} %pad_add_fusion.scalars, ...), custom_call_target="tpu_custom_call", output_to_operand_aliasing={{0}: (21, {}), {1}: (22, {}), {2}: (23, {})} | custom-call | flops 3000000000 | bytes 18000000 | tf_op jit(solution)/shard_map/mix_back/pallas_call | solution.py:729
  74.7 5.8 %mix_back.5 = (bf16[1024,1024]{1,0:T(8,128)(2,1)S(1)}, f32[1024,512]{1,0:T(8,128)S(1)}, f32[8,1024]{1,0:T(8,128)S(1)}, f32[8,1024]{1,0:T(8,128)S(1)}, f32[8,1024]{1,0:T(8,128)S(1)}, /*index=5*/f32[64,768]{1,0:T(8,128)S(1)}) custom-call(s32[3]{0:T(128)S(1)} %pad_add_fusion.scalars, ...), custom_call_target="tpu_custom_call", output_to_operand_aliasing={{0}: (21, {}), {1}: (22, {}), {2}: (23, {})} | custom-call | flops 3000000000 | bytes 18000000 | tf_op jit(solution)/shard_map/mix_back/pallas_call | solution.py:729
  80.7 1.8 %collective-permute-start.6 = (bf16[192,768]{1,0:T(8,128)(2,1)S(1)}, bf16[192,768]{1,0:T(8,128)(2,1)S(1)}, u32[]{:S(2)}, u32[]{:S(2)}) collective-permute-start(bf16[192,768]{1,0:T(8,128)(2,1)S(1)} %get-tuple-element.265), channel_id=1, source_target_pairs={{0,8},{2,10},{4,12},{6,14},{8,0},{10,2},{12,4},{14,6},{16,24},{18,... | collective-permute-start | bytes 884744 | tf_op jit(solution)/shard_map/ppermute | solution.py:766
  82.5 6.0 %mix_back.6 = (bf16[1024,1024]{1,0:T(8,128)(2,1)S(1)}, f32[1024,512]{1,0:T(8,128)S(1)}, f32[8,1024]{1,0:T(8,128)S(1)}, f32[8,1024]{1,0:T(8,128)S(1)}, f32[8,1024]{1,0:T(8,128)S(1)}, /*index=5*/f32[64,768]{1,0:T(8,128)S(1)}) custom-call(s32[3]{0:T(128)S(1)} %pad_add_fusion.scalars, ...), custom_call_target="tpu_custom_call", output_to_operand_aliasing={{0}: (21, {}), {1}: (22, {}), {2}: (23, {})} | custom-call | flops 3000000000 | bytes 18000000 | tf_op jit(solution)/shard_map/mix_back/pallas_call | solution.py:729
  89.3 2.7 %collective-permute-start.8 = (bf16[96,768]{1,0:T(8,128)(2,1)S(1)}, bf16[96,768]{1,0:T(8,128)(2,1)S(1)}, u32[]{:S(2)}, u32[]{:S(2)}) collective-permute-start(bf16[96,768]{1,0:T(8,128)(2,1)S(1)} %add_convert_fusion.10), channel_id=1, source_target_pairs={{0,16},{2,18},{4,20},{6,22},{8,24},{10,26},{12,28},{14,30},{16,0},... | collective-permute-start | bytes 442376 | tf_op jit(solution)/shard_map/ppermute | solution.py:766
  91.9 6.3 %mix_back.7 = (bf16[1024,1024]{1,0:T(8,128)(2,1)S(1)}, f32[1024,512]{1,0:T(8,128)S(1)}, f32[8,1024]{1,0:T(8,128)S(1)}, f32[8,1024]{1,0:T(8,128)S(1)}, f32[8,1024]{1,0:T(8,128)}, /*index=5*/f32[64,768]{1,0:T(8,128)}) custom-call(s32[3]{0:T(128)S(1)} %pad_add_fusion.scalars, ...), custom_call_target="tpu_custom_call", output_to_operand_aliasing={{0}: (21, {}), {1}: (22, {}), {2}: (23, {})} | custom-call | flops 3000000000 | bytes 18000000 | tf_op jit(solution)/shard_map/mix_back/pallas_call | solution.py:729
  100.8 1.9 %rates.1 = (bf16[1024,128]{1,0:T(8,128)(2,1)S(1)}, f32[8,128]{1,0:T(8,128)S(1)}, f32[8,1024]{1,0:T(8,128)S(1)}) custom-call(s32[3]{0:T(128)S(1)} %pad_add_fusion.scalars, f32[1024,512]{1,0:T(8,128)S(1)} %get-tuple-element.203.refs_0_, f32[1024,512]{1,0:T(8,128)S(1)} %get-tuple-element.144.refs_2_.refs_7_.refs_3_.refs_1_, ...), custom_call_target="tpu_custom_call" | custom-call | tf_op jit(solution)/shard_map/rates/pallas_call | solution.py:729
  102.7 2.8 %back_oth.1 = bf16[1040,384]{1,0:T(8,128)(2,1)S(1)} custom-call(s32[3]{0:T(128)S(1)} %pad_add_fusion.scalars, bf16[1024,768]{1,0:T(8,128)(2,1)S(1)} %get-tuple-element.161.dgp, bf16[1024,1024]{1,0:T(8,128)(2,1)S(1)} %get-tuple-element.219.rest, bf16[1024,128]{1,0:T(8,128)(2,1)S(1)} %get-tuple-element.206.dz, f32[8,1024]{1,0:T(8,128)S(1)} %get-tuple-element.215.rd, ...), custom_call_target="tpu_custom_call" | custom-call | tf_op jit(solution)/shard_map/back_oth/pallas_call | solution.py:746
  105.9 1.6 pack_late.1
  109.1 1.8 %collective-permute-start.13 = (bf16[192,768]{1,0:T(8,128)(2,1)S(1)}, bf16[192,768]{1,0:T(8,128)(2,1)S(1)}, u32[]{:S(2)}, u32[]{:S(2)}) collective-permute-start(bf16[192,768]{1,0:T(8,128)(2,1)S(1)} %pad_maximum_fusion.1), channel_id=1, source_target_pairs={{0,8},{2,10},{4,12},{6,14},{8,0},{10,2},{12,4},{14,6},{16,24},{18,... | collective-permute-start | bytes 884744 | tf_op jit(solution)/shard_map/ppermute | solution.py:766
  112.6 2.3 %collective-permute-start.12 = (bf16[288,384]{1,0:T(8,128)(2,1)S(1)}, bf16[288,384]{1,0:T(8,128)(2,1)S(1)}, u32[]{:S(2)}, u32[]{:S(2)}) collective-permute-start(bf16[288,384]{1,0:T(8,128)(2,1)S(1)} %get-tuple-element.218), channel_id=1, source_target_pairs={{0,8},{2,10},{4,12},{6,14},{8,0},{10,2},{12,4},{14,6},{16,24},{18,... | collective-permute-start | bytes 663560 | tf_op jit(solution)/shard_map/ppermute | solution.py:766
  116.4 2.8 %back_own.1 = f32[1024,384]{1,0:T(8,128)S(1)} custom-call(s32[3]{0:T(128)S(1)} %pad_add_fusion.scalars, bf16[1024,768]{1,0:T(8,128)(2,1)S(1)} %get-tuple-element.161.dgp, bf16[1024,1024]{1,0:T(8,128)(2,1)S(1)} %get-tuple-element.219.rest, bf16[1024,128]{1,0:T(8,128)(2,1)S(1)} %get-tuple-element.206.dz, f32[8,1024]{1,0:T(8,128)S(1)} %get-tuple-element.215.rd, ...), custom_call_target="tpu_custom_call" | custom-call | tf_op jit(solution)/shard_map/back_own/pallas_call | solution.py:746
  119.3 4.1 %collective-permute-done.12 = bf16[288,384]{1,0:T(8,128)(2,1)S(1)} collective-permute-done((bf16[288,384]{1,0:T(8,128)(2,1)S(1)}, bf16[288,384]{1,0:T(8,128)(2,1)S(1)}, u32[]{:S(2)}, u32[]{:S(2)}) %collective-permute-start.12) | collective-permute-done | bytes 221216 | tf_op jit(solution)/shard_map/ppermute | solution.py:766
  123.4 1.8 %collective-permute-start.14 = (bf16[144,384]{1,0:T(8,128)(2,1)S(1)}, bf16[144,384]{1,0:T(8,128)(2,1)S(1)}, u32[]{:S(2)}, u32[]{:S(2)}) collective-permute-start(bf16[144,384]{1,0:T(8,128)(2,1)S(1)} %get-tuple-element.269), channel_id=1, source_target_pairs={{0,8},{2,10},{4,12},{6,14},{8,0},{10,2},{12,4},{14,6},{16,24},{18,... | collective-permute-start | bytes 331784 | tf_op jit(solution)/shard_map/ppermute | solution.py:766
  128.3 1.8 %collective-permute-done.15 = bf16[144,384]{1,0:T(8,128)(2,1)S(1)} collective-permute-done((bf16[144,384]{1,0:T(8,128)(2,1)S(1)}, bf16[144,384]{1,0:T(8,128)(2,1)S(1)}, u32[]{:S(2)}, u32[]{:S(2)}) %collective-permute-start.15) | collective-permute-done | bytes 110624 | tf_op jit(solution)/shard_map/ppermute | solution.py:766
  134.3 2.5 %collective-permute-done.16 = bf16[72,768]{1,0:T(8,128)(2,1)S(1)} collective-permute-done((bf16[72,768]{1,0:T(8,128)(2,1)S(1)}, bf16[72,768]{1,0:T(8,128)(2,1)S(1)}, u32[]{:S(2)}, u32[]{:S(2)}) %collective-permute-start.16) | collective-permute-done | bytes 110624 | tf_op jit(solution)/shard_map/ppermute | solution.py:766
  138.4 2.5 %collective-permute-done.18 = bf16[24,768]{1,0:T(8,128)(2,1)S(1)} collective-permute-done((bf16[24,768]{1,0:T(8,128)(2,1)S(1)}, bf16[24,768]{1,0:T(8,128)(2,1)S(1)}, u32[]{:S(2)}, u32[]{:S(2)}) %collective-permute-start.18) | collective-permute-done | bytes 36896 | tf_op jit(solution)/shard_map/ppermute | solution.py:761
  141.2 1.7 %fusion.2 = f32[1024,384]{1,0:T(8,128)} fusion(bf16[1024,384]{1,0:T(8,128)(2,1)S(1)} %copy-done.1, f32[1024,384]{1,0:T(8,128)S(1)} %back_own.1, bf16[1024,384]{1,0:T(8,128)(2,1)S(1)} %copy-done.5, f32[1024]{0:T(1024)S(1)} %get-tuple-element.256, f32[384]{0:T(512)S(1)} %convert_element_type.314, bf16[1040,384]{1,0:T(8,128)(2,1)S(1)} %collective-permute-done.17, ...), kind=kLoop, calls=%fused_computation.5 | loop fusion | flops 3538944 | bytes 5514752 | tf_op jit(solution)/shard_map/sub | solution.py:1184
  142.9 3.8 %collective-permute-done.19 = bf16[72,768]{1,0:T(8,128)(2,1)S(1)} collective-permute-done((bf16[72,768]{1,0:T(8,128)(2,1)S(1)}, bf16[72,768]{1,0:T(8,128)(2,1)S(1)}, u32[]{:S(2)}, u32[]{:S(2)}) %collective-permute-start.19) | collective-permute-done | bytes 110624 | tf_op jit(solution)/shard_map/ppermute | solution.py:766
  148.4 4.1 %collective-permute-done.23 = bf16[144,384]{1,0:T(8,128)(2,1)S(1)} collective-permute-done((bf16[144,384]{1,0:T(8,128)(2,1)S(1)}, bf16[144,384]{1,0:T(8,128)(2,1)S(1)}, u32[]{:S(2)}, u32[]{:S(2)}) %collective-permute-start.23) | collective-permute-done | bytes 110624 | tf_op jit(solution)/shard_map/ppermute | solution.py:766
  154.3 3.0 %unpack_early.1 = (f32[768,768]{1,0:T(8,128)}, f32[768,768]{1,0:T(8,128)}) custom-call(s32[3]{0:T(128)S(1)} %pad_add_fusion.scalars, bf16[768,768]{1,0:T(8,128)(2,1)S(1)} %constant_dynamic-update-slice_fusion.first, bf16[768,768]{1,0:T(8,128)(2,1)S(1)} %collective-permute-done.25.second), custom_call_target="tpu_custom_call" | custom-call | tf_op jit(solution)/shard_map/unpack_early/pallas_call | solution.py:746
  157.4 2.3 %collective-permute-done.24 = bf16[288,384]{1,0:T(8,128)(2,1)S(1)} collective-permute-done((bf16[288,384]{1,0:T(8,128)(2,1)S(1)}, bf16[288,384]{1,0:T(8,128)(2,1)S(1)}, u32[]{:S(2)}, u32[]{:S(2)}) %collective-permute-start.24) | collective-permute-done | bytes 221216 | tf_op jit(solution)/shard_map/ppermute | solution.py:766
  160.5 2.4 %collective-permute-done.26.second = bf16[576,768]{1,0:T(8,128)(2,1)S(1)} collective-permute-done((bf16[576,768]{1,0:T(8,128)(2,1)S(1)}, bf16[576,768]{1,0:T(8,128)(2,1)S(1)}, u32[]{:S(2)}, u32[]{:S(2)}) %collective-permute-start.26) | collective-permute-done | bytes 884768 | tf_op jit(solution)/shard_map/ppermute | solution.py:766
  163.0 2.7 %unpack_late.1 = (f32[768,768]{1,0:T(8,128)}, f32[768,256]{1,0:T(8,128)}, f32[12,2,768]{2,1,0:T(2,128)}, f32[4,768]{1,0:T(4,128)}, f32[768]{0:T(1024)}, /*index=...) custom-call(s32[3]{0:T(128)S(1)} %pad_add_fusion.scalars, ...), custom_call_target="tpu_custom_call" | custom-call | tf_op jit(solution)/shard_map/unpack_late/pallas_call | solution.py:746
  (124 shorter events, 49.1 us)
Async XLA Ops:
  1.3 17.8 %collective-permute-start.1 = (bf16[1,384]{1,0:T(2,128)(2,1)S(1)}, bf16[1,384]{1,0:T(2,128)(2,1)S(1)}, u32[]{:S(2)}, u32[]{:S(2)}) collective-permute-start(bf16[1,384]{1,0:T(2,128)(2,1)S(1)} %concatenate.72), channel_id=1, source_target_pairs={{0,1},{1,0},{2,3},{3,2},{4,5},{5,4},{6,7},{7,6},{8,9},{9,8},{10,11... | collective-permute-start | bytes 2312 | tf_op jit(solution)/shard_map/ppermute | solution.py:761
  4.3 19.2 %collective-permute-start = (bf16[1024,384]{1,0:T(8,128)(2,1)}, bf16[1024,384]{1,0:T(8,128)(2,1)S(1)}, u32[]{:S(2)}, u32[]{:S(2)}) collective-permute-start(bf16[1024,384]{1,0:T(8,128)(2,1)} %refs_0_.1), channel_id=1, source_target_pairs={{0,1},{1,0},{2,3},{3,2},{4,5},{5,4},{6,7},{7,6},{8,9},{9,8},{10,11... | collective-permute-start | bytes 2359304 | tf_op jit(solution)/shard_map/ppermute | solution.py:761
  11.7 1.3 copy-start.2
  23.5 18.5 %collective-permute-start.2 = (bf16[1024,384]{1,0:T(8,128)(2,1)S(1)}, bf16[1024,384]{1,0:T(8,128)(2,1)S(1)}, u32[]{:S(2)}, u32[]{:S(2)}) collective-permute-start(bf16[1024,384]{1,0:T(8,128)(2,1)S(1)} %copy-done.4), channel_id=1, source_target_pairs={{0,1},{1,0},{2,3},{3,2},{4,5},{5,4},{6,7},{7,6},{8,9},{9,8},{10,11... | collective-permute-start | bytes 2359304 | tf_op jit(solution)/shard_map/ppermute | solution.py:761
  45.5 4.0 %collective-permute-start.3 = (f32[8,1024]{1,0:T(8,128)S(1)}, f32[8,1024]{1,0:T(8,128)S(1)}, u32[]{:S(2)}, u32[]{:S(2)}) collective-permute-start(f32[8,1024]{1,0:T(8,128)S(1)} %get-tuple-element.153), channel_id=1, source_target_pairs={{0,1},{1,0},{2,3},{3,2},{4,5},{5,4},{6,7},{7,6},{8,9},{9,8},{10,11... | collective-permute-start | bytes 98312 | tf_op jit(solution)/shard_map/ppermute | solution.py:761
  58.9 1.5 copy-start.3
  61.9 2.9 %collective-permute-start.4 = (bf16[768,768]{1,0:T(8,128)(2,1)S(1)}, bf16[768,768]{1,0:T(8,128)(2,1)S(1)}, u32[]{:S(2)}, u32[]{:S(2)}) collective-permute-start(bf16[768,768]{1,0:T(8,128)(2,1)S(1)} %get-tuple-element.163), channel_id=1, source_target_pairs={{0,2},{2,0},{4,6},{6,4},{8,10},{10,8},{12,14},{14,12},{16,18},{18,... | collective-permute-start | bytes 3538952 | tf_op jit(solution)/shard_map/ppermute | solution.py:766
  65.1 15.5 %collective-permute-start.5 = (bf16[384,768]{1,0:T(8,128)(2,1)S(1)}, bf16[384,768]{1,0:T(8,128)(2,1)S(1)}, u32[]{:S(2)}, u32[]{:S(2)}) collective-permute-start(bf16[384,768]{1,0:T(8,128)(2,1)S(1)} %get-tuple-element.259), channel_id=1, source_target_pairs={{0,4},{2,6},{4,0},{6,2},{8,12},{10,14},{12,8},{14,10},{16,20},{18,... | collective-permute-start | bytes 1769480 | tf_op jit(solution)/shard_map/ppermute | solution.py:766
  66.8 21.7 %collective-permute-start.7 = (bf16[1024,384]{1,0:T(8,128)(2,1)S(1)}, bf16[1024,384]{1,0:T(8,128)(2,1)S(1)}, u32[]{:S(2)}, u32[]{:S(2)}) collective-permute-start(bf16[1024,384]{1,0:T(8,128)(2,1)S(1)} %branch_oth.1), channel_id=1, source_target_pairs={{0,1},{1,0},{2,3},{3,2},{4,5},{5,4},{6,7},{7,6},{8,9},{9,8},{10,11... | collective-permute-start | bytes 2359304 | tf_op jit(solution)/shard_map/ppermute | solution.py:761
  80.7 8.6 %collective-permute-start.6 = (bf16[192,768]{1,0:T(8,128)(2,1)S(1)}, bf16[192,768]{1,0:T(8,128)(2,1)S(1)}, u32[]{:S(2)}, u32[]{:S(2)}) collective-permute-start(bf16[192,768]{1,0:T(8,128)(2,1)S(1)} %get-tuple-element.265), channel_id=1, source_target_pairs={{0,8},{2,10},{4,12},{6,14},{8,0},{10,2},{12,4},{14,6},{16,24},{18,... | collective-permute-start | bytes 884744 | tf_op jit(solution)/shard_map/ppermute | solution.py:766
  89.3 8.9 %collective-permute-start.8 = (bf16[96,768]{1,0:T(8,128)(2,1)S(1)}, bf16[96,768]{1,0:T(8,128)(2,1)S(1)}, u32[]{:S(2)}, u32[]{:S(2)}) collective-permute-start(bf16[96,768]{1,0:T(8,128)(2,1)S(1)} %add_convert_fusion.10), channel_id=1, source_target_pairs={{0,16},{2,18},{4,20},{6,22},{8,24},{10,26},{12,28},{14,30},{16,0},... | collective-permute-start | bytes 442376 | tf_op jit(solution)/shard_map/ppermute | solution.py:766
  100.4 8.6 %collective-permute-start.9 = (bf16[96,768]{1,0:T(8,128)(2,1)S(1)}, bf16[96,768]{1,0:T(8,128)(2,1)S(1)}, u32[]{:S(2)}, u32[]{:S(2)}) collective-permute-start(bf16[96,768]{1,0:T(8,128)(2,1)S(1)} %add_convert_fusion.8), channel_id=1, source_target_pairs={{0,16},{2,18},{4,20},{6,22},{8,24},{10,26},{12,28},{14,30},{16,0},... | collective-permute-start | bytes 442376 | tf_op jit(solution)/shard_map/ppermute | solution.py:766
  105.9 3.2 %copy-start.9 = (bf16[384]{0:T(512)(128)(2,1)S(1)}, bf16[384]{0:T(512)(128)(2,1)}, u32[]{:S(2)}) copy-start(bf16[384]{0:T(512)(128)(2,1)} %param.18) | copy-start | bytes 2308
  109.0 2.5 %collective-permute-start.10 = (bf16[576,768]{1,0:T(8,128)(2,1)S(1)}, bf16[576,768]{1,0:T(8,128)(2,1)S(1)}, u32[]{:S(2)}, u32[]{:S(2)}) collective-permute-start(bf16[576,768]{1,0:T(8,128)(2,1)S(1)} %get-tuple-element.216), channel_id=1, source_target_pairs={{0,2},{2,0},{4,6},{6,4},{8,10},{10,8},{12,14},{14,12},{16,18},{18,... | collective-permute-start | bytes 2654216 | tf_op jit(solution)/shard_map/ppermute | solution.py:766
  109.1 10.1 %collective-permute-start.13 = (bf16[192,768]{1,0:T(8,128)(2,1)S(1)}, bf16[192,768]{1,0:T(8,128)(2,1)S(1)}, u32[]{:S(2)}, u32[]{:S(2)}) collective-permute-start(bf16[192,768]{1,0:T(8,128)(2,1)S(1)} %pad_maximum_fusion.1), channel_id=1, source_target_pairs={{0,8},{2,10},{4,12},{6,14},{8,0},{10,2},{12,4},{14,6},{16,24},{18,... | collective-permute-start | bytes 884744 | tf_op jit(solution)/shard_map/ppermute | solution.py:766
  111.7 7.5 %collective-permute-start.11 = (bf16[288,384]{1,0:T(8,128)(2,1)S(1)}, bf16[288,384]{1,0:T(8,128)(2,1)S(1)}, u32[]{:S(2)}, u32[]{:S(2)}) collective-permute-start(bf16[288,384]{1,0:T(8,128)(2,1)S(1)} %get-tuple-element.217), channel_id=1, source_target_pairs={{0,4},{2,6},{4,0},{6,2},{8,12},{10,14},{12,8},{14,10},{16,20},{18,... | collective-permute-start | bytes 663560 | tf_op jit(solution)/shard_map/ppermute | solution.py:766
  112.6 10.8 %collective-permute-start.12 = (bf16[288,384]{1,0:T(8,128)(2,1)S(1)}, bf16[288,384]{1,0:T(8,128)(2,1)S(1)}, u32[]{:S(2)}, u32[]{:S(2)}) collective-permute-start(bf16[288,384]{1,0:T(8,128)(2,1)S(1)} %get-tuple-element.218), channel_id=1, source_target_pairs={{0,8},{2,10},{4,12},{6,14},{8,0},{10,2},{12,4},{14,6},{16,24},{18,... | collective-permute-start | bytes 663560 | tf_op jit(solution)/shard_map/ppermute | solution.py:766
  114.9 19.4 %collective-permute-start.17 = (bf16[1040,384]{1,0:T(8,128)(2,1)S(1)}, bf16[1040,384]{1,0:T(8,128)(2,1)S(1)}, u32[]{:S(2)}, u32[]{:S(2)}) collective-permute-start(bf16[1040,384]{1,0:T(8,128)(2,1)S(1)} %back_oth.1), channel_id=1, source_target_pairs={{0,1},{1,0},{2,3},{3,2},{4,5},{5,4},{6,7},{7,6},{8,9},{9,8},{10,11... | collective-permute-start | bytes 2396168 | tf_op jit(solution)/shard_map/ppermute | solution.py:761
  123.4 4.8 %collective-permute-start.14 = (bf16[144,384]{1,0:T(8,128)(2,1)S(1)}, bf16[144,384]{1,0:T(8,128)(2,1)S(1)}, u32[]{:S(2)}, u32[]{:S(2)}) collective-permute-start(bf16[144,384]{1,0:T(8,128)(2,1)S(1)} %get-tuple-element.269), channel_id=1, source_target_pairs={{0,8},{2,10},{4,12},{6,14},{8,0},{10,2},{12,4},{14,6},{16,24},{18,... | collective-permute-start | bytes 331784 | tf_op jit(solution)/shard_map/ppermute | solution.py:766
  125.3 7.6 %copy-start.1 = (bf16[1024,384]{1,0:T(8,128)(2,1)S(1)}, bf16[1024,384]{1,0:T(8,128)(2,1)}, u32[]{:S(2)}) copy-start(bf16[1024,384]{1,0:T(8,128)(2,1)} %refs_0_.1) | copy-start | bytes 2359300
  125.3 4.8 %collective-permute-start.15 = (bf16[144,384]{1,0:T(8,128)(2,1)S(1)}, bf16[144,384]{1,0:T(8,128)(2,1)S(1)}, u32[]{:S(2)}, u32[]{:S(2)}) collective-permute-start(bf16[144,384]{1,0:T(8,128)(2,1)S(1)} %get-tuple-element.271), channel_id=1, source_target_pairs={{0,4},{2,6},{4,0},{6,2},{8,12},{10,14},{12,8},{14,10},{16,20},{18,... | collective-permute-start | bytes 331784 | tf_op jit(solution)/shard_map/ppermute | solution.py:766
  130.2 6.6 %collective-permute-start.16 = (bf16[72,768]{1,0:T(8,128)(2,1)S(1)}, bf16[72,768]{1,0:T(8,128)(2,1)S(1)}, u32[]{:S(2)}, u32[]{:S(2)}) collective-permute-start(bf16[72,768]{1,0:T(8,128)(2,1)S(1)} %pad_maximum_fusion.5), channel_id=1, source_target_pairs={{0,16},{2,18},{4,20},{6,22},{8,24},{10,26},{12,28},{14,30},{16,0},... | collective-permute-start | bytes 331784 | tf_op jit(solution)/shard_map/ppermute | solution.py:766
  131.2 15.5 %collective-permute-start.20 = (bf16[384,768]{1,0:T(8,128)(2,1)S(1)}, bf16[384,768]{1,0:T(8,128)(2,1)S(1)}, u32[]{:S(2)}, u32[]{:S(2)}) collective-permute-start(bf16[384,768]{1,0:T(8,128)(2,1)S(1)} %pad_maximum_fusion), channel_id=1, source_target_pairs={{0,4},{2,6},{4,0},{6,2},{8,12},{10,14},{12,8},{14,10},{16,20},{18,... | collective-permute-start | bytes 1769480 | tf_op jit(solution)/shard_map/ppermute | solution.py:766
  134.2 7.0 %copy-start.5 = (bf16[1024,384]{1,0:T(8,128)(2,1)S(1)}, bf16[1024,384]{1,0:T(8,128)(2,1)}, u32[]{:S(2)}) copy-start(bf16[1024,384]{1,0:T(8,128)(2,1)} %refs_1_.1) | copy-start | bytes 2359300
  136.9 4.0 %collective-permute-start.18 = (bf16[24,768]{1,0:T(8,128)(2,1)S(1)}, bf16[24,768]{1,0:T(8,128)(2,1)S(1)}, u32[]{:S(2)}, u32[]{:S(2)}) collective-permute-start(bf16[24,768]{1,0:T(8,128)(2,1)S(1)} %slice.218), channel_id=1, source_target_pairs={{0,1},{1,0},{2,3},{3,2},{4,5},{5,4},{6,7},{7,6},{8,9},{9,8},{10,11... | collective-permute-start | bytes 110600 | tf_op jit(solution)/shard_map/ppermute | solution.py:761
  141.0 5.8 %collective-permute-start.19 = (bf16[72,768]{1,0:T(8,128)(2,1)S(1)}, bf16[72,768]{1,0:T(8,128)(2,1)S(1)}, u32[]{:S(2)}, u32[]{:S(2)}) collective-permute-start(bf16[72,768]{1,0:T(8,128)(2,1)S(1)} %pad_maximum_fusion.6), channel_id=1, source_target_pairs={{0,16},{2,18},{4,20},{6,22},{8,24},{10,26},{12,28},{14,30},{16,0},... | collective-permute-start | bytes 331784 | tf_op jit(solution)/shard_map/ppermute | solution.py:766
  146.8 7.5 %collective-permute-start.25 = (bf16[768,768]{1,0:T(8,128)(2,1)S(1)}, bf16[768,768]{1,0:T(8,128)(2,1)S(1)}, u32[]{:S(2)}, u32[]{:S(2)}) collective-permute-start(bf16[768,768]{1,0:T(8,128)(2,1)S(1)} %constant_dynamic-update-slice_fusion.first), channel_id=1, source_target_pairs={{0,2},{2,0},{4,6},{6,4},{8,10},{10,8},{12,14},{14,12},{16,18},{18,... | collective-permute-start | bytes 3538952 | tf_op jit(solution)/shard_map/ppermute | solution.py:766
  147.0 5.5 %collective-permute-start.23 = (bf16[144,384]{1,0:T(8,128)(2,1)S(1)}, bf16[144,384]{1,0:T(8,128)(2,1)S(1)}, u32[]{:S(2)}, u32[]{:S(2)}) collective-permute-start(bf16[144,384]{1,0:T(8,128)(2,1)S(1)} %get-tuple-element.272), channel_id=1, source_target_pairs={{0,4},{2,6},{4,0},{6,2},{8,12},{10,14},{12,8},{14,10},{16,20},{18,... | collective-permute-start | bytes 331784 | tf_op jit(solution)/shard_map/ppermute | solution.py:766
  148.4 5.2 %collective-permute-start.21 = (bf16[144,384]{1,0:T(8,128)(2,1)S(1)}, bf16[144,384]{1,0:T(8,128)(2,1)S(1)}, u32[]{:S(2)}, u32[]{:S(2)}) collective-permute-start(bf16[144,384]{1,0:T(8,128)(2,1)S(1)} %get-tuple-element.273), channel_id=1, source_target_pairs={{0,8},{2,10},{4,12},{6,14},{8,0},{10,2},{12,4},{14,6},{16,24},{18,... | collective-permute-start | bytes 331784 | tf_op jit(solution)/shard_map/ppermute | solution.py:766
  152.5 7.1 %collective-permute-start.24 = (bf16[288,384]{1,0:T(8,128)(2,1)S(1)}, bf16[288,384]{1,0:T(8,128)(2,1)S(1)}, u32[]{:S(2)}, u32[]{:S(2)}) collective-permute-start(bf16[288,384]{1,0:T(8,128)(2,1)S(1)} %pad_maximum_fusion.4), channel_id=1, source_target_pairs={{0,8},{2,10},{4,12},{6,14},{8,0},{10,2},{12,4},{14,6},{16,24},{18,... | collective-permute-start | bytes 663560 | tf_op jit(solution)/shard_map/ppermute | solution.py:766
  153.6 6.8 %collective-permute-start.22 = (bf16[288,384]{1,0:T(8,128)(2,1)S(1)}, bf16[288,384]{1,0:T(8,128)(2,1)S(1)}, u32[]{:S(2)}, u32[]{:S(2)}) collective-permute-start(bf16[288,384]{1,0:T(8,128)(2,1)S(1)} %pad_maximum_fusion.3), channel_id=1, source_target_pairs={{0,4},{2,6},{4,0},{6,2},{8,12},{10,14},{12,8},{14,10},{16,20},{18,... | collective-permute-start | bytes 663560 | tf_op jit(solution)/shard_map/ppermute | solution.py:766
  160.5 2.5 %collective-permute-start.26 = (bf16[576,768]{1,0:T(8,128)(2,1)S(1)}, bf16[576,768]{1,0:T(8,128)(2,1)S(1)}, u32[]{:S(2)}, u32[]{:S(2)}) collective-permute-start(bf16[576,768]{1,0:T(8,128)(2,1)S(1)} %maximum_maximum_fusion.first), channel_id=1, source_target_pairs={{0,2},{2,0},{4,6},{6,4},{8,10},{10,8},{12,14},{14,12},{16,18},{18,... | collective-permute-start | bytes 2654216 | tf_op jit(solution)/shard_map/ppermute | solution.py:766
  (5 other events, 5.8 us)

commit v5 on v4

--- a/solution.py
+++ b/solution.py
@@ -9,7 +9,7 @@
 
 EPSILON = 1e-05
 CHUNK = 128
-PROJECT_BLOCK, MIX_BLOCK, GATE_BLOCK, BACK_BLOCK, RATES_BLOCK = 256, 256, 256, 128, 512
+PROJECT_BLOCK, MIX_BLOCK, GATE_BLOCK, GATE_BACK_BLOCK, BACK_BLOCK, RATES_BLOCK = 256, 256, 512, 256, 128, 512
 LANES = 128
 F32 = jnp.float32
 BF16 = jnp.bfloat16
@@ -941,6 +941,8 @@
     branch_got = swap_mp(after(branch_oth, sums))
     sums_in = after(sums, branch_oth)
 
+    block = GATE_BACK_BLOCK
+    up, states, up_lanes = rows_of(block), states_of(block), lanes_of(block)
     g, dgp, dbr, dc, gb, gf, rd_gate, row_sums, small = call(
         partial(gate_back_kernel, block=block, inner_width=inner_width, **sizes),
         rows // block,
@@ -1066,27 +1068,25 @@
         jnp.zeros((rows, 4 * LANES), F32),
         jnp.zeros((8, rows), F32),
     )
-    parts = 4
-    count = rows // BACK_BLOCK // parts
     g = after(g, send)
     sent, x = swap_dp(send, order_a[1]), None
-    for k in range(parts):
-        outs = back_part((parts - k) * count - 1, count, g, state)
+    left = rows // BACK_BLOCK
+    for k, share in enumerate((2, 4, 4)):
+        count = rows // BACK_BLOCK // share
+        outs = back_part(left - 1, count, g, state)
+        left -= count
         rest, rates, rd_rest, gconv, ext_carry, carry = outs
-        if k == 1:
+        h = keep.shape[0] // 2
+        if k < 2:
             sent, carry = lax.optimization_barrier((sent, carry))
-        elif k == 2:
-            sent, carry, branch_got = lax.optimization_barrier((sent, carry, branch_got))
-        elif k == 3:
+            if k == 1:
+                carry, branch_got = lax.optimization_barrier((carry, branch_got))
+            keep, send = add_low(keep[:h], sent[:h]), add_low(keep[h:], sent[h:])
+            carry = after(carry, send)
+            sent = swap_dp(send, order_a[k + 2])
+        else:
             sent, rest = lax.optimization_barrier((sent, rest))
-        if k > 0:
-            h = keep.shape[0] // 2
-            if k < 3:
-                keep, send = add_low(keep[:h], sent[:h]), add_low(keep[h:], sent[h:])
-                carry = after(carry, send)
-                sent = swap_dp(send, order_a[k + 1])
-            else:
-                x = rest_of_dp(add_low(keep, sent))
+            x = rest_of_dp(add_low(keep, sent))
         state = (ext_carry, carry, gconv, rest, rates, rd_rest)
 
     block = RATES_BLOCK

time: 166 us -> 166 us (level)
  waiting for transfers between devices: 35.9 us -> 33.7 us
  starting transfers between devices: 29.6 us -> 31.4 us
    ppermute x20, starting transfers between devices: 20 us -> 21.8 us  [swap_dp(): return lax.ppermute(x, 'dp', [(i, i ^ 1 << bit) for i in range(size)])]
    pallas_call x9 -> x8, Pallas kernels: 55.4 us -> 54.2 us  [call(): pl.pallas_call(looped, out_shape=[pltpu.VMEM(o.shape, o.dtype) for o in o...]
    unnamed x23 -> x27, local copies, waits for them, and re-layouts: 7.91 us -> 8.55 us
  transfers between devices with their start and end apart: 27 -> 27, of which waited for: 18 -> 16; matrix products, arithmetic and copies ran while one was open for 6% -> 6% of each run, Pallas kernels for 35% -> 36%
where the time goes in v5:
time: 166 us
  Pallas kernels  74 us (45%)
  waiting for transfers between devices  33.7 us (20%)
  starting transfers between devices  31.4 us (19%)
  local copies, waits for them, and re-layouts  12.3 us (7%)
  other arithmetic  6.89 us (4%)
  matrix products  5.43 us (3%)
  between operations  1.96 us (1%)
    pallas_call x8, Pallas kernels, call(): pl.pallas_call(looped, out_shape=[pltpu.VMEM(o.shape, o.dtype) for o in o...  54.2 us
    ppermute x20, waiting for transfers between devices, swap_dp(): return lax.ppermute(x, 'dp', [(i, i ^ 1 << bit) for i in range(size)])  26.9 us
    ppermute x20, starting transfers between devices, swap_dp(): return lax.ppermute(x, 'dp', [(i, i ^ 1 << bit) for i in range(size)])  21.8 us
    pallas_call x8, Pallas kernels, whole(): pl.pallas_call(kernel, out_shape=[pltpu.VMEM(o.shape, o.dtype) if in_vmem...  18.3 us
    ppermute x7, starting transfers between devices, swap_mp(): return lax.ppermute(x, 'mp', [(0, 1), (1, 0)])  9.57 us
    unnamed x27, local copies, waits for them, and re-layouts  8.55 us
    ppermute x7, waiting for transfers between devices, swap_mp(): return lax.ppermute(x, 'mp', [(0, 1), (1, 0)])  6.78 us
    dot_general x5, matrix products, mm_tn(): lax.dot_general(a, b, (((0,), (0,)), ((), ())), preferred_element_type=F32)  5.43 us
  transfers between devices with their start and end apart: 27, of which 16 were waited for; matrix products, arithmetic and copies ran while one was open for 6% of the time, Pallas kernels for 36%

profile of v5, /device:TPU:0, one launch (start us, length us, event | category | flops | bytes accessed | tf_op | source)
XLA Modules:
  0.0 165.7 jit_solution(5356246649472340595)
XLA Ops:
  1.3 3.0 %collective-permute-start.1 = (bf16[1,384]{1,0:T(2,128)(2,1)S(1)}, bf16[1,384]{1,0:T(2,128)(2,1)S(1)}, u32[]{:S(2)}, u32[]{:S(2)}) collective-permute-start(bf16[1,384]{1,0:T(2,128)(2,1)S(1)} %concatenate.72), channel_id=1, source_target_pairs={{0,1},{1,0},{2,3},{3,2},{4,5},{5,4},{6,7},{7,6},{8,9},{9,8},{10,11... | collective-permute-start | bytes 2312 | tf_op jit(solution)/shard_map/ppermute | solution.py:761
  19.2 4.3 %collective-permute-done.refs_1_ = bf16[1024,384]{1,0:T(8,128)(2,1)S(1)} collective-permute-done((bf16[1024,384]{1,0:T(8,128)(2,1)}, bf16[1024,384]{1,0:T(8,128)(2,1)S(1)}, u32[]{:S(2)}, u32[]{:S(2)}) %collective-permute-start) | collective-permute-done | bytes 786464 | tf_op jit(solution)/shard_map/ppermute | solution.py:761
  23.8 11.2 %project.1 = (bf16[1024,768]{1,0:T(8,128)(2,1)S(1)}, f32[1024,768]{1,0:T(8,128)S(1)}, bf16[1024,1024]{1,0:T(8,128)(2,1)S(1)}, bf16[1024,1024]{1,0:T(8,128)(2,1)S...) custom-call(s32[3]{0:T(128)S(1)} %pad_add_fusion.scalars, ...), custom_call_target="tpu_custom_call" | custom-call | flops 6000000000 | bytes 36000000 | tf_op jit(solution)/shard_map/project/pallas_call | solution.py:729
  35.0 7.1 %mix.1 = (f32[1024,768]{1,0:T(8,128)S(1)}, bf16[8,64,768]{2,1,0:T(8,128)(2,1)S(1)}) custom-call(s32[3]{0:T(128)S(1)} %pad_add_fusion.scalars, f32[1024,768]{1,0:T(8,128)S(1)} %get-tuple-element.137.refs_0_.refs_3_.refs_1_, bf16[1024,256]{1,0:T(8,128)(2,1)S(1)} %get-tuple-element.138.refs_1_.refs_8_.refs_2_, ...), custom_call_target="tpu_custom_call" | custom-call | flops 3500000000 | bytes 21000000 | tf_op jit(solution)/shard_map/mix/pallas_call | solution.py:729
  42.1 3.0 %gate.1 = (f32[1024,768]{1,0:T(8,128)S(1)}, bf16[1024,768]{1,0:T(8,128)(2,1)S(1)}, f32[8,1024]{1,0:T(8,128)S(1)}) custom-call(s32[3]{0:T(128)S(1)} %pad_add_fusion.scalars, f32[1024,768]{1,0:T(8,128)S(1)} %get-tuple-element.143.refs_0_.refs_2_, f32[1024,768]{1,0:T(8,128)S(1)} %get-tuple-element.144.refs_1_, ...), custom_call_target="tpu_custom_call" | custom-call | flops 1500000000 | bytes 9000000 | tf_op jit(solution)/shard_map/gate/pallas_call | solution.py:729
  45.1 1.7 %collective-permute-start.3 = (f32[8,1024]{1,0:T(8,128)S(1)}, f32[8,1024]{1,0:T(8,128)S(1)}, u32[]{:S(2)}, u32[]{:S(2)}) collective-permute-start(f32[8,1024]{1,0:T(8,128)S(1)} %get-tuple-element.148), channel_id=1, source_target_pairs={{0,1},{1,0},{2,3},{3,2},{4,5},{5,4},{6,7},{7,6},{8,9},{9,8},{10,11... | collective-permute-start | bytes 98312 | tf_op jit(solution)/shard_map/ppermute | solution.py:761
  46.9 2.4 %branch_oth.1 = bf16[1024,384]{1,0:T(8,128)(2,1)} custom-call(s32[3]{0:T(128)S(1)} %pad_add_fusion.scalars, bf16[1024,768]{1,0:T(8,128)(2,1)S(1)} %get-tuple-element.159.gz, bf16[768,768]{1,0:T(8,128)(2,1)S(1)} %get-tuple-element.147.refs_4_.po), custom_call_target="tpu_custom_call" | custom-call | flops 1500000000 | bytes 9000000 | tf_op jit(solution)/shard_map/branch_oth/pallas_call | solution.py:746
  49.3 7.8 %gate_back.1 = (bf16[1024,768]{1,0:T(8,128)(2,1)S(1)}, bf16[1024,768]{1,0:T(8,128)(2,1)S(1)}, bf16[1024,768]{1,0:T(8,128)(2,1)S(1)}, f32[1024,128]{1,0:T(8,128)S...) custom-call(s32[3]{0:T(128)S(1)} %pad_add_fusion.scalars, ...), custom_call_target="tpu_custom_call" | custom-call | flops 4000000000 | bytes 24000000 | tf_op jit(solution)/shard_map/gate_back/pallas_call | solution.py:729
  68.3 11.1 %mix_back.3 = (bf16[1024,1024]{1,0:T(8,128)(2,1)S(1)}, f32[1024,512]{1,0:T(8,128)S(1)}, f32[8,1024]{1,0:T(8,128)S(1)}, f32[8,1024]{1,0:T(8,128)S(1)}, f32[8,1024]{1,0:T(8,128)S(1)}, /*index=5*/f32[64,768]{1,0:T(8,128)S(1)}) custom-call(s32[3]{0:T(128)S(1)} %pad_add_fusion.scalars, ...), custom_call_target="tpu_custom_call", output_to_operand_aliasing={{0}: (21, {}), {1}: (22, {}), {2}: (23, {})} | custom-call | flops 6000000000 | bytes 36000000 | tf_op jit(solution)/shard_map/mix_back/pallas_call | solution.py:729
  80.3 1.7 %collective-permute-start.6 = (bf16[192,768]{1,0:T(8,128)(2,1)S(1)}, bf16[192,768]{1,0:T(8,128)(2,1)S(1)}, u32[]{:S(2)}, u32[]{:S(2)}) collective-permute-start(bf16[192,768]{1,0:T(8,128)(2,1)S(1)} %get-tuple-element.255), channel_id=1, source_target_pairs={{0,8},{2,10},{4,12},{6,14},{8,0},{10,2},{12,4},{14,6},{16,24},{18,... | collective-permute-start | bytes 884744 | tf_op jit(solution)/shard_map/ppermute | solution.py:766
  82.0 5.8 %mix_back.4 = (bf16[1024,1024]{1,0:T(8,128)(2,1)S(1)}, f32[1024,512]{1,0:T(8,128)S(1)}, f32[8,1024]{1,0:T(8,128)S(1)}, f32[8,1024]{1,0:T(8,128)S(1)}, f32[8,1024]{1,0:T(8,128)S(1)}, /*index=5*/f32[64,768]{1,0:T(8,128)S(1)}) custom-call(s32[3]{0:T(128)S(1)} %pad_add_fusion.scalars, ...), custom_call_target="tpu_custom_call", output_to_operand_aliasing={{0}: (21, {}), {1}: (22, {}), {2}: (23, {})} | custom-call | flops 3000000000 | bytes 18000000 | tf_op jit(solution)/shard_map/mix_back/pallas_call | solution.py:729
  88.6 2.7 %collective-permute-start.8 = (bf16[96,768]{1,0:T(8,128)(2,1)S(1)}, bf16[96,768]{1,0:T(8,128)(2,1)S(1)}, u32[]{:S(2)}, u32[]{:S(2)}) collective-permute-start(bf16[96,768]{1,0:T(8,128)(2,1)S(1)} %add_convert_fusion.10), channel_id=1, source_target_pairs={{0,16},{2,18},{4,20},{6,22},{8,24},{10,26},{12,28},{14,30},{16,0},... | collective-permute-start | bytes 442376 | tf_op jit(solution)/shard_map/ppermute | solution.py:766
  91.3 6.5 %mix_back.5 = (bf16[1024,1024]{1,0:T(8,128)(2,1)S(1)}, f32[1024,512]{1,0:T(8,128)S(1)}, f32[8,1024]{1,0:T(8,128)S(1)}, f32[8,1024]{1,0:T(8,128)S(1)}, f32[8,1024]{1,0:T(8,128)}, /*index=5*/f32[64,768]{1,0:T(8,128)}) custom-call(s32[3]{0:T(128)S(1)} %pad_add_fusion.scalars, ...), custom_call_target="tpu_custom_call", output_to_operand_aliasing={{0}: (21, {}), {1}: (22, {}), {2}: (23, {})} | custom-call | flops 3000000000 | bytes 18000000 | tf_op jit(solution)/shard_map/mix_back/pallas_call | solution.py:729
  100.4 1.6 rates.1
  102.0 2.8 %back_oth.1 = bf16[1040,384]{1,0:T(8,128)(2,1)S(1)} custom-call(s32[3]{0:T(128)S(1)} %pad_add_fusion.scalars, bf16[1024,768]{1,0:T(8,128)(2,1)S(1)} %get-tuple-element.156.dgp, bf16[1024,1024]{1,0:T(8,128)(2,1)S(1)} %get-tuple-element.209.rest, bf16[1024,128]{1,0:T(8,128)(2,1)S(1)} %get-tuple-element.196.dz, f32[8,1024]{1,0:T(8,128)S(1)} %get-tuple-element.205.rd, ...), custom_call_target="tpu_custom_call" | custom-call | tf_op jit(solution)/shard_map/back_oth/pallas_call | solution.py:746
  105.9 1.6 pack_late.1
  108.2 2.5 %collective-permute-start.13 = (bf16[192,768]{1,0:T(8,128)(2,1)S(1)}, bf16[192,768]{1,0:T(8,128)(2,1)S(1)}, u32[]{:S(2)}, u32[]{:S(2)}) collective-permute-start(bf16[192,768]{1,0:T(8,128)(2,1)S(1)} %pad_maximum_fusion.1), channel_id=1, source_target_pairs={{0,8},{2,10},{4,12},{6,14},{8,0},{10,2},{12,4},{14,6},{16,24},{18,... | collective-permute-start | bytes 884744 | tf_op jit(solution)/shard_map/ppermute | solution.py:766
  112.4 2.3 %collective-permute-start.12 = (bf16[288,384]{1,0:T(8,128)(2,1)S(1)}, bf16[288,384]{1,0:T(8,128)(2,1)S(1)}, u32[]{:S(2)}, u32[]{:S(2)}) collective-permute-start(bf16[288,384]{1,0:T(8,128)(2,1)S(1)} %get-tuple-element.208), channel_id=1, source_target_pairs={{0,8},{2,10},{4,12},{6,14},{8,0},{10,2},{12,4},{14,6},{16,24},{18,... | collective-permute-start | bytes 663560 | tf_op jit(solution)/shard_map/ppermute | solution.py:766
  116.2 2.8 %back_own.1 = f32[1024,384]{1,0:T(8,128)S(1)} custom-call(s32[3]{0:T(128)S(1)} %pad_add_fusion.scalars, bf16[1024,768]{1,0:T(8,128)(2,1)S(1)} %get-tuple-element.156.dgp, bf16[1024,1024]{1,0:T(8,128)(2,1)S(1)} %get-tuple-element.209.rest, bf16[1024,128]{1,0:T(8,128)(2,1)S(1)} %get-tuple-element.196.dz, f32[8,1024]{1,0:T(8,128)S(1)} %get-tuple-element.205.rd, ...), custom_call_target="tpu_custom_call" | custom-call | tf_op jit(solution)/shard_map/back_own/pallas_call | solution.py:746
  119.0 4.0 %collective-permute-done.12 = bf16[288,384]{1,0:T(8,128)(2,1)S(1)} collective-permute-done((bf16[288,384]{1,0:T(8,128)(2,1)S(1)}, bf16[288,384]{1,0:T(8,128)(2,1)S(1)}, u32[]{:S(2)}, u32[]{:S(2)}) %collective-permute-start.12) | collective-permute-done | bytes 221216 | tf_op jit(solution)/shard_map/ppermute | solution.py:766
  123.1 1.8 %collective-permute-start.14 = (bf16[144,384]{1,0:T(8,128)(2,1)S(1)}, bf16[144,384]{1,0:T(8,128)(2,1)S(1)}, u32[]{:S(2)}, u32[]{:S(2)}) collective-permute-start(bf16[144,384]{1,0:T(8,128)(2,1)S(1)} %get-tuple-element.259), channel_id=1, source_target_pairs={{0,8},{2,10},{4,12},{6,14},{8,0},{10,2},{12,4},{14,6},{16,24},{18,... | collective-permute-start | bytes 331784 | tf_op jit(solution)/shard_map/ppermute | solution.py:766
  128.0 1.7 %collective-permute-done.15 = bf16[144,384]{1,0:T(8,128)(2,1)S(1)} collective-permute-done((bf16[144,384]{1,0:T(8,128)(2,1)S(1)}, bf16[144,384]{1,0:T(8,128)(2,1)S(1)}, u32[]{:S(2)}, u32[]{:S(2)}) %collective-permute-start.15) | collective-permute-done | bytes 110624 | tf_op jit(solution)/shard_map/ppermute | solution.py:766
  134.4 2.2 %collective-permute-done.16 = bf16[72,768]{1,0:T(8,128)(2,1)S(1)} collective-permute-done((bf16[72,768]{1,0:T(8,128)(2,1)S(1)}, bf16[72,768]{1,0:T(8,128)(2,1)S(1)}, u32[]{:S(2)}, u32[]{:S(2)}) %collective-permute-start.16) | collective-permute-done | bytes 110624 | tf_op jit(solution)/shard_map/ppermute | solution.py:766
  136.7 1.6 collective-permute-start.18
  138.3 2.4 %collective-permute-done.18 = bf16[24,768]{1,0:T(8,128)(2,1)S(1)} collective-permute-done((bf16[24,768]{1,0:T(8,128)(2,1)S(1)}, bf16[24,768]{1,0:T(8,128)(2,1)S(1)}, u32[]{:S(2)}, u32[]{:S(2)}) %collective-permute-start.18) | collective-permute-done | bytes 36896 | tf_op jit(solution)/shard_map/ppermute | solution.py:761
  141.2 1.7 %fusion.2 = f32[1024,384]{1,0:T(8,128)} fusion(bf16[1024,384]{1,0:T(8,128)(2,1)S(1)} %copy-done.1, f32[1024,384]{1,0:T(8,128)S(1)} %back_own.1, bf16[1024,384]{1,0:T(8,128)(2,1)S(1)} %copy-done.5, f32[1024]{0:T(1024)S(1)} %get-tuple-element.246, f32[384]{0:T(512)S(1)} %convert_element_type.314, bf16[1040,384]{1,0:T(8,128)(2,1)S(1)} %collective-permute-done.17, ...), kind=kLoop, calls=%fused_computation.5 | loop fusion | flops 3538944 | bytes 5514752 | tf_op jit(solution)/shard_map/sub | solution.py:1184
  142.9 3.6 %collective-permute-done.19 = bf16[72,768]{1,0:T(8,128)(2,1)S(1)} collective-permute-done((bf16[72,768]{1,0:T(8,128)(2,1)S(1)}, bf16[72,768]{1,0:T(8,128)(2,1)S(1)}, u32[]{:S(2)}, u32[]{:S(2)}) %collective-permute-start.19) | collective-permute-done | bytes 110624 | tf_op jit(solution)/shard_map/ppermute | solution.py:766
  148.2 4.0 %collective-permute-done.23 = bf16[144,384]{1,0:T(8,128)(2,1)S(1)} collective-permute-done((bf16[144,384]{1,0:T(8,128)(2,1)S(1)}, bf16[144,384]{1,0:T(8,128)(2,1)S(1)}, u32[]{:S(2)}, u32[]{:S(2)}) %collective-permute-start.23) | collective-permute-done | bytes 110624 | tf_op jit(solution)/shard_map/ppermute | solution.py:766
  154.0 3.0 %unpack_early.1 = (f32[768,768]{1,0:T(8,128)}, f32[768,768]{1,0:T(8,128)}) custom-call(s32[3]{0:T(128)S(1)} %pad_add_fusion.scalars, bf16[768,768]{1,0:T(8,128)(2,1)S(1)} %constant_dynamic-update-slice_fusion.first, bf16[768,768]{1,0:T(8,128)(2,1)S(1)} %collective-permute-done.25.second), custom_call_target="tpu_custom_call" | custom-call | tf_op jit(solution)/shard_map/unpack_early/pallas_call | solution.py:746
  157.1 2.3 %collective-permute-done.24 = bf16[288,384]{1,0:T(8,128)(2,1)S(1)} collective-permute-done((bf16[288,384]{1,0:T(8,128)(2,1)S(1)}, bf16[288,384]{1,0:T(8,128)(2,1)S(1)}, u32[]{:S(2)}, u32[]{:S(2)}) %collective-permute-start.24) | collective-permute-done | bytes 221216 | tf_op jit(solution)/shard_map/ppermute | solution.py:766
  160.4 2.4 %collective-permute-done.26.second = bf16[576,768]{1,0:T(8,128)(2,1)S(1)} collective-permute-done((bf16[576,768]{1,0:T(8,128)(2,1)S(1)}, bf16[576,768]{1,0:T(8,128)(2,1)S(1)}, u32[]{:S(2)}, u32[]{:S(2)}) %collective-permute-start.26) | collective-permute-done | bytes 884768 | tf_op jit(solution)/shard_map/ppermute | solution.py:766
  162.8 2.7 %unpack_late.1 = (f32[768,768]{1,0:T(8,128)}, f32[768,256]{1,0:T(8,128)}, f32[12,2,768]{2,1,0:T(2,128)}, f32[4,768]{1,0:T(4,128)}, f32[768]{0:T(1024)}, /*index=...) custom-call(s32[3]{0:T(128)S(1)} %pad_add_fusion.scalars, ...), custom_call_target="tpu_custom_call" | custom-call | tf_op jit(solution)/shard_map/unpack_late/pallas_call | solution.py:746
  (127 shorter events, 48.4 us)
Async XLA Ops:
  1.3 17.8 %collective-permute-start.1 = (bf16[1,384]{1,0:T(2,128)(2,1)S(1)}, bf16[1,384]{1,0:T(2,128)(2,1)S(1)}, u32[]{:S(2)}, u32[]{:S(2)}) collective-permute-start(bf16[1,384]{1,0:T(2,128)(2,1)S(1)} %concatenate.72), channel_id=1, source_target_pairs={{0,1},{1,0},{2,3},{3,2},{4,5},{5,4},{6,7},{7,6},{8,9},{9,8},{10,11... | collective-permute-start | bytes 2312 | tf_op jit(solution)/shard_map/ppermute | solution.py:761
  4.3 19.2 %collective-permute-start = (bf16[1024,384]{1,0:T(8,128)(2,1)}, bf16[1024,384]{1,0:T(8,128)(2,1)S(1)}, u32[]{:S(2)}, u32[]{:S(2)}) collective-permute-start(bf16[1024,384]{1,0:T(8,128)(2,1)} %refs_0_.1), channel_id=1, source_target_pairs={{0,1},{1,0},{2,3},{3,2},{4,5},{5,4},{6,7},{7,6},{8,9},{9,8},{10,11... | collective-permute-start | bytes 2359304 | tf_op jit(solution)/shard_map/ppermute | solution.py:761
  19.1 15.9 %copy-start.9 = (bf16[384,768]{1,0:T(8,128)(2,1)}, bf16[384,768]{1,0:T(8,128)(2,1)S(1)}, u32[]{:S(2)}) copy-start(bf16[384,768]{1,0:T(8,128)(2,1)S(1)} %get-tuple-element.197.w_state_t) | copy-start | bytes 1769476
  23.5 18.6 %collective-permute-start.2 = (bf16[1024,384]{1,0:T(8,128)(2,1)S(1)}, bf16[1024,384]{1,0:T(8,128)(2,1)S(1)}, u32[]{:S(2)}, u32[]{:S(2)}) collective-permute-start(bf16[1024,384]{1,0:T(8,128)(2,1)S(1)} %copy-done.4), channel_id=1, source_target_pairs={{0,1},{1,0},{2,3},{3,2},{4,5},{5,4},{6,7},{7,6},{8,9},{9,8},{10,11... | collective-permute-start | bytes 2359304 | tf_op jit(solution)/shard_map/ppermute | solution.py:761
  45.1 4.1 %collective-permute-start.3 = (f32[8,1024]{1,0:T(8,128)S(1)}, f32[8,1024]{1,0:T(8,128)S(1)}, u32[]{:S(2)}, u32[]{:S(2)}) collective-permute-start(f32[8,1024]{1,0:T(8,128)S(1)} %get-tuple-element.148), channel_id=1, source_target_pairs={{0,1},{1,0},{2,3},{3,2},{4,5},{5,4},{6,7},{7,6},{8,9},{9,8},{10,11... | collective-permute-start | bytes 98312 | tf_op jit(solution)/shard_map/ppermute | solution.py:761
  58.6 1.5 copy-start.3
  61.5 2.9 %collective-permute-start.4 = (bf16[768,768]{1,0:T(8,128)(2,1)S(1)}, bf16[768,768]{1,0:T(8,128)(2,1)S(1)}, u32[]{:S(2)}, u32[]{:S(2)}) collective-permute-start(bf16[768,768]{1,0:T(8,128)(2,1)S(1)} %get-tuple-element.158), channel_id=1, source_target_pairs={{0,2},{2,0},{4,6},{6,4},{8,10},{10,8},{12,14},{14,12},{16,18},{18,... | collective-permute-start | bytes 3538952 | tf_op jit(solution)/shard_map/ppermute | solution.py:766
  64.7 15.4 %collective-permute-start.5 = (bf16[384,768]{1,0:T(8,128)(2,1)S(1)}, bf16[384,768]{1,0:T(8,128)(2,1)S(1)}, u32[]{:S(2)}, u32[]{:S(2)}) collective-permute-start(bf16[384,768]{1,0:T(8,128)(2,1)S(1)} %get-tuple-element.249), channel_id=1, source_target_pairs={{0,4},{2,6},{4,0},{6,2},{8,12},{10,14},{12,8},{14,10},{16,20},{18,... | collective-permute-start | bytes 1769480 | tf_op jit(solution)/shard_map/ppermute | solution.py:766
  66.3 22.3 %collective-permute-start.7 = (bf16[1024,384]{1,0:T(8,128)(2,1)}, bf16[1024,384]{1,0:T(8,128)(2,1)S(1)}, u32[]{:S(2)}, u32[]{:S(2)}) collective-permute-start(bf16[1024,384]{1,0:T(8,128)(2,1)} %branch_oth.1), channel_id=1, source_target_pairs={{0,1},{1,0},{2,3},{3,2},{4,5},{5,4},{6,7},{7,6},{8,9},{9,8},{10,11... | collective-permute-start | bytes 2359304 | tf_op jit(solution)/shard_map/ppermute | solution.py:761
  80.3 8.3 %collective-permute-start.6 = (bf16[192,768]{1,0:T(8,128)(2,1)S(1)}, bf16[192,768]{1,0:T(8,128)(2,1)S(1)}, u32[]{:S(2)}, u32[]{:S(2)}) collective-permute-start(bf16[192,768]{1,0:T(8,128)(2,1)S(1)} %get-tuple-element.255), channel_id=1, source_target_pairs={{0,8},{2,10},{4,12},{6,14},{8,0},{10,2},{12,4},{14,6},{16,24},{18,... | collective-permute-start | bytes 884744 | tf_op jit(solution)/shard_map/ppermute | solution.py:766
  88.6 9.2 %collective-permute-start.8 = (bf16[96,768]{1,0:T(8,128)(2,1)S(1)}, bf16[96,768]{1,0:T(8,128)(2,1)S(1)}, u32[]{:S(2)}, u32[]{:S(2)}) collective-permute-start(bf16[96,768]{1,0:T(8,128)(2,1)S(1)} %add_convert_fusion.10), channel_id=1, source_target_pairs={{0,16},{2,18},{4,20},{6,22},{8,24},{10,26},{12,28},{14,30},{16,0},... | collective-permute-start | bytes 442376 | tf_op jit(solution)/shard_map/ppermute | solution.py:766
  100.0 8.0 %collective-permute-start.9 = (bf16[96,768]{1,0:T(8,128)(2,1)S(1)}, bf16[96,768]{1,0:T(8,128)(2,1)S(1)}, u32[]{:S(2)}, u32[]{:S(2)}) collective-permute-start(bf16[96,768]{1,0:T(8,128)(2,1)S(1)} %add_convert_fusion.8), channel_id=1, source_target_pairs={{0,16},{2,18},{4,20},{6,22},{8,24},{10,26},{12,28},{14,30},{16,0},... | collective-permute-start | bytes 442376 | tf_op jit(solution)/shard_map/ppermute | solution.py:766
  105.9 2.2 %copy-start.11 = (bf16[384]{0:T(512)(128)(2,1)S(1)}, bf16[384]{0:T(512)(128)(2,1)}, u32[]{:S(2)}) copy-start(bf16[384]{0:T(512)(128)(2,1)} %param.18) | copy-start | bytes 2308
  108.0 2.6 %collective-permute-start.10 = (bf16[576,768]{1,0:T(8,128)(2,1)S(1)}, bf16[576,768]{1,0:T(8,128)(2,1)S(1)}, u32[]{:S(2)}, u32[]{:S(2)}) collective-permute-start(bf16[576,768]{1,0:T(8,128)(2,1)S(1)} %get-tuple-element.206), channel_id=1, source_target_pairs={{0,2},{2,0},{4,6},{6,4},{8,10},{10,8},{12,14},{14,12},{16,18},{18,... | collective-permute-start | bytes 2654216 | tf_op jit(solution)/shard_map/ppermute | solution.py:766
  108.2 10.9 %collective-permute-start.13 = (bf16[192,768]{1,0:T(8,128)(2,1)S(1)}, bf16[192,768]{1,0:T(8,128)(2,1)S(1)}, u32[]{:S(2)}, u32[]{:S(2)}) collective-permute-start(bf16[192,768]{1,0:T(8,128)(2,1)S(1)} %pad_maximum_fusion.1), channel_id=1, source_target_pairs={{0,8},{2,10},{4,12},{6,14},{8,0},{10,2},{12,4},{14,6},{16,24},{18,... | collective-permute-start | bytes 884744 | tf_op jit(solution)/shard_map/ppermute | solution.py:766
  110.9 8.2 %collective-permute-start.11 = (bf16[288,384]{1,0:T(8,128)(2,1)S(1)}, bf16[288,384]{1,0:T(8,128)(2,1)S(1)}, u32[]{:S(2)}, u32[]{:S(2)}) collective-permute-start(bf16[288,384]{1,0:T(8,128)(2,1)S(1)} %get-tuple-element.207), channel_id=1, source_target_pairs={{0,4},{2,6},{4,0},{6,2},{8,12},{10,14},{12,8},{14,10},{16,20},{18,... | collective-permute-start | bytes 663560 | tf_op jit(solution)/shard_map/ppermute | solution.py:766
  112.4 10.6 %collective-permute-start.12 = (bf16[288,384]{1,0:T(8,128)(2,1)S(1)}, bf16[288,384]{1,0:T(8,128)(2,1)S(1)}, u32[]{:S(2)}, u32[]{:S(2)}) collective-permute-start(bf16[288,384]{1,0:T(8,128)(2,1)S(1)} %get-tuple-element.208), channel_id=1, source_target_pairs={{0,8},{2,10},{4,12},{6,14},{8,0},{10,2},{12,4},{14,6},{16,24},{18,... | collective-permute-start | bytes 663560 | tf_op jit(solution)/shard_map/ppermute | solution.py:766
  114.7 19.6 %collective-permute-start.17 = (bf16[1040,384]{1,0:T(8,128)(2,1)S(1)}, bf16[1040,384]{1,0:T(8,128)(2,1)S(1)}, u32[]{:S(2)}, u32[]{:S(2)}) collective-permute-start(bf16[1040,384]{1,0:T(8,128)(2,1)S(1)} %back_oth.1), channel_id=1, source_target_pairs={{0,1},{1,0},{2,3},{3,2},{4,5},{5,4},{6,7},{7,6},{8,9},{9,8},{10,11... | collective-permute-start | bytes 2396168 | tf_op jit(solution)/shard_map/ppermute | solution.py:761
  123.1 4.9 %collective-permute-start.14 = (bf16[144,384]{1,0:T(8,128)(2,1)S(1)}, bf16[144,384]{1,0:T(8,128)(2,1)S(1)}, u32[]{:S(2)}, u32[]{:S(2)}) collective-permute-start(bf16[144,384]{1,0:T(8,128)(2,1)S(1)} %get-tuple-element.259), channel_id=1, source_target_pairs={{0,8},{2,10},{4,12},{6,14},{8,0},{10,2},{12,4},{14,6},{16,24},{18,... | collective-permute-start | bytes 331784 | tf_op jit(solution)/shard_map/ppermute | solution.py:766
  124.9 8.0 %copy-start.1 = (bf16[1024,384]{1,0:T(8,128)(2,1)S(1)}, bf16[1024,384]{1,0:T(8,128)(2,1)}, u32[]{:S(2)}) copy-start(bf16[1024,384]{1,0:T(8,128)(2,1)} %refs_0_.1) | copy-start | bytes 2359300
  125.0 4.8 %collective-permute-start.15 = (bf16[144,384]{1,0:T(8,128)(2,1)S(1)}, bf16[144,384]{1,0:T(8,128)(2,1)S(1)}, u32[]{:S(2)}, u32[]{:S(2)}) collective-permute-start(bf16[144,384]{1,0:T(8,128)(2,1)S(1)} %get-tuple-element.261), channel_id=1, source_target_pairs={{0,4},{2,6},{4,0},{6,2},{8,12},{10,14},{12,8},{14,10},{16,20},{18,... | collective-permute-start | bytes 331784 | tf_op jit(solution)/shard_map/ppermute | solution.py:766
  129.8 6.8 %collective-permute-start.16 = (bf16[72,768]{1,0:T(8,128)(2,1)S(1)}, bf16[72,768]{1,0:T(8,128)(2,1)S(1)}, u32[]{:S(2)}, u32[]{:S(2)}) collective-permute-start(bf16[72,768]{1,0:T(8,128)(2,1)S(1)} %pad_maximum_fusion.5), channel_id=1, source_target_pairs={{0,16},{2,18},{4,20},{6,22},{8,24},{10,26},{12,28},{14,30},{16,0},... | collective-permute-start | bytes 331784 | tf_op jit(solution)/shard_map/ppermute | solution.py:766
  131.2 15.3 %collective-permute-start.20 = (bf16[384,768]{1,0:T(8,128)(2,1)S(1)}, bf16[384,768]{1,0:T(8,128)(2,1)S(1)}, u32[]{:S(2)}, u32[]{:S(2)}) collective-permute-start(bf16[384,768]{1,0:T(8,128)(2,1)S(1)} %pad_maximum_fusion), channel_id=1, source_target_pairs={{0,4},{2,6},{4,0},{6,2},{8,12},{10,14},{12,8},{14,10},{16,20},{18,... | collective-permute-start | bytes 1769480 | tf_op jit(solution)/shard_map/ppermute | solution.py:766
  134.3 6.9 %copy-start.5 = (bf16[1024,384]{1,0:T(8,128)(2,1)S(1)}, bf16[1024,384]{1,0:T(8,128)(2,1)}, u32[]{:S(2)}) copy-start(bf16[1024,384]{1,0:T(8,128)(2,1)} %refs_1_.1) | copy-start | bytes 2359300
  136.7 4.0 %collective-permute-start.18 = (bf16[24,768]{1,0:T(8,128)(2,1)S(1)}, bf16[24,768]{1,0:T(8,128)(2,1)S(1)}, u32[]{:S(2)}, u32[]{:S(2)}) collective-permute-start(bf16[24,768]{1,0:T(8,128)(2,1)S(1)} %slice.218), channel_id=1, source_target_pairs={{0,1},{1,0},{2,3},{3,2},{4,5},{5,4},{6,7},{7,6},{8,9},{9,8},{10,11... | collective-permute-start | bytes 110600 | tf_op jit(solution)/shard_map/ppermute | solution.py:761
  140.8 5.7 %collective-permute-start.19 = (bf16[72,768]{1,0:T(8,128)(2,1)S(1)}, bf16[72,768]{1,0:T(8,128)(2,1)S(1)}, u32[]{:S(2)}, u32[]{:S(2)}) collective-permute-start(bf16[72,768]{1,0:T(8,128)(2,1)S(1)} %pad_maximum_fusion.6), channel_id=1, source_target_pairs={{0,16},{2,18},{4,20},{6,22},{8,24},{10,26},{12,28},{14,30},{16,0},... | collective-permute-start | bytes 331784 | tf_op jit(solution)/shard_map/ppermute | solution.py:766
  146.6 7.5 %collective-permute-start.25 = (bf16[768,768]{1,0:T(8,128)(2,1)S(1)}, bf16[768,768]{1,0:T(8,128)(2,1)S(1)}, u32[]{:S(2)}, u32[]{:S(2)}) collective-permute-start(bf16[768,768]{1,0:T(8,128)(2,1)S(1)} %constant_dynamic-update-slice_fusion.first), channel_id=1, source_target_pairs={{0,2},{2,0},{4,6},{6,4},{8,10},{10,8},{12,14},{14,12},{16,18},{18,... | collective-permute-start | bytes 3538952 | tf_op jit(solution)/shard_map/ppermute | solution.py:766
  146.7 5.5 %collective-permute-start.23 = (bf16[144,384]{1,0:T(8,128)(2,1)S(1)}, bf16[144,384]{1,0:T(8,128)(2,1)S(1)}, u32[]{:S(2)}, u32[]{:S(2)}) collective-permute-start(bf16[144,384]{1,0:T(8,128)(2,1)S(1)} %get-tuple-element.262), channel_id=1, source_target_pairs={{0,4},{2,6},{4,0},{6,2},{8,12},{10,14},{12,8},{14,10},{16,20},{18,... | collective-permute-start | bytes 331784 | tf_op jit(solution)/shard_map/ppermute | solution.py:766
  148.2 5.2 %collective-permute-start.21 = (bf16[144,384]{1,0:T(8,128)(2,1)S(1)}, bf16[144,384]{1,0:T(8,128)(2,1)S(1)}, u32[]{:S(2)}, u32[]{:S(2)}) collective-permute-start(bf16[144,384]{1,0:T(8,128)(2,1)S(1)} %get-tuple-element.263), channel_id=1, source_target_pairs={{0,8},{2,10},{4,12},{6,14},{8,0},{10,2},{12,4},{14,6},{16,24},{18,... | collective-permute-start | bytes 331784 | tf_op jit(solution)/shard_map/ppermute | solution.py:766
  152.2 7.1 %collective-permute-start.24 = (bf16[288,384]{1,0:T(8,128)(2,1)S(1)}, bf16[288,384]{1,0:T(8,128)(2,1)S(1)}, u32[]{:S(2)}, u32[]{:S(2)}) collective-permute-start(bf16[288,384]{1,0:T(8,128)(2,1)S(1)} %pad_maximum_fusion.4), channel_id=1, source_target_pairs={{0,8},{2,10},{4,12},{6,14},{8,0},{10,2},{12,4},{14,6},{16,24},{18,... | collective-permute-start | bytes 663560 | tf_op jit(solution)/shard_map/ppermute | solution.py:766
  153.4 6.8 %collective-permute-start.22 = (bf16[288,384]{1,0:T(8,128)(2,1)S(1)}, bf16[288,384]{1,0:T(8,128)(2,1)S(1)}, u32[]{:S(2)}, u32[]{:S(2)}) collective-permute-start(bf16[288,384]{1,0:T(8,128)(2,1)S(1)} %pad_maximum_fusion.3), channel_id=1, source_target_pairs={{0,4},{2,6},{4,0},{6,2},{8,12},{10,14},{12,8},{14,10},{16,20},{18,... | collective-permute-start | bytes 663560 | tf_op jit(solution)/shard_map/ppermute | solution.py:766
  160.3 2.5 %collective-permute-start.26 = (bf16[576,768]{1,0:T(8,128)(2,1)S(1)}, bf16[576,768]{1,0:T(8,128)(2,1)S(1)}, u32[]{:S(2)}, u32[]{:S(2)}) collective-permute-start(bf16[576,768]{1,0:T(8,128)(2,1)S(1)} %maximum_maximum_fusion.first), channel_id=1, source_target_pairs={{0,2},{2,0},{4,6},{6,4},{8,10},{10,8},{12,14},{14,12},{16,18},{18,... | collective-permute-start | bytes 2654216 | tf_op jit(solution)/shard_map/ppermute | solution.py:766
  (7 other events, 8.1 us)

commit v6 on v5

--- a/solution.py
+++ b/solution.py
@@ -9,7 +9,7 @@
 
 EPSILON = 1e-05
 CHUNK = 128
-PROJECT_BLOCK, MIX_BLOCK, GATE_BLOCK, GATE_BACK_BLOCK, BACK_BLOCK, RATES_BLOCK = 256, 256, 512, 256, 128, 512
+PROJECT_BLOCK, MIX_BLOCK, GATE_BLOCK, GATE_BACK_BLOCK, BACK_BLOCK, RATES_BLOCK = 256, 512, 512, 256, 128, 1024
 LANES = 128
 F32 = jnp.float32
 BF16 = jnp.bfloat16

time: 166 us -> 166 us (level)
  transfers between devices with their start and end apart: 27 -> 27, of which waited for: 16 -> 16; matrix products, arithmetic and copies ran while one was open for 6% -> 6% of each run, Pallas kernels for 36% -> 35%
where the time goes in v6:
time: 166 us; the launch traced here: 165 us
  Pallas kernels  73.1 us (44%)
  waiting for transfers between devices  34.3 us (21%)
  starting transfers between devices  31 us (19%)
  local copies, waits for them, and re-layouts  12.3 us (7%)
  other arithmetic  6.89 us (4%)
  matrix products  5.43 us (3%)
  between operations  1.95 us (1%)
    pallas_call x8, Pallas kernels, call(): pl.pallas_call(looped, out_shape=[pltpu.VMEM(o.shape, o.dtype) for o in o...  53.2 us
    ppermute x20, waiting for transfers between devices, swap_dp(): return lax.ppermute(x, 'dp', [(i, i ^ 1 << bit) for i in range(size)])  27.5 us
    ppermute x20, starting transfers between devices, swap_dp(): return lax.ppermute(x, 'dp', [(i, i ^ 1 << bit) for i in range(size)])  21.4 us
    pallas_call x8, Pallas kernels, whole(): pl.pallas_call(kernel, out_shape=[pltpu.VMEM(o.shape, o.dtype) if in_vmem...  18.3 us
    ppermute x7, starting transfers between devices, swap_mp(): return lax.ppermute(x, 'mp', [(0, 1), (1, 0)])  9.57 us
    unnamed x27, local copies, waits for them, and re-layouts  8.56 us
    ppermute x7, waiting for transfers between devices, swap_mp(): return lax.ppermute(x, 'mp', [(0, 1), (1, 0)])  6.81 us
    dot_general x5, matrix products, mm_tn(): lax.dot_general(a, b, (((0,), (0,)), ((), ())), preferred_element_type=F32)  5.43 us
  transfers between devices with their start and end apart: 27, of which 16 were waited for; matrix products, arithmetic and copies ran while one was open for 6% of the time, Pallas kernels for 35%

profile of v6, /device:TPU:0, one launch (start us, length us, event | category | flops | bytes accessed | tf_op | source)
XLA Modules:
  0.0 165.0 jit_solution(17271574385679442395)
XLA Ops:
  1.3 3.0 %collective-permute-start.1 = (bf16[1,384]{1,0:T(2,128)(2,1)S(1)}, bf16[1,384]{1,0:T(2,128)(2,1)S(1)}, u32[]{:S(2)}, u32[]{:S(2)}) collective-permute-start(bf16[1,384]{1,0:T(2,128)(2,1)S(1)} %concatenate.72), channel_id=1, source_target_pairs={{0,1},{1,0},{2,3},{3,2},{4,5},{5,4},{6,7},{7,6},{8,9},{9,8},{10,11... | collective-permute-start | bytes 2312 | tf_op jit(solution)/shard_map/ppermute | solution.py:761
  19.2 4.3 %collective-permute-done.refs_1_ = bf16[1024,384]{1,0:T(8,128)(2,1)S(1)} collective-permute-done((bf16[1024,384]{1,0:T(8,128)(2,1)}, bf16[1024,384]{1,0:T(8,128)(2,1)S(1)}, u32[]{:S(2)}, u32[]{:S(2)}) %collective-permute-start) | collective-permute-done | bytes 786464 | tf_op jit(solution)/shard_map/ppermute | solution.py:761
  23.8 11.2 %project.1 = (bf16[1024,768]{1,0:T(8,128)(2,1)S(1)}, f32[1024,768]{1,0:T(8,128)S(1)}, bf16[1024,1024]{1,0:T(8,128)(2,1)S(1)}, bf16[1024,1024]{1,0:T(8,128)(2,1)S...) custom-call(s32[3]{0:T(128)S(1)} %pad_add_fusion.scalars, ...), custom_call_target="tpu_custom_call" | custom-call | flops 6000000000 | bytes 36000000 | tf_op jit(solution)/shard_map/project/pallas_call | solution.py:729
  35.0 6.6 %mix.1 = (f32[1024,768]{1,0:T(8,128)S(1)}, bf16[8,64,768]{2,1,0:T(8,128)(2,1)S(1)}) custom-call(s32[3]{0:T(128)S(1)} %pad_add_fusion.scalars, f32[1024,768]{1,0:T(8,128)S(1)} %get-tuple-element.137.refs_0_.refs_3_.refs_1_, bf16[1024,256]{1,0:T(8,128)(2,1)S(1)} %get-tuple-element.138.refs_1_.refs_8_.refs_2_, ...), custom_call_target="tpu_custom_call" | custom-call | flops 3500000000 | bytes 21000000 | tf_op jit(solution)/shard_map/mix/pallas_call | solution.py:729
  41.6 3.0 %gate.1 = (f32[1024,768]{1,0:T(8,128)S(1)}, bf16[1024,768]{1,0:T(8,128)(2,1)S(1)}, f32[8,1024]{1,0:T(8,128)S(1)}) custom-call(s32[3]{0:T(128)S(1)} %pad_add_fusion.scalars, f32[1024,768]{1,0:T(8,128)S(1)} %get-tuple-element.143.refs_0_.refs_2_, f32[1024,768]{1,0:T(8,128)S(1)} %get-tuple-element.144.refs_1_, ...), custom_call_target="tpu_custom_call" | custom-call | flops 1500000000 | bytes 9000000 | tf_op jit(solution)/shard_map/gate/pallas_call | solution.py:729
  44.6 1.7 %collective-permute-start.3 = (f32[8,1024]{1,0:T(8,128)S(1)}, f32[8,1024]{1,0:T(8,128)S(1)}, u32[]{:S(2)}, u32[]{:S(2)}) collective-permute-start(f32[8,1024]{1,0:T(8,128)S(1)} %get-tuple-element.148), channel_id=1, source_target_pairs={{0,1},{1,0},{2,3},{3,2},{4,5},{5,4},{6,7},{7,6},{8,9},{9,8},{10,11... | collective-permute-start | bytes 98312 | tf_op jit(solution)/shard_map/ppermute | solution.py:761
  46.4 2.4 %branch_oth.1 = bf16[1024,384]{1,0:T(8,128)(2,1)} custom-call(s32[3]{0:T(128)S(1)} %pad_add_fusion.scalars, bf16[1024,768]{1,0:T(8,128)(2,1)S(1)} %get-tuple-element.159.gz, bf16[768,768]{1,0:T(8,128)(2,1)S(1)} %get-tuple-element.147.refs_4_.po), custom_call_target="tpu_custom_call" | custom-call | flops 1500000000 | bytes 9000000 | tf_op jit(solution)/shard_map/branch_oth/pallas_call | solution.py:746
  48.8 7.8 %gate_back.1 = (bf16[1024,768]{1,0:T(8,128)(2,1)S(1)}, bf16[1024,768]{1,0:T(8,128)(2,1)S(1)}, bf16[1024,768]{1,0:T(8,128)(2,1)S(1)}, f32[1024,128]{1,0:T(8,128)S...) custom-call(s32[3]{0:T(128)S(1)} %pad_add_fusion.scalars, ...), custom_call_target="tpu_custom_call" | custom-call | flops 4000000000 | bytes 24000000 | tf_op jit(solution)/shard_map/gate_back/pallas_call | solution.py:729
  67.8 11.1 %mix_back.3 = (bf16[1024,1024]{1,0:T(8,128)(2,1)S(1)}, f32[1024,512]{1,0:T(8,128)S(1)}, f32[8,1024]{1,0:T(8,128)S(1)}, f32[8,1024]{1,0:T(8,128)S(1)}, f32[8,1024]{1,0:T(8,128)S(1)}, /*index=5*/f32[64,768]{1,0:T(8,128)S(1)}) custom-call(s32[3]{0:T(128)S(1)} %pad_add_fusion.scalars, ...), custom_call_target="tpu_custom_call", output_to_operand_aliasing={{0}: (21, {}), {1}: (22, {}), {2}: (23, {})} | custom-call | flops 6000000000 | bytes 36000000 | tf_op jit(solution)/shard_map/mix_back/pallas_call | solution.py:729
  79.8 1.6 collective-permute-start.6
  81.5 5.8 %mix_back.4 = (bf16[1024,1024]{1,0:T(8,128)(2,1)S(1)}, f32[1024,512]{1,0:T(8,128)S(1)}, f32[8,1024]{1,0:T(8,128)S(1)}, f32[8,1024]{1,0:T(8,128)S(1)}, f32[8,1024]{1,0:T(8,128)S(1)}, /*index=5*/f32[64,768]{1,0:T(8,128)S(1)}) custom-call(s32[3]{0:T(128)S(1)} %pad_add_fusion.scalars, ...), custom_call_target="tpu_custom_call", output_to_operand_aliasing={{0}: (21, {}), {1}: (22, {}), {2}: (23, {})} | custom-call | flops 3000000000 | bytes 18000000 | tf_op jit(solution)/shard_map/mix_back/pallas_call | solution.py:729
  88.1 2.6 %collective-permute-start.8 = (bf16[96,768]{1,0:T(8,128)(2,1)S(1)}, bf16[96,768]{1,0:T(8,128)(2,1)S(1)}, u32[]{:S(2)}, u32[]{:S(2)}) collective-permute-start(bf16[96,768]{1,0:T(8,128)(2,1)S(1)} %add_convert_fusion.10), channel_id=1, source_target_pairs={{0,16},{2,18},{4,20},{6,22},{8,24},{10,26},{12,28},{14,30},{16,0},... | collective-permute-start | bytes 442376 | tf_op jit(solution)/shard_map/ppermute | solution.py:766
  90.8 6.3 %mix_back.5 = (bf16[1024,1024]{1,0:T(8,128)(2,1)S(1)}, f32[1024,512]{1,0:T(8,128)S(1)}, f32[8,1024]{1,0:T(8,128)S(1)}, f32[8,1024]{1,0:T(8,128)S(1)}, f32[8,1024]{1,0:T(8,128)}, /*index=5*/f32[64,768]{1,0:T(8,128)}) custom-call(s32[3]{0:T(128)S(1)} %pad_add_fusion.scalars, ...), custom_call_target="tpu_custom_call", output_to_operand_aliasing={{0}: (21, {}), {1}: (22, {}), {2}: (23, {})} | custom-call | flops 3000000000 | bytes 18000000 | tf_op jit(solution)/shard_map/mix_back/pallas_call | solution.py:729
  101.1 2.8 %back_oth.1 = bf16[1040,384]{1,0:T(8,128)(2,1)S(1)} custom-call(s32[3]{0:T(128)S(1)} %pad_add_fusion.scalars, bf16[1024,768]{1,0:T(8,128)(2,1)S(1)} %get-tuple-element.156.dgp, bf16[1024,1024]{1,0:T(8,128)(2,1)S(1)} %get-tuple-element.209.rest, bf16[1024,128]{1,0:T(8,128)(2,1)S(1)} %get-tuple-element.196.dz, f32[8,1024]{1,0:T(8,128)S(1)} %get-tuple-element.205.rd, ...), custom_call_target="tpu_custom_call" | custom-call | tf_op jit(solution)/shard_map/back_oth/pallas_call | solution.py:746
  105.0 1.6 pack_late.1
  107.4 2.5 %collective-permute-start.13 = (bf16[192,768]{1,0:T(8,128)(2,1)S(1)}, bf16[192,768]{1,0:T(8,128)(2,1)S(1)}, u32[]{:S(2)}, u32[]{:S(2)}) collective-permute-start(bf16[192,768]{1,0:T(8,128)(2,1)S(1)} %pad_maximum_fusion.1), channel_id=1, source_target_pairs={{0,8},{2,10},{4,12},{6,14},{8,0},{10,2},{12,4},{14,6},{16,24},{18,... | collective-permute-start | bytes 884744 | tf_op jit(solution)/shard_map/ppermute | solution.py:766
  110.2 1.6 collective-permute-start.11
  111.7 2.3 %collective-permute-start.12 = (bf16[288,384]{1,0:T(8,128)(2,1)S(1)}, bf16[288,384]{1,0:T(8,128)(2,1)S(1)}, u32[]{:S(2)}, u32[]{:S(2)}) collective-permute-start(bf16[288,384]{1,0:T(8,128)(2,1)S(1)} %get-tuple-element.208), channel_id=1, source_target_pairs={{0,8},{2,10},{4,12},{6,14},{8,0},{10,2},{12,4},{14,6},{16,24},{18,... | collective-permute-start | bytes 663560 | tf_op jit(solution)/shard_map/ppermute | solution.py:766
  115.5 2.8 %back_own.1 = f32[1024,384]{1,0:T(8,128)S(1)} custom-call(s32[3]{0:T(128)S(1)} %pad_add_fusion.scalars, bf16[1024,768]{1,0:T(8,128)(2,1)S(1)} %get-tuple-element.156.dgp, bf16[1024,1024]{1,0:T(8,128)(2,1)S(1)} %get-tuple-element.209.rest, bf16[1024,128]{1,0:T(8,128)(2,1)S(1)} %get-tuple-element.196.dz, f32[8,1024]{1,0:T(8,128)S(1)} %get-tuple-element.205.rd, ...), custom_call_target="tpu_custom_call" | custom-call | tf_op jit(solution)/shard_map/back_own/pallas_call | solution.py:746
  118.4 4.0 %collective-permute-done.12 = bf16[288,384]{1,0:T(8,128)(2,1)S(1)} collective-permute-done((bf16[288,384]{1,0:T(8,128)(2,1)S(1)}, bf16[288,384]{1,0:T(8,128)(2,1)S(1)}, u32[]{:S(2)}, u32[]{:S(2)}) %collective-permute-start.12) | collective-permute-done | bytes 221216 | tf_op jit(solution)/shard_map/ppermute | solution.py:766
  122.4 1.8 %collective-permute-start.14 = (bf16[144,384]{1,0:T(8,128)(2,1)S(1)}, bf16[144,384]{1,0:T(8,128)(2,1)S(1)}, u32[]{:S(2)}, u32[]{:S(2)}) collective-permute-start(bf16[144,384]{1,0:T(8,128)(2,1)S(1)} %get-tuple-element.259), channel_id=1, source_target_pairs={{0,8},{2,10},{4,12},{6,14},{8,0},{10,2},{12,4},{14,6},{16,24},{18,... | collective-permute-start | bytes 331784 | tf_op jit(solution)/shard_map/ppermute | solution.py:766
  127.3 1.7 %collective-permute-done.15 = bf16[144,384]{1,0:T(8,128)(2,1)S(1)} collective-permute-done((bf16[144,384]{1,0:T(8,128)(2,1)S(1)}, bf16[144,384]{1,0:T(8,128)(2,1)S(1)}, u32[]{:S(2)}, u32[]{:S(2)}) %collective-permute-start.15) | collective-permute-done | bytes 110624 | tf_op jit(solution)/shard_map/ppermute | solution.py:766
  133.4 2.5 %collective-permute-done.16 = bf16[72,768]{1,0:T(8,128)(2,1)S(1)} collective-permute-done((bf16[72,768]{1,0:T(8,128)(2,1)S(1)}, bf16[72,768]{1,0:T(8,128)(2,1)S(1)}, u32[]{:S(2)}, u32[]{:S(2)}) %collective-permute-start.16) | collective-permute-done | bytes 110624 | tf_op jit(solution)/shard_map/ppermute | solution.py:766
  137.5 2.5 %collective-permute-done.18 = bf16[24,768]{1,0:T(8,128)(2,1)S(1)} collective-permute-done((bf16[24,768]{1,0:T(8,128)(2,1)S(1)}, bf16[24,768]{1,0:T(8,128)(2,1)S(1)}, u32[]{:S(2)}, u32[]{:S(2)}) %collective-permute-start.18) | collective-permute-done | bytes 36896 | tf_op jit(solution)/shard_map/ppermute | solution.py:761
  140.3 1.7 %fusion.2 = f32[1024,384]{1,0:T(8,128)} fusion(bf16[1024,384]{1,0:T(8,128)(2,1)S(1)} %copy-done.1, f32[1024,384]{1,0:T(8,128)S(1)} %back_own.1, bf16[1024,384]{1,0:T(8,128)(2,1)S(1)} %copy-done.5, f32[1024]{0:T(1024)S(1)} %get-tuple-element.246, f32[384]{0:T(512)S(1)} %convert_element_type.314, bf16[1040,384]{1,0:T(8,128)(2,1)S(1)} %collective-permute-done.17, ...), kind=kLoop, calls=%fused_computation.5 | loop fusion | flops 3538944 | bytes 5514752 | tf_op jit(solution)/shard_map/sub | solution.py:1184
  142.0 3.8 %collective-permute-done.19 = bf16[72,768]{1,0:T(8,128)(2,1)S(1)} collective-permute-done((bf16[72,768]{1,0:T(8,128)(2,1)S(1)}, bf16[72,768]{1,0:T(8,128)(2,1)S(1)}, u32[]{:S(2)}, u32[]{:S(2)}) %collective-permute-start.19) | collective-permute-done | bytes 110624 | tf_op jit(solution)/shard_map/ppermute | solution.py:766
  146.0 1.6 collective-permute-start.23
  147.5 4.0 %collective-permute-done.23 = bf16[144,384]{1,0:T(8,128)(2,1)S(1)} collective-permute-done((bf16[144,384]{1,0:T(8,128)(2,1)S(1)}, bf16[144,384]{1,0:T(8,128)(2,1)S(1)}, u32[]{:S(2)}, u32[]{:S(2)}) %collective-permute-start.23) | collective-permute-done | bytes 110624 | tf_op jit(solution)/shard_map/ppermute | solution.py:766
  153.3 3.0 %unpack_early.1 = (f32[768,768]{1,0:T(8,128)}, f32[768,768]{1,0:T(8,128)}) custom-call(s32[3]{0:T(128)S(1)} %pad_add_fusion.scalars, bf16[768,768]{1,0:T(8,128)(2,1)S(1)} %constant_dynamic-update-slice_fusion.first, bf16[768,768]{1,0:T(8,128)(2,1)S(1)} %collective-permute-done.25.second), custom_call_target="tpu_custom_call" | custom-call | tf_op jit(solution)/shard_map/unpack_early/pallas_call | solution.py:746
  156.4 2.3 %collective-permute-done.24 = bf16[288,384]{1,0:T(8,128)(2,1)S(1)} collective-permute-done((bf16[288,384]{1,0:T(8,128)(2,1)S(1)}, bf16[288,384]{1,0:T(8,128)(2,1)S(1)}, u32[]{:S(2)}, u32[]{:S(2)}) %collective-permute-start.24) | collective-permute-done | bytes 221216 | tf_op jit(solution)/shard_map/ppermute | solution.py:766
  159.7 2.4 %collective-permute-done.26.second = bf16[576,768]{1,0:T(8,128)(2,1)S(1)} collective-permute-done((bf16[576,768]{1,0:T(8,128)(2,1)S(1)}, bf16[576,768]{1,0:T(8,128)(2,1)S(1)}, u32[]{:S(2)}, u32[]{:S(2)}) %collective-permute-start.26) | collective-permute-done | bytes 884768 | tf_op jit(solution)/shard_map/ppermute | solution.py:766
  162.1 2.7 %unpack_late.1 = (f32[768,768]{1,0:T(8,128)}, f32[768,256]{1,0:T(8,128)}, f32[12,2,768]{2,1,0:T(2,128)}, f32[4,768]{1,0:T(4,128)}, f32[768]{0:T(1024)}, /*index=...) custom-call(s32[3]{0:T(128)S(1)} %pad_add_fusion.scalars, ...), custom_call_target="tpu_custom_call" | custom-call | tf_op jit(solution)/shard_map/unpack_late/pallas_call | solution.py:746
  (127 shorter events, 48.1 us)
Async XLA Ops:
  1.3 17.8 %collective-permute-start.1 = (bf16[1,384]{1,0:T(2,128)(2,1)S(1)}, bf16[1,384]{1,0:T(2,128)(2,1)S(1)}, u32[]{:S(2)}, u32[]{:S(2)}) collective-permute-start(bf16[1,384]{1,0:T(2,128)(2,1)S(1)} %concatenate.72), channel_id=1, source_target_pairs={{0,1},{1,0},{2,3},{3,2},{4,5},{5,4},{6,7},{7,6},{8,9},{9,8},{10,11... | collective-permute-start | bytes 2312 | tf_op jit(solution)/shard_map/ppermute | solution.py:761
  4.3 19.2 %collective-permute-start = (bf16[1024,384]{1,0:T(8,128)(2,1)}, bf16[1024,384]{1,0:T(8,128)(2,1)S(1)}, u32[]{:S(2)}, u32[]{:S(2)}) collective-permute-start(bf16[1024,384]{1,0:T(8,128)(2,1)} %refs_0_.1), channel_id=1, source_target_pairs={{0,1},{1,0},{2,3},{3,2},{4,5},{5,4},{6,7},{7,6},{8,9},{9,8},{10,11... | collective-permute-start | bytes 2359304 | tf_op jit(solution)/shard_map/ppermute | solution.py:761
  19.1 15.9 %copy-start.9 = (bf16[384,768]{1,0:T(8,128)(2,1)}, bf16[384,768]{1,0:T(8,128)(2,1)S(1)}, u32[]{:S(2)}) copy-start(bf16[384,768]{1,0:T(8,128)(2,1)S(1)} %get-tuple-element.197.w_state_t) | copy-start | bytes 1769476
  23.5 18.1 %collective-permute-start.2 = (bf16[1024,384]{1,0:T(8,128)(2,1)S(1)}, bf16[1024,384]{1,0:T(8,128)(2,1)S(1)}, u32[]{:S(2)}, u32[]{:S(2)}) collective-permute-start(bf16[1024,384]{1,0:T(8,128)(2,1)S(1)} %copy-done.4), channel_id=1, source_target_pairs={{0,1},{1,0},{2,3},{3,2},{4,5},{5,4},{6,7},{7,6},{8,9},{9,8},{10,11... | collective-permute-start | bytes 2359304 | tf_op jit(solution)/shard_map/ppermute | solution.py:761
  44.6 4.1 %collective-permute-start.3 = (f32[8,1024]{1,0:T(8,128)S(1)}, f32[8,1024]{1,0:T(8,128)S(1)}, u32[]{:S(2)}, u32[]{:S(2)}) collective-permute-start(f32[8,1024]{1,0:T(8,128)S(1)} %get-tuple-element.148), channel_id=1, source_target_pairs={{0,1},{1,0},{2,3},{3,2},{4,5},{5,4},{6,7},{7,6},{8,9},{9,8},{10,11... | collective-permute-start | bytes 98312 | tf_op jit(solution)/shard_map/ppermute | solution.py:761
  58.1 1.5 copy-start.3
  61.0 2.9 %collective-permute-start.4 = (bf16[768,768]{1,0:T(8,128)(2,1)S(1)}, bf16[768,768]{1,0:T(8,128)(2,1)S(1)}, u32[]{:S(2)}, u32[]{:S(2)}) collective-permute-start(bf16[768,768]{1,0:T(8,128)(2,1)S(1)} %get-tuple-element.158), channel_id=1, source_target_pairs={{0,2},{2,0},{4,6},{6,4},{8,10},{10,8},{12,14},{14,12},{16,18},{18,... | collective-permute-start | bytes 3538952 | tf_op jit(solution)/shard_map/ppermute | solution.py:766
  64.2 15.4 %collective-permute-start.5 = (bf16[384,768]{1,0:T(8,128)(2,1)S(1)}, bf16[384,768]{1,0:T(8,128)(2,1)S(1)}, u32[]{:S(2)}, u32[]{:S(2)}) collective-permute-start(bf16[384,768]{1,0:T(8,128)(2,1)S(1)} %get-tuple-element.249), channel_id=1, source_target_pairs={{0,4},{2,6},{4,0},{6,2},{8,12},{10,14},{12,8},{14,10},{16,20},{18,... | collective-permute-start | bytes 1769480 | tf_op jit(solution)/shard_map/ppermute | solution.py:766
  65.8 22.3 %collective-permute-start.7 = (bf16[1024,384]{1,0:T(8,128)(2,1)}, bf16[1024,384]{1,0:T(8,128)(2,1)S(1)}, u32[]{:S(2)}, u32[]{:S(2)}) collective-permute-start(bf16[1024,384]{1,0:T(8,128)(2,1)} %branch_oth.1), channel_id=1, source_target_pairs={{0,1},{1,0},{2,3},{3,2},{4,5},{5,4},{6,7},{7,6},{8,9},{9,8},{10,11... | collective-permute-start | bytes 2359304 | tf_op jit(solution)/shard_map/ppermute | solution.py:761
  79.8 8.3 %collective-permute-start.6 = (bf16[192,768]{1,0:T(8,128)(2,1)S(1)}, bf16[192,768]{1,0:T(8,128)(2,1)S(1)}, u32[]{:S(2)}, u32[]{:S(2)}) collective-permute-start(bf16[192,768]{1,0:T(8,128)(2,1)S(1)} %get-tuple-element.255), channel_id=1, source_target_pairs={{0,8},{2,10},{4,12},{6,14},{8,0},{10,2},{12,4},{14,6},{16,24},{18,... | collective-permute-start | bytes 884744 | tf_op jit(solution)/shard_map/ppermute | solution.py:766
  88.1 9.0 %collective-permute-start.8 = (bf16[96,768]{1,0:T(8,128)(2,1)S(1)}, bf16[96,768]{1,0:T(8,128)(2,1)S(1)}, u32[]{:S(2)}, u32[]{:S(2)}) collective-permute-start(bf16[96,768]{1,0:T(8,128)(2,1)S(1)} %add_convert_fusion.10), channel_id=1, source_target_pairs={{0,16},{2,18},{4,20},{6,22},{8,24},{10,26},{12,28},{14,30},{16,0},... | collective-permute-start | bytes 442376 | tf_op jit(solution)/shard_map/ppermute | solution.py:766
  99.3 8.0 %collective-permute-start.9 = (bf16[96,768]{1,0:T(8,128)(2,1)S(1)}, bf16[96,768]{1,0:T(8,128)(2,1)S(1)}, u32[]{:S(2)}, u32[]{:S(2)}) collective-permute-start(bf16[96,768]{1,0:T(8,128)(2,1)S(1)} %add_convert_fusion.8), channel_id=1, source_target_pairs={{0,16},{2,18},{4,20},{6,22},{8,24},{10,26},{12,28},{14,30},{16,0},... | collective-permute-start | bytes 442376 | tf_op jit(solution)/shard_map/ppermute | solution.py:766
  105.0 2.3 %copy-start.11 = (bf16[384]{0:T(512)(128)(2,1)S(1)}, bf16[384]{0:T(512)(128)(2,1)}, u32[]{:S(2)}) copy-start(bf16[384]{0:T(512)(128)(2,1)} %param.18) | copy-start | bytes 2308
  107.3 2.6 %collective-permute-start.10 = (bf16[576,768]{1,0:T(8,128)(2,1)S(1)}, bf16[576,768]{1,0:T(8,128)(2,1)S(1)}, u32[]{:S(2)}, u32[]{:S(2)}) collective-permute-start(bf16[576,768]{1,0:T(8,128)(2,1)S(1)} %get-tuple-element.206), channel_id=1, source_target_pairs={{0,2},{2,0},{4,6},{6,4},{8,10},{10,8},{12,14},{14,12},{16,18},{18,... | collective-permute-start | bytes 2654216 | tf_op jit(solution)/shard_map/ppermute | solution.py:766
  107.4 10.9 %collective-permute-start.13 = (bf16[192,768]{1,0:T(8,128)(2,1)S(1)}, bf16[192,768]{1,0:T(8,128)(2,1)S(1)}, u32[]{:S(2)}, u32[]{:S(2)}) collective-permute-start(bf16[192,768]{1,0:T(8,128)(2,1)S(1)} %pad_maximum_fusion.1), channel_id=1, source_target_pairs={{0,8},{2,10},{4,12},{6,14},{8,0},{10,2},{12,4},{14,6},{16,24},{18,... | collective-permute-start | bytes 884744 | tf_op jit(solution)/shard_map/ppermute | solution.py:766
  110.2 8.2 %collective-permute-start.11 = (bf16[288,384]{1,0:T(8,128)(2,1)S(1)}, bf16[288,384]{1,0:T(8,128)(2,1)S(1)}, u32[]{:S(2)}, u32[]{:S(2)}) collective-permute-start(bf16[288,384]{1,0:T(8,128)(2,1)S(1)} %get-tuple-element.207), channel_id=1, source_target_pairs={{0,4},{2,6},{4,0},{6,2},{8,12},{10,14},{12,8},{14,10},{16,20},{18,... | collective-permute-start | bytes 663560 | tf_op jit(solution)/shard_map/ppermute | solution.py:766
  111.7 10.6 %collective-permute-start.12 = (bf16[288,384]{1,0:T(8,128)(2,1)S(1)}, bf16[288,384]{1,0:T(8,128)(2,1)S(1)}, u32[]{:S(2)}, u32[]{:S(2)}) collective-permute-start(bf16[288,384]{1,0:T(8,128)(2,1)S(1)} %get-tuple-element.208), channel_id=1, source_target_pairs={{0,8},{2,10},{4,12},{6,14},{8,0},{10,2},{12,4},{14,6},{16,24},{18,... | collective-permute-start | bytes 663560 | tf_op jit(solution)/shard_map/ppermute | solution.py:766
  114.0 19.4 %collective-permute-start.17 = (bf16[1040,384]{1,0:T(8,128)(2,1)S(1)}, bf16[1040,384]{1,0:T(8,128)(2,1)S(1)}, u32[]{:S(2)}, u32[]{:S(2)}) collective-permute-start(bf16[1040,384]{1,0:T(8,128)(2,1)S(1)} %back_oth.1), channel_id=1, source_target_pairs={{0,1},{1,0},{2,3},{3,2},{4,5},{5,4},{6,7},{7,6},{8,9},{9,8},{10,11... | collective-permute-start | bytes 2396168 | tf_op jit(solution)/shard_map/ppermute | solution.py:761
  122.4 4.9 %collective-permute-start.14 = (bf16[144,384]{1,0:T(8,128)(2,1)S(1)}, bf16[144,384]{1,0:T(8,128)(2,1)S(1)}, u32[]{:S(2)}, u32[]{:S(2)}) collective-permute-start(bf16[144,384]{1,0:T(8,128)(2,1)S(1)} %get-tuple-element.259), channel_id=1, source_target_pairs={{0,8},{2,10},{4,12},{6,14},{8,0},{10,2},{12,4},{14,6},{16,24},{18,... | collective-permute-start | bytes 331784 | tf_op jit(solution)/shard_map/ppermute | solution.py:766
  124.2 7.8 %copy-start.1 = (bf16[1024,384]{1,0:T(8,128)(2,1)S(1)}, bf16[1024,384]{1,0:T(8,128)(2,1)}, u32[]{:S(2)}) copy-start(bf16[1024,384]{1,0:T(8,128)(2,1)} %refs_0_.1) | copy-start | bytes 2359300
  124.2 4.8 %collective-permute-start.15 = (bf16[144,384]{1,0:T(8,128)(2,1)S(1)}, bf16[144,384]{1,0:T(8,128)(2,1)S(1)}, u32[]{:S(2)}, u32[]{:S(2)}) collective-permute-start(bf16[144,384]{1,0:T(8,128)(2,1)S(1)} %get-tuple-element.261), channel_id=1, source_target_pairs={{0,4},{2,6},{4,0},{6,2},{8,12},{10,14},{12,8},{14,10},{16,20},{18,... | collective-permute-start | bytes 331784 | tf_op jit(solution)/shard_map/ppermute | solution.py:766
  129.1 6.8 %collective-permute-start.16 = (bf16[72,768]{1,0:T(8,128)(2,1)S(1)}, bf16[72,768]{1,0:T(8,128)(2,1)S(1)}, u32[]{:S(2)}, u32[]{:S(2)}) collective-permute-start(bf16[72,768]{1,0:T(8,128)(2,1)S(1)} %pad_maximum_fusion.5), channel_id=1, source_target_pairs={{0,16},{2,18},{4,20},{6,22},{8,24},{10,26},{12,28},{14,30},{16,0},... | collective-permute-start | bytes 331784 | tf_op jit(solution)/shard_map/ppermute | solution.py:766
  130.3 15.5 %collective-permute-start.20 = (bf16[384,768]{1,0:T(8,128)(2,1)S(1)}, bf16[384,768]{1,0:T(8,128)(2,1)S(1)}, u32[]{:S(2)}, u32[]{:S(2)}) collective-permute-start(bf16[384,768]{1,0:T(8,128)(2,1)S(1)} %pad_maximum_fusion), channel_id=1, source_target_pairs={{0,4},{2,6},{4,0},{6,2},{8,12},{10,14},{12,8},{14,10},{16,20},{18,... | collective-permute-start | bytes 1769480 | tf_op jit(solution)/shard_map/ppermute | solution.py:766
  133.4 6.9 %copy-start.5 = (bf16[1024,384]{1,0:T(8,128)(2,1)S(1)}, bf16[1024,384]{1,0:T(8,128)(2,1)}, u32[]{:S(2)}) copy-start(bf16[1024,384]{1,0:T(8,128)(2,1)} %refs_1_.1) | copy-start | bytes 2359300
  136.0 4.0 %collective-permute-start.18 = (bf16[24,768]{1,0:T(8,128)(2,1)S(1)}, bf16[24,768]{1,0:T(8,128)(2,1)S(1)}, u32[]{:S(2)}, u32[]{:S(2)}) collective-permute-start(bf16[24,768]{1,0:T(8,128)(2,1)S(1)} %slice.218), channel_id=1, source_target_pairs={{0,1},{1,0},{2,3},{3,2},{4,5},{5,4},{6,7},{7,6},{8,9},{9,8},{10,11... | collective-permute-start | bytes 110600 | tf_op jit(solution)/shard_map/ppermute | solution.py:761
  140.1 5.7 %collective-permute-start.19 = (bf16[72,768]{1,0:T(8,128)(2,1)S(1)}, bf16[72,768]{1,0:T(8,128)(2,1)S(1)}, u32[]{:S(2)}, u32[]{:S(2)}) collective-permute-start(bf16[72,768]{1,0:T(8,128)(2,1)S(1)} %pad_maximum_fusion.6), channel_id=1, source_target_pairs={{0,16},{2,18},{4,20},{6,22},{8,24},{10,26},{12,28},{14,30},{16,0},... | collective-permute-start | bytes 331784 | tf_op jit(solution)/shard_map/ppermute | solution.py:766
  145.8 7.5 %collective-permute-start.25 = (bf16[768,768]{1,0:T(8,128)(2,1)S(1)}, bf16[768,768]{1,0:T(8,128)(2,1)S(1)}, u32[]{:S(2)}, u32[]{:S(2)}) collective-permute-start(bf16[768,768]{1,0:T(8,128)(2,1)S(1)} %constant_dynamic-update-slice_fusion.first), channel_id=1, source_target_pairs={{0,2},{2,0},{4,6},{6,4},{8,10},{10,8},{12,14},{14,12},{16,18},{18,... | collective-permute-start | bytes 3538952 | tf_op jit(solution)/shard_map/ppermute | solution.py:766
  146.0 5.5 %collective-permute-start.23 = (bf16[144,384]{1,0:T(8,128)(2,1)S(1)}, bf16[144,384]{1,0:T(8,128)(2,1)S(1)}, u32[]{:S(2)}, u32[]{:S(2)}) collective-permute-start(bf16[144,384]{1,0:T(8,128)(2,1)S(1)} %get-tuple-element.262), channel_id=1, source_target_pairs={{0,4},{2,6},{4,0},{6,2},{8,12},{10,14},{12,8},{14,10},{16,20},{18,... | collective-permute-start | bytes 331784 | tf_op jit(solution)/shard_map/ppermute | solution.py:766
  147.5 5.2 %collective-permute-start.21 = (bf16[144,384]{1,0:T(8,128)(2,1)S(1)}, bf16[144,384]{1,0:T(8,128)(2,1)S(1)}, u32[]{:S(2)}, u32[]{:S(2)}) collective-permute-start(bf16[144,384]{1,0:T(8,128)(2,1)S(1)} %get-tuple-element.263), channel_id=1, source_target_pairs={{0,8},{2,10},{4,12},{6,14},{8,0},{10,2},{12,4},{14,6},{16,24},{18,... | collective-permute-start | bytes 331784 | tf_op jit(solution)/shard_map/ppermute | solution.py:766
  151.5 7.1 %collective-permute-start.24 = (bf16[288,384]{1,0:T(8,128)(2,1)S(1)}, bf16[288,384]{1,0:T(8,128)(2,1)S(1)}, u32[]{:S(2)}, u32[]{:S(2)}) collective-permute-start(bf16[288,384]{1,0:T(8,128)(2,1)S(1)} %pad_maximum_fusion.4), channel_id=1, source_target_pairs={{0,8},{2,10},{4,12},{6,14},{8,0},{10,2},{12,4},{14,6},{16,24},{18,... | collective-permute-start | bytes 663560 | tf_op jit(solution)/shard_map/ppermute | solution.py:766
  152.7 6.8 %collective-permute-start.22 = (bf16[288,384]{1,0:T(8,128)(2,1)S(1)}, bf16[288,384]{1,0:T(8,128)(2,1)S(1)}, u32[]{:S(2)}, u32[]{:S(2)}) collective-permute-start(bf16[288,384]{1,0:T(8,128)(2,1)S(1)} %pad_maximum_fusion.3), channel_id=1, source_target_pairs={{0,4},{2,6},{4,0},{6,2},{8,12},{10,14},{12,8},{14,10},{16,20},{18,... | collective-permute-start | bytes 663560 | tf_op jit(solution)/shard_map/ppermute | solution.py:766
  159.6 2.5 %collective-permute-start.26 = (bf16[576,768]{1,0:T(8,128)(2,1)S(1)}, bf16[576,768]{1,0:T(8,128)(2,1)S(1)}, u32[]{:S(2)}, u32[]{:S(2)}) collective-permute-start(bf16[576,768]{1,0:T(8,128)(2,1)S(1)} %maximum_maximum_fusion.first), channel_id=1, source_target_pairs={{0,2},{2,0},{4,6},{6,4},{8,10},{10,8},{12,14},{14,12},{16,18},{18,... | collective-permute-start | bytes 2654216 | tf_op jit(solution)/shard_map/ppermute | solution.py:766
  (7 other events, 8.1 us)
